TPU v7x, 32 devices: a whole 2x2x4 slice. The times are simulated.
32 devices in a mesh: shard: 4 (over z), context: 2 (over x), tensor: 4 (over y, core).
Axes of the slice: x: 2, y: 2, z: 4, core: 2. Of those that a mesh axis runs over, the one named last changes fastest.
Arguments:
- tokens: bfloat16 [4, 2048, 1024], P('shard', ('context', 'tensor'))
- piece_ids: int32 [4, 2048], P('shard', 'context'), may hold values from 0 to 4, as said below
- tok_qkv: bfloat16 [1024, 8, 384], P('shard', 'tensor'), may hold values from -0.1875 to 0.1875
- state_qkv: bfloat16 [1024, 8, 384], P('shard', 'tensor'), may hold values from -0.1875 to 0.1875
- tok_out: bfloat16 [8, 128, 1024], P('tensor', None, 'shard'), may hold values from -0.75 to 0.75
- state_out: bfloat16 [8, 128, 1024], P('tensor', None, 'shard'), may hold values from -0.75 to 0.75
- mlp_in: bfloat16 [1024, 4096], P('shard', 'tensor'), may hold values from -0.1875 to 0.1875
- mlp_out: bfloat16 [4096, 1024], P('tensor', 'shard'), may hold values from -0.09375 to 0.09375
- rel_bias: bfloat16 [32, 8], P('shard', 'tensor'), may hold values from -4 to 4
- init_state: bfloat16 [512, 1024], P('tensor', 'shard'), may hold values from -5 to 5
- norm_gains: bfloat16 [3, 1024], P(None, ('shard', 'tensor')), may hold values from 0.5 to 1.5
- decay_param: bfloat16 [1024], P(('shard', 'tensor')), may hold values from 1 to 4
- cotangent: bfloat16 [4, 2048, 1024], P('shard', ('context', 'tensor')), may hold values from -6 to 6
Outputs:
- output: bfloat16 [4, 2048, 1024], P('shard', ('context', 'tensor'))
- grad_tokens: bfloat16 [4, 2048, 1024], P('shard', ('context', 'tensor'))
- grad_tok_qkv: float32 [1024, 8, 384], P('shard', 'tensor')
- grad_state_qkv: float32 [1024, 8, 384], P('shard', 'tensor')
- grad_tok_out: float32 [8, 128, 1024], P('tensor', None, 'shard')
- grad_state_out: float32 [8, 128, 1024], P('tensor', None, 'shard')
- grad_mlp_in: float32 [1024, 4096], P('shard', 'tensor')
- grad_mlp_out: float32 [4096, 1024], P('tensor', 'shard')
- grad_rel_bias: float32 [32, 8], P('shard', 'tensor')
- grad_init_state: float32 [512, 1024], P('tensor', 'shard')
- grad_norm_gains: float32 [3, 1024], P(None, ('shard', 'tensor'))
- grad_decay_param: float32 [1024], P(('shard', 'tensor'))
- rms_out: float32 [3], replicated
Inputs may be any that keep to these rules, and one draw needn't show every extreme that they name: `piece_ids`: in every aligned block of 512 positions of a sequence exactly 256 consecutive positions form one picture piece and hold the number of that block plus one (1 for the first block); all other positions hold 0.
All inputs are finite; a program needn't handle non-finite values.
Results may differ from a plain program's by a relative error of at most 0.024.
Values may be sent and summed in bfloat16 or wider, within the bound.
No kernel may reach another device: no remote copies, remote signals or barrier semaphores. Data moves between devices by JAX's collectives and lax.ppermute only.
A program may use at most 192 MiB of HBM per device.

v0:
```python
import jax
import jax.numpy as jnp
import numpy as np
from jax import lax
from jax.sharding import PartitionSpec as P

HS = 128
BLK = 512
NBUCKET = 32


HIGHEST = lax.Precision.HIGHEST
EDGES = (12, 16, 23, 32, 46, 64, 91)


def passed_along(array, axis, by):
    size = lax.axis_size(axis)
    pairs = [(i, i + by) for i in range(size) if 0 <= i + by < size]
    return lax.ppermute(array, axis, pairs)


def bucket_of(offsets):
    distance = np.abs(offsets)
    far_part = 8 + np.sum(distance[..., None] >= np.array(EDGES), axis=-1)
    near_part = np.where(distance < 8, distance, far_part)
    return np.where(offsets < 0, 16 + near_part, near_part)


def bucket_onehot(block_len, buckets):
    offsets = np.arange(3 * block_len - 1) - (block_len - 1)
    return (bucket_of(offsets)[:, None] == np.arange(buckets)[None, :]).astype(np.float32)


def spread_bias(vector, block_len):
    head_count = vector.shape[0]
    diag_count = 3 * block_len - 1
    tiled_rows = jnp.broadcast_to(vector[:, None, :], (head_count, block_len, diag_count)).reshape(
        head_count, block_len * diag_count
    )
    tiled_rows = jnp.pad(tiled_rows, ((0, 0), (0, block_len)))
    skewed = tiled_rows.reshape(head_count, block_len, 3 * block_len)[:, :, : 2 * block_len]
    return skewed[:, :, ::-1]


def collapse_bias(grad_window, block_len):
    head_count = grad_window.shape[0]
    diag_count = 3 * block_len - 1
    padded = jnp.pad(grad_window[:, :, ::-1], ((0, 0), (0, 0), (0, block_len))).reshape(
        head_count, 3 * block_len * block_len
    )
    sheared = padded[:, : block_len * diag_count].reshape(head_count, block_len, diag_count)
    return jnp.sum(sheared, axis=1)


def root_mean(features, gain_row):
    return (
        features
        * lax.rsqrt(jnp.mean(features * features, axis=-1, keepdims=True) + 1e-06)
        * gain_row
    )


def gelu_exact(features):
    return jax.nn.gelu(features, approximate=False)


def rows_full(part_rows):
    return lax.all_gather(part_rows, "tensor", axis=1, tiled=True)


def rows_part(whole_rows):
    return lax.psum_scatter(
        whole_rows.astype(jnp.bfloat16), "tensor", scatter_dimension=1, tiled=True
    ).astype(jnp.float32)


def shards(
    tokens,
    piece_ids,
    tok_qkv,
    state_qkv,
    tok_out,
    state_out,
    mlp_in,
    mlp_out,
    rel_bias,
    init_state,
    norm_gains,
    decay_param,
    cotangent,
):
    block_len = BLK
    head_size = HS
    scaling = head_size ** (-0.5)
    gathered = (
        lax.all_gather(tok_qkv, "shard", axis=0, tiled=True),
        lax.all_gather(state_qkv, "shard", axis=0, tiled=True),
        lax.all_gather(tok_out, "shard", axis=2, tiled=True),
        lax.all_gather(state_out, "shard", axis=2, tiled=True),
        lax.all_gather(mlp_in, "shard", axis=0, tiled=True),
        lax.all_gather(mlp_out, "shard", axis=1, tiled=True),
        lax.all_gather(rel_bias, "shard", axis=0, tiled=True),
        lax.all_gather(init_state, "shard", axis=1, tiled=True),
    )
    w_tqkv, w_sqkv, w_tout, w_sout, w_in, w_out, bias_table, start_state = gathered
    small_full = (
        lax.all_gather(norm_gains, ("shard", "tensor"), axis=1, tiled=True),
        lax.all_gather(decay_param, ("shard", "tensor"), axis=0, tiled=True),
    )
    gain_rows = small_full[0].astype(jnp.float32)
    decay_rate = jax.nn.sigmoid(small_full[1].astype(jnp.float32))
    context_pos = lax.axis_index("context")
    context_count = lax.axis_size("context")
    seq_count = tokens.shape[0]
    inputs = tokens.astype(jnp.float32)
    normed_a = root_mean(inputs, gain_rows[0]).astype(jnp.bfloat16)
    attn_rows = rows_full(normed_a)
    ctx_rows = attn_rows.shape[1]
    block_count = ctx_rows // block_len
    head_local = w_tqkv.shape[1]
    projected = jnp.einsum(
        "srd,dhe->srhe", attn_rows, w_tqkv, preferred_element_type=jnp.float32
    ).astype(jnp.bfloat16)
    blocked = projected.reshape(seq_count, block_count, block_len, head_local, 3 * head_size)
    queries = blocked[..., :head_size]
    keys_tok = blocked[..., head_size : 2 * head_size]
    values_tok = blocked[..., 2 * head_size :]
    prior_keys, prior_values = passed_along(
        (keys_tok[:, block_count - 1], values_tok[:, block_count - 1]), "context", 1
    )
    start_rows = start_state.astype(jnp.float32)[None]
    incoming = start_rows
    chain_kept = []
    for round_index in range(context_count):
        current = jnp.where(context_pos == 0, start_rows, incoming)
        chain_kept = []
        for block_idx in range(block_count):
            normed_all = rows_full(root_mean(current, gain_rows[2]).astype(jnp.bfloat16))
            state_proj = jnp.einsum(
                "snd,dhe->snhe", normed_all, w_sqkv, preferred_element_type=jnp.float32
            ).astype(jnp.bfloat16)
            state_slogits = (
                jnp.einsum(
                    "snhe,sjhe->shnj",
                    state_proj[..., :head_size],
                    keys_tok[:, block_idx],
                    preferred_element_type=jnp.float32,
                )
                * scaling
            )
            state_sprobs = jax.nn.softmax(state_slogits, axis=-1).astype(jnp.bfloat16)
            smixed = jnp.einsum(
                "shnj,sjhe->snhe",
                state_sprobs,
                values_tok[:, block_idx],
                preferred_element_type=jnp.float32,
            ).astype(jnp.bfloat16)
            mix_rows = smixed
            update = rows_part(
                jnp.einsum("snhe,hed->snd", smixed, w_sout, preferred_element_type=jnp.float32)
            )
            normed_all, state_proj, update, mix_rows, following = (
                normed_all,
                state_proj,
                update,
                mix_rows,
                decay_rate * current + (1.0 - decay_rate) * update,
            )
            chain_kept.append((current, normed_all, state_proj, update, mix_rows))
            current = following
        if round_index + 1 < context_count:
            incoming = passed_along(current.astype(jnp.bfloat16), "context", 1).astype(
                current.dtype
            )
    onehot = jnp.asarray(bucket_onehot(block_len, NBUCKET))
    bias_vectors = jnp.dot(onehot, bias_table.astype(jnp.float32), precision=HIGHEST).T
    state_count = chain_kept[0][1].shape[1]
    full_bias = jnp.concatenate(
        [
            jnp.zeros((head_local, block_len, state_count), jnp.float32),
            spread_bias(bias_vectors, block_len),
        ],
        axis=2,
    )
    ids_blocks = piece_ids.reshape(seq_count, block_count, block_len)
    position = jnp.arange(block_len)
    causal = position[None, :] <= position[:, None]

    def allowed_keys(block_idx):
        ids_now = ids_blocks[:, block_idx]
        same_piece = (ids_now[:, :, None] == ids_now[:, None, :]) & (ids_now[:, :, None] > 0)
        current_ok = causal[None] | same_piece
        prior_ok = jnp.broadcast_to(
            (context_pos > 0) | (block_idx > 0), (seq_count, block_len, block_len)
        )
        state_ok = jnp.ones((seq_count, block_len, state_count), jnp.bool_)
        return jnp.concatenate([state_ok, prior_ok, current_ok], axis=2)

    def keys_for(block_idx):
        state_proj = chain_kept[block_idx][2]
        if block_idx == 0:
            prev_keys, prev_values = (prior_keys, prior_values)
        else:
            prev_keys, prev_values = (keys_tok[:, block_idx - 1], values_tok[:, block_idx - 1])
        keys_all = jnp.concatenate(
            [state_proj[..., head_size : 2 * head_size], prev_keys, keys_tok[:, block_idx]], axis=1
        )
        values_all = jnp.concatenate(
            [state_proj[..., 2 * head_size :], prev_values, values_tok[:, block_idx]], axis=1
        )
        return (keys_all, values_all)

    def block_logits(block_idx, keys_all):
        logits = (
            jnp.einsum(
                "sihe,sjhe->shij",
                queries[:, block_idx],
                keys_all,
                preferred_element_type=jnp.float32,
            )
            * scaling
            + full_bias[None]
        )
        return jnp.where(allowed_keys(block_idx)[:, None], logits, -1e30)

    mixed_blocks = []
    lse_blocks = []
    for block_idx in range(block_count):
        keys_all, values_all = keys_for(block_idx)
        logits = block_logits(block_idx, keys_all)
        row_peak = jnp.max(logits, axis=-1, keepdims=True)
        exponent = jnp.exp(logits - row_peak)
        row_total = jnp.sum(exponent, axis=-1, keepdims=True)
        lse_blocks.append(row_peak + jnp.log(row_total))
        mixed_blk = jnp.einsum(
            "shij,sjhe->sihe",
            (exponent / row_total).astype(jnp.bfloat16),
            values_all,
            preferred_element_type=jnp.float32,
        )
        mixed_blocks.append(mixed_blk.astype(jnp.bfloat16))
    mixed_all = jnp.stack(mixed_blocks, axis=1).reshape(seq_count, ctx_rows, head_local, head_size)
    branch_a = rows_part(
        jnp.einsum("srhe,hed->srd", mixed_all, w_tout, preferred_element_type=jnp.float32)
    )
    residual = inputs + branch_a
    normed_m = root_mean(residual, gain_rows[1]).astype(jnp.bfloat16)
    mlp_rows = rows_full(normed_m)
    pre_act = jnp.einsum("srd,df->srf", mlp_rows, w_in, preferred_element_type=jnp.float32)
    hidden = gelu_exact(pre_act).astype(jnp.bfloat16)
    branch_m = rows_part(
        jnp.einsum("srf,fd->srd", hidden, w_out, preferred_element_type=jnp.float32)
    )
    output = residual + branch_m
    squares = jnp.stack(
        [jnp.sum(inputs * inputs), jnp.sum(branch_a * branch_a), jnp.sum(branch_m * branch_m)]
    )
    totals = lax.psum(squares, ("shard", "context", "tensor"))
    entry_count = inputs.size * lax.axis_size("shard") * context_count * lax.axis_size("tensor")
    rms_out = jnp.sqrt(totals / entry_count)
    grad_out = cotangent.astype(jnp.float32)
    gelu_pair = jax.vjp(gelu_exact, pre_act)
    grad_rows = rows_full(cotangent)
    grad_hidden = jnp.einsum("srd,fd->srf", grad_rows, w_out, preferred_element_type=jnp.float32)
    grad_pre = gelu_pair[1](grad_hidden)[0].astype(jnp.bfloat16)
    grad_w_out = jnp.einsum("srf,srd->fd", hidden, grad_rows, preferred_element_type=jnp.float32)
    grad_w_in = jnp.einsum("srd,srf->df", mlp_rows, grad_pre, preferred_element_type=jnp.float32)
    grad_normed_m = rows_part(
        jnp.einsum("srf,df->srd", grad_pre, w_in, preferred_element_type=jnp.float32)
    )
    norm_m_back = jax.vjp(root_mean, residual, gain_rows[1])[1]
    grad_resid_n, grad_gain_m = norm_m_back(grad_normed_m)
    grad_resid = grad_out + grad_resid_n
    grad_branch = rows_full(grad_resid.astype(jnp.bfloat16))
    grad_w_tout = jnp.einsum(
        "srhe,srd->hed", mixed_all, grad_branch, preferred_element_type=jnp.float32
    )
    grad_mixed = jnp.einsum(
        "srd,hed->srhe", grad_branch, w_tout, preferred_element_type=jnp.float32
    ).astype(jnp.bfloat16)
    grad_mixed = grad_mixed.reshape(seq_count, block_count, block_len, head_local, head_size)
    grad_queries = []
    grad_keys_cur = []
    grad_values_cur = []
    grad_keys_prior = []
    grad_values_prior = []
    grad_state_keys = []
    grad_state_values = []
    bias_grad = jnp.zeros((head_local, block_len, 2 * block_len), jnp.float32)
    for block_idx in range(block_count):
        keys_all, values_all = keys_for(block_idx)
        weights_blk = jnp.exp(block_logits(block_idx, keys_all) - lse_blocks[block_idx])
        grad_mixed_blk = grad_mixed[:, block_idx]
        grad_probs = jnp.einsum(
            "sihe,sjhe->shij", grad_mixed_blk, values_all, preferred_element_type=jnp.float32
        )
        grad_values_all = jnp.einsum(
            "shij,sihe->sjhe",
            weights_blk.astype(jnp.bfloat16),
            grad_mixed_blk,
            preferred_element_type=jnp.float32,
        )
        row_inner = jnp.sum(grad_probs * weights_blk, axis=-1, keepdims=True)
        grad_logits = (weights_blk * (grad_probs - row_inner)).astype(jnp.bfloat16)
        grad_queries.append(
            jnp.einsum("shij,sjhe->sihe", grad_logits, keys_all, preferred_element_type=jnp.float32)
            * scaling
        )
        grad_keys_all = (
            jnp.einsum(
                "shij,sihe->sjhe",
                grad_logits,
                queries[:, block_idx],
                preferred_element_type=jnp.float32,
            )
            * scaling
        )
        bias_grad = bias_grad + jnp.sum(grad_logits[..., state_count:].astype(jnp.float32), axis=0)
        grad_state_keys.append(grad_keys_all[:, :state_count])
        grad_state_values.append(grad_values_all[:, :state_count])
        grad_keys_prior.append(grad_keys_all[:, state_count : state_count + block_len])
        grad_values_prior.append(grad_values_all[:, state_count : state_count + block_len])
        grad_keys_cur.append(grad_keys_all[:, state_count + block_len :])
        grad_values_cur.append(grad_values_all[:, state_count + block_len :])
    back_keys, back_values = (
        passed_along(grad_keys_prior[0].astype(jnp.bfloat16), "context", -1).astype(jnp.float32),
        passed_along(grad_values_prior[0].astype(jnp.bfloat16), "context", -1).astype(jnp.float32),
    )
    incoming_grad = jnp.zeros_like(start_rows)
    carried = incoming_grad
    grad_w_sqkv = jnp.zeros(w_sqkv.shape, jnp.float32)
    grad_w_sout = jnp.zeros(w_sout.shape, jnp.float32)
    grad_decay = jnp.zeros(decay_rate.shape, jnp.float32)
    grad_gain_s = jnp.zeros(decay_rate.shape, jnp.float32)
    grad_keys_state = [None] * block_count
    grad_values_state = [None] * block_count
    for round_index in range(context_count):
        carried = jnp.where(context_pos == context_count - 1, 0.0, incoming_grad)
        grad_w_sqkv = jnp.zeros(w_sqkv.shape, jnp.float32)
        grad_w_sout = jnp.zeros(w_sout.shape, jnp.float32)
        grad_decay = jnp.zeros(decay_rate.shape, jnp.float32)
        grad_gain_s = jnp.zeros(decay_rate.shape, jnp.float32)
        for block_idx in reversed(range(block_count)):
            state_now, normed_all, state_proj, update, mix_rows = chain_kept[block_idx]
            keys_blk = keys_tok[:, block_idx]
            values_blk = values_tok[:, block_idx]
            grad_decay = grad_decay + jnp.sum(carried * (state_now - update), axis=(0, 1))
            grad_update_own = ((1.0 - decay_rate) * carried).astype(jnp.bfloat16)
            grad_update = rows_full(grad_update_own)
            grad_w_sout = grad_w_sout + jnp.einsum(
                "snhe,snd->hed", mix_rows, grad_update, preferred_element_type=jnp.float32
            )
            grad_smixed = jnp.einsum(
                "snd,hed->snhe", grad_update, w_sout, preferred_element_type=jnp.float32
            ).astype(jnp.bfloat16)
            squery = state_proj[..., :head_size]
            slogits = (
                jnp.einsum("snhe,sjhe->shnj", squery, keys_blk, preferred_element_type=jnp.float32)
                * scaling
            )
            sprobs = jax.nn.softmax(slogits, axis=-1)
            sprobs_low = sprobs.astype(jnp.bfloat16)
            grad_sprobs = jnp.einsum(
                "snhe,sjhe->shnj", grad_smixed, values_blk, preferred_element_type=jnp.float32
            )
            grad_values_state[block_idx] = jnp.einsum(
                "shnj,snhe->sjhe", sprobs_low, grad_smixed, preferred_element_type=jnp.float32
            )
            row_inner = jnp.sum(grad_sprobs * sprobs, axis=-1, keepdims=True)
            grad_slogits = (sprobs * (grad_sprobs - row_inner)).astype(jnp.bfloat16)
            grad_squery = (
                jnp.einsum(
                    "shnj,sjhe->snhe", grad_slogits, keys_blk, preferred_element_type=jnp.float32
                )
                * scaling
            )
            grad_keys_state[block_idx] = (
                jnp.einsum(
                    "shnj,snhe->sjhe", grad_slogits, squery, preferred_element_type=jnp.float32
                )
                * scaling
            )
            grad_sproj = jnp.concatenate(
                [grad_squery, grad_state_keys[block_idx], grad_state_values[block_idx]], axis=-1
            ).astype(jnp.bfloat16)
            grad_w_sqkv = grad_w_sqkv + jnp.einsum(
                "snd,snhe->dhe", normed_all, grad_sproj, preferred_element_type=jnp.float32
            )
            grad_normed_s = rows_part(
                jnp.einsum("snhe,dhe->snd", grad_sproj, w_sqkv, preferred_element_type=jnp.float32)
            )
            norm_s_back = jax.vjp(root_mean, state_now, gain_rows[2])[1]
            grad_state_n, gain_part = norm_s_back(grad_normed_s)
            grad_gain_s = grad_gain_s + gain_part
            carried = carried * decay_rate + grad_state_n
        if round_index + 1 < context_count:
            incoming_grad = passed_along(carried.astype(jnp.bfloat16), "context", -1).astype(
                carried.dtype
            )
    grad_start = jnp.where(context_pos == 0, jnp.sum(carried, axis=0), 0.0)
    grad_key_blocks = []
    grad_value_blocks = []
    for block_idx in range(block_count):
        if block_idx + 1 < block_count:
            later_keys, later_values = (
                grad_keys_prior[block_idx + 1],
                grad_values_prior[block_idx + 1],
            )
        else:
            later_keys, later_values = (back_keys, back_values)
        grad_key_blocks.append(grad_keys_cur[block_idx] + grad_keys_state[block_idx] + later_keys)
        grad_value_blocks.append(
            grad_values_cur[block_idx] + grad_values_state[block_idx] + later_values
        )
    grad_proj = jnp.concatenate(
        [
            jnp.stack(grad_queries, axis=1),
            jnp.stack(grad_key_blocks, axis=1),
            jnp.stack(grad_value_blocks, axis=1),
        ],
        axis=-1,
    )
    grad_proj = grad_proj.astype(jnp.bfloat16).reshape(
        seq_count, ctx_rows, head_local, 3 * head_size
    )
    grad_w_tqkv = jnp.einsum(
        "srd,srhe->dhe", attn_rows, grad_proj, preferred_element_type=jnp.float32
    )
    grad_normed_a = rows_part(
        jnp.einsum("srhe,dhe->srd", grad_proj, w_tqkv, preferred_element_type=jnp.float32)
    )
    norm_a_back = jax.vjp(root_mean, inputs, gain_rows[0])[1]
    grad_in_n, grad_gain_a = norm_a_back(grad_normed_a)
    grad_tokens = (grad_resid + grad_in_n).astype(jnp.bfloat16)
    grad_table = jnp.dot(collapse_bias(bias_grad, block_len), onehot, precision=HIGHEST).T
    grad_gains = jnp.stack([grad_gain_a, grad_gain_m, grad_gain_s])
    grad_decay_param = grad_decay * decay_rate * (1.0 - decay_rate)
    weight_parts = (
        lax.psum_scatter(
            grad_w_tqkv.astype(jnp.bfloat16), "shard", scatter_dimension=0, tiled=True
        ).astype(jnp.float32),
        lax.psum_scatter(
            grad_w_sqkv.astype(jnp.bfloat16), "shard", scatter_dimension=0, tiled=True
        ).astype(jnp.float32),
        lax.psum_scatter(
            grad_w_tout.astype(jnp.bfloat16), "shard", scatter_dimension=2, tiled=True
        ).astype(jnp.float32),
        lax.psum_scatter(
            grad_w_sout.astype(jnp.bfloat16), "shard", scatter_dimension=2, tiled=True
        ).astype(jnp.float32),
        lax.psum_scatter(
            grad_w_in.astype(jnp.bfloat16), "shard", scatter_dimension=0, tiled=True
        ).astype(jnp.float32),
        lax.psum_scatter(
            grad_w_out.astype(jnp.bfloat16), "shard", scatter_dimension=1, tiled=True
        ).astype(jnp.float32),
        lax.psum_scatter(
            grad_table.astype(jnp.bfloat16), "shard", scatter_dimension=0, tiled=True
        ).astype(jnp.float32),
        lax.psum_scatter(
            grad_start.astype(jnp.bfloat16), "shard", scatter_dimension=1, tiled=True
        ).astype(jnp.float32),
    )
    small_parts = (
        lax.psum_scatter(grad_gains, ("shard", "tensor"), scatter_dimension=1, tiled=True),
        lax.psum_scatter(grad_decay_param, ("shard", "tensor"), scatter_dimension=0, tiled=True),
    )
    summed = (
        lax.psum(weight_parts[0].astype(jnp.bfloat16), "context").astype(jnp.float32),
        lax.psum(weight_parts[1].astype(jnp.bfloat16), "context").astype(jnp.float32),
        lax.psum(weight_parts[2].astype(jnp.bfloat16), "context").astype(jnp.float32),
        lax.psum(weight_parts[3].astype(jnp.bfloat16), "context").astype(jnp.float32),
        lax.psum(weight_parts[4].astype(jnp.bfloat16), "context").astype(jnp.float32),
        lax.psum(weight_parts[5].astype(jnp.bfloat16), "context").astype(jnp.float32),
        lax.psum(weight_parts[6].astype(jnp.bfloat16), "context").astype(jnp.float32),
        lax.psum(weight_parts[7].astype(jnp.bfloat16), "context").astype(jnp.float32),
        lax.psum(small_parts[0].astype(jnp.bfloat16), "context").astype(jnp.float32),
        lax.psum(small_parts[1].astype(jnp.bfloat16), "context").astype(jnp.float32),
    )
    return (
        output.astype(jnp.bfloat16),
        grad_tokens,
        summed[0],
        summed[1],
        summed[2],
        summed[3],
        summed[4],
        summed[5],
        summed[6],
        summed[7],
        summed[8],
        summed[9],
        rms_out,
    )


def solution(mesh):
    return jax.shard_map(
        shards,
        mesh=mesh,
        in_specs=(
            P("shard", ("context", "tensor"), None),
            P("shard", "context"),
            P("shard", "tensor", None),
            P("shard", "tensor", None),
            P("tensor", None, "shard"),
            P("tensor", None, "shard"),
            P("shard", "tensor"),
            P("tensor", "shard"),
            P("shard", "tensor"),
            P("tensor", "shard"),
            P(None, ("shard", "tensor")),
            P(("shard", "tensor")),
            P("shard", ("context", "tensor"), None),
        ),
        out_specs=(
            P("shard", ("context", "tensor"), None),
            P("shard", ("context", "tensor"), None),
            P("shard", "tensor", None),
            P("shard", "tensor", None),
            P("tensor", None, "shard"),
            P("tensor", None, "shard"),
            P("shard", "tensor"),
            P("tensor", "shard"),
            P("shard", "tensor"),
            P("tensor", "shard"),
            P(None, ("shard", "tensor")),
            P(("shard", "tensor")),
            P(),
        ),
        check_vma=False,
    )
```

profile of v0, /device:TPU:0, one launch (start us, length us, event | category | flops | bytes accessed | tf_op | source)
XLA Modules:
  0.0 1362.0 jit_solution(10396557022152602500)
XLA Ops:
  7.2 23.5 %all-gather.1 = bf16[16,64,3]{1,2,0:T(4,128)(2,1)S(1)} all-gather(bf16[1,64,3]{1,2,0:T(4,128)(2,1)} %bitcast.769), channel_id=1, replica_groups=mesh['shard'=4,'context'=2,'tensor'=4] {'shard','tensor'}, dimensions={0}, use_global_device_ids=true | all-gather | bytes 6528 | tf_op jit(solution)/shard_map/all_gather | solution.py:107
  30.8 14.6 %all_gather.66 = bf16[128,1024]{1,0:T(8,128)(2,1)S(1)} all-gather(bf16[128,256]{1,0:T(8,128)(2,1)} %param.23), channel_id=1, replica_groups=mesh['shard'=4,'context'=2,'tensor'=4] {'shard'}, dimensions={1}, use_global_device_ids=true | all-gather | bytes 327680 | tf_op jit(solution)/shard_map/all_gather | solution.py:103
  50.5 14.8 %all_gather.73 = bf16[2,128,1024]{2,1,0:T(8,128)(2,1)S(1)} all-gather(bf16[2,128,256]{2,1,0:T(8,128)(2,1)S(1)} %copy-done.77), channel_id=1, replica_groups=mesh['shard'=4,'context'=2,'tensor'=4] {'shard'}, dimensions={2}, use_global_device_ids=true | all-gather | bytes 655360 | tf_op jit(solution)/shard_map/all_gather | solution.py:99
  65.3 34.6 %all-gather.24.cloned.1.call-done = bf16[1024,2,384]{2,0,1:T(8,128)(2,1)} async-done(((bf16[256,2,384]{2,0,1:T(8,128)(2,1)}), bf16[1024,2,384]{2,0,1:T(8,128)(2,1)}) %all-gather.24.cloned.1.call-update) | async-done | bytes 1572880 | tf_op jit(solution)/shard_map/all_gather | solution.py:97
  102.6 35.4 %all-gather.22.cloned.1.call-done = bf16[1024,2,384]{2,0,1:T(8,128)(2,1)} async-done(((bf16[256,2,384]{2,0,1:T(8,128)(2,1)}), bf16[1024,2,384]{2,0,1:T(8,128)(2,1)}) %all-gather.22.cloned.1.call-update) | async-done | bytes 1572880 | tf_op jit(solution)/shard_map/all_gather | solution.py:96
  138.1 23.5 %all-gather.20.cloned.1.call-done = bf16[1,1024,1024]{2,1,0:T(8,128)(2,1)} async-done(((bf16[1,256,1024]{2,1,0:T(8,128)(2,1)}), bf16[1,1024,1024]{2,1,0:T(8,128)(2,1)}) %all-gather.20.cloned.1.call-update) | async-done | bytes 2097168 | tf_op jit(solution)/shard_map/all_gather | solution.py:68
  174.7 32.8 %all-reduce.4 = bf16[1024]{0:T(1024)(128)(2,1)S(1)} all-reduce(bf16[1024]{0:T(1024)(128)(2,1)S(1)} %dynamic-update-slice), channel_id=1, replica_groups=mesh['shard'=4,'context'=2,'tensor'=4] {'shard','tensor'}, use_global_device_ids=true, to_apply=%add.4 | all-reduce | flops 1024 | bytes 4096
  234.1 25.0 %reduce-scatter.26.cloned.1.call-done = bf16[1,128,1024]{2,1,0:T(8,128)(2,1)} async-done(((bf16[1,512,1024]{2,1,0:T(8,128)(2,1)}), bf16[1,128,1024]{2,1,0:T(8,128)(2,1)}) %reduce-scatter.26.cloned.1.call-update) | async-done | bytes 262160 | tf_op jit(solution)/shard_map/reduce_scatter | solution.py:72
  309.3 34.4 %rev.6 = f32[2,512,1024]{2,1,0:T(8,128)} reverse(f32[2,512,1024]{2,1,0:T(8,128)} %slice.220), dimensions={2} | reverse | bytes 8388608 | tf_op jit(solution)/shard_map/rev | solution.py:42
  353.5 14.8 %all_gather.78 = bf16[2,128,1024]{2,1,0:T(8,128)(2,1)S(1)} all-gather(bf16[2,128,256]{2,1,0:T(8,128)(2,1)S(1)} %copy-done.78), channel_id=1, replica_groups=mesh['shard'=4,'context'=2,'tensor'=4] {'shard'}, dimensions={2}, use_global_device_ids=true | all-gather | bytes 655360 | tf_op jit(solution)/shard_map/all_gather | solution.py:98
  412.3 31.0 %reduce-scatter.30.cloned.1.call-done = bf16[1,256,1024]{2,1,0:T(8,128)(2,1)} async-done(((bf16[1,1024,1024]{2,1,0:T(8,128)(2,1)}), bf16[1,256,1024]{2,1,0:T(8,128)(2,1)}) %reduce-scatter.30.cloned.1.call-update) | async-done | bytes 524304 | tf_op jit(solution)/shard_map/reduce_scatter | solution.py:72
  448.0 42.6 %all-gather.34.cloned.1.call-done = bf16[1024,1024]{1,0:T(8,128)(2,1)} async-done(((bf16[256,1024]{1,0:T(8,128)(2,1)}), bf16[1024,1024]{1,0:T(8,128)(2,1)}) %all-gather.34.cloned.1.call-update) | async-done | bytes 2097168 | tf_op jit(solution)/shard_map/all_gather | solution.py:100
  490.6 23.5 %all-gather.32.cloned.1.call-done = bf16[1,1024,1024]{2,1,0:T(8,128)(2,1)} async-done(((bf16[1,256,1024]{2,1,0:T(8,128)(2,1)}), bf16[1,1024,1024]{2,1,0:T(8,128)(2,1)}) %all-gather.32.cloned.1.call-update) | async-done | bytes 2097168 | tf_op jit(solution)/shard_map/all_gather | solution.py:68
  514.1 14.7 %multiply_convert_fusion.2 = (bf16[1024,1024]{1,0:T(8,128)(2,1)}, f32[1024,1024]{1,0:T(8,128)}, f32[1024,1024]{1,0:T(8,128)}) fusion(bf16[1024,1024]{1,0:T(8,128)(2,1)} %all-gather.34.cloned.1.call-done, bf16[1,1024,1024]{2,1,0:T(8,128)(2,1)} %all-gather.32.cloned.1.call-done), kind=kOutput, calls=%fused_computation.30 | convolution fusion | flops 2215641088 | bytes 14680064 | tf_op jit(solution)/shard_map/srd,df->srf/dot_general | solution.py:249
  528.8 32.9 %all-gather.36.cloned.1.call-done = bf16[1024,1024]{1,0:T(8,128)(2,1)} async-done(((bf16[1024,256]{1,0:T(8,128)(2,1)}), bf16[1024,1024]{1,0:T(8,128)(2,1)}) %all-gather.36.cloned.1.call-update) | async-done | bytes 2097168 | tf_op jit(solution)/shard_map/all_gather | solution.py:101
  561.8 22.3 %all-gather.38.cloned.1.call-done = bf16[1,1024,1024]{2,1,0:T(8,128)(2,1)} async-done(((bf16[1,256,1024]{2,1,0:T(8,128)(2,1)}), bf16[1,1024,1024]{2,1,0:T(8,128)(2,1)}) %all-gather.38.cloned.1.call-update) | async-done | bytes 2097168 | tf_op jit(solution)/shard_map/all_gather | solution.py:68
  598.2 30.7 %reduce-scatter.34.cloned.1.call-done = bf16[1,256,1024]{2,1,0:T(8,128)(2,1)} async-done(((bf16[1,1024,1024]{2,1,0:T(8,128)(2,1)}), bf16[1,256,1024]{2,1,0:T(8,128)(2,1)}) %reduce-scatter.34.cloned.1.call-update) | async-done | bytes 524304 | tf_op jit(solution)/shard_map/reduce_scatter | solution.py:72
  656.3 16.1 %all-gather.40.cloned.1.call-done = bf16[1,1024,1024]{2,1,0:T(8,128)(2,1)} async-done(((bf16[1,256,1024]{2,1,0:T(8,128)(2,1)}), bf16[1,1024,1024]{2,1,0:T(8,128)(2,1)}) %all-gather.40.cloned.1.call-update) | async-done | bytes 2097168 | tf_op jit(solution)/shard_map/all_gather | solution.py:68
  698.7 14.7 %reduce-scatter.36.cloned.1.call-done = bf16[1,128,1024]{2,1,0:T(8,128)(2,1)} async-done(((bf16[1,512,1024]{2,1,0:T(8,128)(2,1)}), bf16[1,128,1024]{2,1,0:T(8,128)(2,1)}) %reduce-scatter.36.cloned.1.call-update) | async-done | bytes 262160 | tf_op jit(solution)/shard_map/reduce_scatter | solution.py:72
  744.8 25.0 %reduce-scatter.38.cloned.1.call-done = bf16[1,128,1024]{2,1,0:T(8,128)(2,1)} async-done(((bf16[1,512,1024]{2,1,0:T(8,128)(2,1)}), bf16[1,128,1024]{2,1,0:T(8,128)(2,1)}) %reduce-scatter.38.cloned.1.call-update) | async-done | bytes 262160 | tf_op jit(solution)/shard_map/reduce_scatter | solution.py:72
  807.8 19.4 %reduce-scatter.60.cloned.1.call-done = bf16[1,128,1024]{2,1,0:T(8,128)(2,1)} async-done(((bf16[1,512,1024]{2,1,0:T(8,128)(2,1)}), bf16[1,128,1024]{2,1,0:T(8,128)(2,1)}) %reduce-scatter.60.cloned.1.call-update) | async-done | bytes 262160 | tf_op jit(solution)/shard_map/reduce_scatter | solution.py:72
  827.1 27.9 %reduce-scatter.40.cloned.1.call-done = bf16[1,128,1024]{2,1,0:T(8,128)(2,1)} async-done(((bf16[1,512,1024]{2,1,0:T(8,128)(2,1)}), bf16[1,128,1024]{2,1,0:T(8,128)(2,1)}) %reduce-scatter.40.cloned.1.call-update) | async-done | bytes 262160 | tf_op jit(solution)/shard_map/reduce_scatter | solution.py:72
  955.3 34.2 %reduce-scatter.52.cloned.1.call-done = bf16[256,1024]{1,0:T(8,128)(2,1)} async-done(((bf16[1024,1024]{1,0:T(8,128)(2,1)}), bf16[256,1024]{1,0:T(8,128)(2,1)}) %reduce-scatter.52.cloned.1.call-update) | async-done | bytes 524304 | tf_op jit(solution)/shard_map/reduce_scatter | solution.py:451
  989.5 45.5 %reduce-scatter.54.cloned.1.call-done = bf16[1024,256]{1,0:T(8,128)(2,1)} async-done(((bf16[1024,1024]{1,0:T(8,128)(2,1)}), bf16[1024,256]{1,0:T(8,128)(2,1)}) %reduce-scatter.54.cloned.1.call-update) | async-done | bytes 524304 | tf_op jit(solution)/shard_map/reduce_scatter | solution.py:454
  1035.0 23.8 %reduce-scatter.48.cloned.1.call-done = bf16[2,128,256]{2,1,0:T(8,128)(2,1)} async-done(((bf16[2,128,1024]{2,1,0:T(8,128)(2,1)}), bf16[2,128,256]{2,1,0:T(8,128)(2,1)}) %reduce-scatter.48.cloned.1.call-update) | async-done | bytes 131088 | tf_op jit(solution)/shard_map/reduce_scatter | solution.py:445
  1058.8 22.8 %reduce-scatter.50.cloned.1.call-done = bf16[2,128,256]{2,1,0:T(8,128)(2,1)} async-done(((bf16[2,128,1024]{2,1,0:T(8,128)(2,1)}), bf16[2,128,256]{2,1,0:T(8,128)(2,1)}) %reduce-scatter.50.cloned.1.call-update) | async-done | bytes 131088 | tf_op jit(solution)/shard_map/reduce_scatter | solution.py:448
  1081.6 20.8 %reduce-scatter.58.cloned.1.call-done = bf16[128,256]{1,0:T(8,128)(2,1)} async-done(((bf16[128,1024]{1,0:T(8,128)(2,1)}), bf16[128,256]{1,0:T(8,128)(2,1)}) %reduce-scatter.58.cloned.1.call-update) | async-done | bytes 65552 | tf_op jit(solution)/shard_map/reduce_scatter | solution.py:460
  1102.5 35.7 %reduce-scatter.44.cloned.1.call-done = bf16[256,2,384]{2,0,1:T(8,128)(2,1)} async-done(((bf16[1024,2,384]{2,0,1:T(8,128)(2,1)}), bf16[256,2,384]{2,0,1:T(8,128)(2,1)}) %reduce-scatter.44.cloned.1.call-update) | async-done | bytes 393232 | tf_op jit(solution)/shard_map/reduce_scatter | solution.py:439
  1138.2 36.6 %reduce-scatter.46.cloned.1.call-done = bf16[256,2,384]{2,0,1:T(8,128)(2,1)} async-done(((bf16[1024,2,384]{2,0,1:T(8,128)(2,1)}), bf16[256,2,384]{2,0,1:T(8,128)(2,1)}) %reduce-scatter.46.cloned.1.call-update) | async-done | bytes 393232 | tf_op jit(solution)/shard_map/reduce_scatter | solution.py:442
  1179.9 34.4 %rev.7 = f32[2,512,1024]{2,1,0:T(8,128)} reverse(f32[2,512,1024]{2,1,0:T(8,128)} %add_bitcast_fusion), dimensions={2} | reverse | bytes 8388608 | tf_op jit(solution)/shard_map/rev | solution.py:48
  1263.9 29.5 %all-reduce.6 = bf16[1024]{0:T(1024)(128)(2,1)S(1)} all-reduce(f32[1024]{0:T(1024)S(1)} %multiply_multiply_fusion.5), channel_id=24, replica_groups=mesh['shard'=4,'context'=2,'tensor'=4] {'shard','tensor'}, use_global_device_ids=true, to_apply=%region_67.68.clone | all-reduce | flops 1024 | bytes 6144
  1299.1 37.1 %psum.87 = f32[3]{0:T(128)S(1)} all-reduce(f32[3]{0:T(128)S(1)} %pad_maximum_fusion.22), channel_id=1, replica_groups=mesh['shard'=4,'context'=2,'tensor'=4] {'shard','context','tensor'}, use_global_device_ids=true, to_apply=%region_72.73 | all-reduce | flops 3 | bytes 24 | tf_op jit(solution)/shard_map/psum | solution.py:258
  (494 shorter events, 469.0 us)
Async XLA Ops:
  7.2 58.1 %all-gather.50.cloned.1.call-start = ((), (), s32[]{:S(2)}) async-start(), calls=%async_computation.54 | async-start | bytes 1310720 | tf_op jit(solution)/shard_map/all_gather | solution.py:68
  46.4 53.5 %all-gather.24.cloned.1.call-start = ((), (), s32[]{:S(2)}) async-start(), calls=%async_computation.22 | async-start | bytes 1966080 | tf_op jit(solution)/shard_map/all_gather | solution.py:97
  48.3 89.8 %all-gather.22.cloned.1.call-start = ((), (), s32[]{:S(2)}) async-start(), calls=%async_computation.21 | async-start | bytes 1966080 | tf_op jit(solution)/shard_map/all_gather | solution.py:96
  49.2 112.4 %all-gather.20.cloned.1.call-start = ((), (), s32[]{:S(2)}) async-start(), calls=%async_computation.20 | async-start | bytes 2621440 | tf_op jit(solution)/shard_map/all_gather | solution.py:68
  50.5 157.1 %reduce-scatter.24.cloned.1.call-start = ((), (), s32[]{:S(2)}) async-start(), calls=%async_computation.23 | async-start | bytes 1310720 | tf_op jit(solution)/shard_map/reduce_scatter | solution.py:72
  173.1 51.6 %all-gather.26.cloned.1.call-start = ((), (), s32[]{:S(2)}) async-start(), calls=%async_computation.24 | async-start | bytes 1310720 | tf_op jit(solution)/shard_map/all_gather | solution.py:68
  234.0 109.7 %all-gather.28.cloned.1.call-start = ((), (), s32[]{:S(2)}) async-start(), calls=%async_computation.26 | async-start | bytes 1310720 | tf_op jit(solution)/shard_map/all_gather | solution.py:68
  270.2 110.8 %reduce-scatter.28.cloned.1.call-start = ((), (), s32[]{:S(2)}) async-start(), calls=%async_computation.27 | async-start | bytes 1310720 | tf_op jit(solution)/shard_map/reduce_scatter | solution.py:72
  383.1 60.2 %reduce-scatter.30.cloned.1.call-start = ((), (), s32[]{:S(2)}) async-start(), calls=%async_computation.29 | async-start | bytes 2621440 | tf_op jit(solution)/shard_map/reduce_scatter | solution.py:72
  411.7 79.0 %all-gather.34.cloned.1.call-start = ((), (), s32[]{:S(2)}) async-start(), calls=%async_computation.31 | async-start | bytes 2621440 | tf_op jit(solution)/shard_map/all_gather | solution.py:100
  412.2 101.9 %all-gather.32.cloned.1.call-start = ((), (), s32[]{:S(2)}) async-start(), calls=%async_computation.30 | async-start | bytes 2621440 | tf_op jit(solution)/shard_map/all_gather | solution.py:68
  446.6 115.2 %all-gather.36.cloned.1.call-start = ((), (), s32[]{:S(2)}) async-start(), calls=%async_computation.32 | async-start | bytes 2621440 | tf_op jit(solution)/shard_map/all_gather | solution.py:101
  447.2 136.9 %all-gather.38.cloned.1.call-start = ((), (), s32[]{:S(2)}) async-start(), calls=%async_computation.34 | async-start | bytes 2621440 | tf_op jit(solution)/shard_map/all_gather | solution.py:68
  447.8 181.1 %reduce-scatter.34.cloned.1.call-start = ((), (), s32[]{:S(2)}) async-start(), calls=%async_computation.35 | async-start | bytes 2621440 | tf_op jit(solution)/shard_map/reduce_scatter | solution.py:72
  598.1 74.3 %all-gather.40.cloned.1.call-start = ((), (), s32[]{:S(2)}) async-start(), calls=%async_computation.36 | async-start | bytes 2621440 | tf_op jit(solution)/shard_map/all_gather | solution.py:68
  633.8 79.7 %reduce-scatter.36.cloned.1.call-start = ((), (), s32[]{:S(2)}) async-start(), calls=%async_computation.38 | async-start | bytes 1310720 | tf_op jit(solution)/shard_map/reduce_scatter | solution.py:72
  716.4 53.3 %reduce-scatter.38.cloned.1.call-start = ((), (), s32[]{:S(2)}) async-start(), calls=%async_computation.40 | async-start | bytes 1310720 | tf_op jit(solution)/shard_map/reduce_scatter | solution.py:72
  744.7 54.2 %all-gather.46.cloned.1.call-start = ((), (), s32[]{:S(2)}) async-start(), calls=%async_computation.41 | async-start | bytes 1310720 | tf_op jit(solution)/shard_map/all_gather | solution.py:68
  786.7 68.3 %reduce-scatter.40.cloned.1.call-start = ((), (), s32[]{:S(2)}) async-start(), calls=%async_computation.42 | async-start | bytes 1310720 | tf_op jit(solution)/shard_map/reduce_scatter | solution.py:72
  807.7 67.6 %all-gather.48.cloned.1.call-start = ((), (), s32[]{:S(2)}) async-start(), calls=%async_computation.43 | async-start | bytes 1310720 | tf_op jit(solution)/shard_map/all_gather | solution.py:68
  858.4 72.3 %reduce-scatter.56.cloned.1.call-start = ((), (), s32[]{:S(2)}) async-start(), calls=%async_computation.51 | async-start | bytes 1310720 | tf_op jit(solution)/shard_map/reduce_scatter | solution.py:72
  884.4 65.4 %reduce-scatter.42.cloned.1.call-start = ((), (), s32[]{:S(2)}) async-start(), calls=%async_computation.44 | async-start | bytes 2621440 | tf_op jit(solution)/shard_map/reduce_scatter | solution.py:72
  909.3 80.2 %reduce-scatter.52.cloned.1.call-start = ((), (), s32[]{:S(2)}) async-start(), calls=%async_computation.49 | async-start | bytes 2621440 | tf_op jit(solution)/shard_map/reduce_scatter | solution.py:451
  915.3 119.7 %reduce-scatter.54.cloned.1.call-start = ((), (), s32[]{:S(2)}) async-start(), calls=%async_computation.50 | async-start | bytes 2621440 | tf_op jit(solution)/shard_map/reduce_scatter | solution.py:454
  921.9 136.9 %reduce-scatter.48.cloned.1.call-start = ((), (), s32[]{:S(2)}) async-start(), calls=%async_computation.47 | async-start | bytes 655360 | tf_op jit(solution)/shard_map/reduce_scatter | solution.py:445
  926.0 155.6 %reduce-scatter.50.cloned.1.call-start = ((), (), s32[]{:S(2)}) async-start(), calls=%async_computation.48 | async-start | bytes 655360 | tf_op jit(solution)/shard_map/reduce_scatter | solution.py:448
  930.6 171.8 %reduce-scatter.58.cloned.1.call-start = ((), (), s32[]{:S(2)}) async-start(), calls=%async_computation.52 | async-start | bytes 327680 | tf_op jit(solution)/shard_map/reduce_scatter | solution.py:460
  934.0 204.2 %reduce-scatter.44.cloned.1.call-start = ((), (), s32[]{:S(2)}) async-start(), calls=%async_computation.45 | async-start | bytes 1966080 | tf_op jit(solution)/shard_map/reduce_scatter | solution.py:439
  939.0 235.8 %reduce-scatter.46.cloned.1.call-start = ((), (), s32[]{:S(2)}) async-start(), calls=%async_computation.46 | async-start | bytes 1966080 | tf_op jit(solution)/shard_map/reduce_scatter | solution.py:442
  943.7 349.8 %reduce-scatter.32.cloned.1.call-start = ((), (), s32[]{:S(2)}) async-start(), calls=%async_computation.33 | async-start | bytes 2621440 | tf_op jit(solution)/shard_map/reduce_scatter | solution.py:72
  949.7 386.5 %reduce-scatter.62.cloned.1.call-start = ((), (), s32[]{:S(2)}) async-start(), calls=%async_computation.55 | async-start | bytes 557056
  952.9 391.5 %all-reduce.11.cloned.1.call-start = ((), (), s32[]{:S(2)}) async-start(), calls=%async_computation.56 | async-start | bytes 4325376 | tf_op jit(solution)/shard_map/psum | solution.py:469
  (116 other events, 2498.3 us)
Sparse Core Ops, SparseCore 0:
  62.8 37.0 all-gather.23
  102.1 35.9 all-gather.21
  140.0 21.4 all-gather.19
  173.2 25.0 reduce-scatter.23
  234.1 24.8 reduce-scatter.25
  270.3 17.7 all-gather.27
  353.5 23.1 reduce-scatter.27
  411.8 31.4 reduce-scatter.29
  444.7 45.8 all-gather.33
  492.7 21.3 all-gather.31
  515.5 46.2 all-gather.35
  563.2 20.8 all-gather.37
  597.4 31.4 reduce-scatter.33
  630.9 16.7 all-gather.41
  649.8 22.5 all-gather.39
  688.5 24.8 reduce-scatter.35
  716.5 16.7 all-gather.43
  744.8 24.8 reduce-scatter.37
  802.2 24.8 reduce-scatter.59
  830.1 24.8 reduce-scatter.39
  884.5 24.8 reduce-scatter.55
  911.7 31.4 reduce-scatter.41
  945.6 43.8 reduce-scatter.51
  991.8 43.1 reduce-scatter.53
  1037.8 20.9 reduce-scatter.47
  1061.7 19.8 reduce-scatter.49
  1084.6 17.8 reduce-scatter.57
  1104.6 33.5 reduce-scatter.43
  1140.5 34.2 reduce-scatter.45
  1177.3 30.4 reduce-scatter.31
  1212.2 55.7 reduce-scatter.61
  1270.6 65.6 all-reduce.10
  (5 shorter events, 73.9 us)
where the time goes:
time: 1380 us; the launch traced here: 1360 us
  waiting for transfers between devices  700 us (51%)
  matrix products  199 us (14%)
  blocking collectives  193 us (14%)
  local copies, waits for them, and re-layouts  164 us (12%)
  other arithmetic  69.7 us (5%)
  between operations  18.4 us (1%)
  starting transfers between devices  17.9 us (1%)
    reduce_scatter x12, waiting for transfers between devices, rows_part(): lax.psum_scatter(whole_rows.astype(jnp.bfloat16), 'tensor', scatter_dimen...  174 us
    all_gather x12, waiting for transfers between devices, rows_full(): return lax.all_gather(part_rows, 'tensor', axis=1, tiled=True)  145 us
    unnamed x3, blocking collectives  72.1 us
    reduce_scatter x1, waiting for transfers between devices, shards(): lax.psum_scatter(grad_w_out.astype(jnp.bfloat16), 'shard', scatter_dimens...  45.5 us
    all_gather x1, waiting for transfers between devices, shards(): lax.all_gather(mlp_in, 'shard', axis=0, tiled=True)  42.6 us
    unnamed x227, local copies, waits for them, and re-layouts  39.4 us
    psum x1, blocking collectives, shards(): totals = lax.psum(squares, ('shard', 'context', 'tensor'))  37.1 us
    reduce_scatter x1, waiting for transfers between devices, shards(): lax.psum_scatter(grad_w_sqkv.astype(jnp.bfloat16), 'shard', scatter_dimen...  36.6 us
  transfers between devices with their start and end apart: 43, of which 30 were waited for; matrix products, arithmetic and copies ran while one was open for 23% of the time, Pallas kernels for 0%

commit v1 on v0

v1 whole, which is shorter than its diff:
```python
import functools

import jax
import jax.numpy as jnp
from jax import lax
from jax.experimental import pallas as pl
from jax.experimental.pallas import tpu as pltpu
from jax.sharding import PartitionSpec as P

HS = 128
BLK = 512
NBUCKET = 32
EDGES = (12, 16, 23, 32, 46, 64, 91)
LOW = jnp.bfloat16
F32 = jnp.float32
SCALE = HS ** (-0.5)
EPS = 1e-06
DIAG = 3 * BLK
VMEM_LIMIT = 60 * 1024 * 1024


def mm(a, b, ca, cb):
    return lax.dot_general(a, b, (((ca,), (cb,)), ((), ())), preferred_element_type=F32)


def whole():
    return pl.BlockSpec(memory_space=pltpu.VMEM)


def scalars():
    return pl.BlockSpec(memory_space=pltpu.SMEM)


def params(grid_rank=0):
    if grid_rank:
        return pltpu.CompilerParams(
            dimension_semantics=("arbitrary",) * grid_rank, vmem_limit_bytes=VMEM_LIMIT
        )
    return pltpu.CompilerParams(vmem_limit_bytes=VMEM_LIMIT)


def cost(flops, nbytes, trans=0):
    return pl.CostEstimate(flops=int(flops), bytes_accessed=int(nbytes), transcendentals=int(trans))


def rms_scale(v):
    return lax.rsqrt(jnp.mean(v * v, axis=-1, keepdims=True) + EPS)


def token_proj_kernel(count, me_ref, gain_ref, w_ref, *refs):
    pieces = refs[:count]
    q_ref, kv_ref, normed_ref = refs[count:]
    heads = w_ref.shape[0]
    rows = pieces[0].shape[0]
    for m in range(count):
        start = pl.multiple_of((me_ref[0] ^ m) * rows, rows)
        v = pieces[m][...].astype(F32)
        normed = (v * rms_scale(v) * gain_ref[...]).astype(LOW)
        normed_ref[pl.ds(start, rows), :] = normed
        for h in range(heads):
            out = mm(normed, w_ref[h], 1, 0).astype(LOW)
            q_ref[pl.ds(start, rows), h * HS : (h + 1) * HS] = out[:, :HS]
            kv_ref[pl.ds(start, rows), h * HS : (h + 1) * HS] = out[:, HS : 2 * HS]
            kv_ref[pl.ds(start, rows), (heads + h) * HS : (heads + h + 1) * HS] = out[:, 2 * HS :]


def token_proj(me, gain, weight, pieces):
    heads, width, _ = weight.shape
    rows = pieces[0].shape[0] * len(pieces)
    return pl.pallas_call(
        functools.partial(token_proj_kernel, len(pieces)),
        out_shape=(
            jax.ShapeDtypeStruct((rows, heads * HS), LOW),
            jax.ShapeDtypeStruct((rows, 2 * heads * HS), LOW),
            jax.ShapeDtypeStruct((rows, width), LOW),
        ),
        in_specs=[scalars(), whole(), whole()] + [whole()] * len(pieces),
        out_specs=(whole(),) * 3,
        compiler_params=params(),
        cost_estimate=cost(2 * rows * width * heads * 384, rows * width * 6),
        name="token_proj",
    )(me, gain, weight, *pieces)


def state_proj_kernel(count, w_ref, *refs):
    pieces = refs[:count]
    out_ref = refs[count]
    rows = pieces[0].shape[0]
    for m in range(count):
        for h in range(w_ref.shape[0]):
            out_ref[m * rows : (m + 1) * rows, h * 384 : (h + 1) * 384] = mm(
                pieces[m][...], w_ref[h], 1, 0
            ).astype(LOW)


def state_proj(weight, pieces):
    heads, width, _ = weight.shape
    rows = pieces[0].shape[0] * len(pieces)
    return pl.pallas_call(
        functools.partial(state_proj_kernel, len(pieces)),
        out_shape=jax.ShapeDtypeStruct((rows, heads * 384), LOW),
        in_specs=[whole()] * (1 + len(pieces)),
        out_specs=whole(),
        compiler_params=params(),
        cost_estimate=cost(2 * rows * width * heads * 384, rows * width * 4),
        name="state_proj",
    )(weight, *pieces)


def proj_back_kernel(first, g_ref, w_ref, out_ref):
    span = w_ref.shape[2] - first
    total = None
    for h in range(w_ref.shape[0]):
        term = mm(g_ref[:, h * span : (h + 1) * span], w_ref[h, :, first:], 1, 1)
        total = term if total is None else total + term
    out_ref[...] = total.astype(LOW)


def proj_back(grads, weight, first):
    heads, width, _ = weight.shape
    rows = grads.shape[0]
    tile = min(256, rows)
    return pl.pallas_call(
        functools.partial(proj_back_kernel, first),
        grid=(rows // tile,),
        out_shape=jax.ShapeDtypeStruct((rows, width), LOW),
        in_specs=[
            pl.BlockSpec((tile, grads.shape[1]), lambda i: (i, 0)),
            pl.BlockSpec(weight.shape, lambda i: (0, 0, 0)),
        ],
        out_specs=pl.BlockSpec((tile, width), lambda i: (i, 0)),
        compiler_params=params(1),
        cost_estimate=cost(2 * rows * width * grads.shape[1], rows * width * 4),
        name="proj_back",
    )(grads, weight)


def column_softmax(scores):
    peak = jnp.max(scores, axis=0, keepdims=True)
    exponent = jnp.exp(scores - peak)
    return exponent * (1.0 / jnp.sum(exponent, axis=0, keepdims=True))


def chain_forward_kernel(count, heads, blocks, start_ref, gain_ref, dec_ref, *refs):
    kv = refs[:count]
    w = refs[count : 2 * count]
    keep_ref, normed_ref, update_ref, last_ref = refs[2 * count :]
    span = heads * HS
    dec = dec_ref[...]
    state = start_ref[...]
    for b in range(blocks):
        lo, hi = b * BLK, (b + 1) * BLK
        keep_ref[b] = state
        normed = (state * rms_scale(state) * gain_ref[...]).astype(LOW)
        normed_ref[b] = normed
        update = None
        for m in range(count):
            q = mm(w[m][:span, :], normed, 1, 1).astype(LOW)
            mixed = []
            for h in range(heads):
                k = kv[m][lo:hi, h * HS : (h + 1) * HS]
                v = kv[m][lo:hi, (heads + h) * HS : (heads + h + 1) * HS]
                weights = column_softmax(mm(k, q[h * HS : (h + 1) * HS], 1, 0) * SCALE)
                mixed.append(mm(v, weights.astype(LOW), 0, 0).astype(LOW))
            mixed = mixed[0] if heads == 1 else jnp.concatenate(mixed, axis=0)
            term = mm(mixed, w[m][span:, :], 0, 0)
            update = term if update is None else update + term
        update_ref[b] = update
        state = dec * state + (1.0 - dec) * update
    last_ref[...] = state


def chain_forward(start, gain, dec, kv, weights, blocks):
    count = len(kv)
    rows, width = start.shape
    heads = kv[0].shape[1] // (2 * HS)
    flops = blocks * (4 * rows * width * count * heads * HS + 4 * rows * BLK * count * heads * HS)
    return pl.pallas_call(
        functools.partial(chain_forward_kernel, count, heads, blocks),
        out_shape=(
            jax.ShapeDtypeStruct((blocks, rows, width), F32),
            jax.ShapeDtypeStruct((blocks, rows, width), LOW),
            jax.ShapeDtypeStruct((blocks, rows, width), F32),
            jax.ShapeDtypeStruct((rows, width), F32),
        ),
        in_specs=[whole()] * (3 + 2 * count),
        out_specs=(whole(),) * 4,
        compiler_params=params(),
        cost_estimate=cost(flops, 8 * 1024 * 1024),
        name="chain_forward",
    )(start, gain, dec, *kv, *weights)


def chain_backward_kernel(
    count, heads, blocks, carry_ref, gain_ref, dec_ref, keep_ref, normed_ref, update_ref, gkv_ref, *refs
):
    kv = refs[:count]
    w = refs[count : 2 * count]
    gup_ref, last_ref, small_ref = refs[2 * count :]
    span = heads * HS
    dec = dec_ref[...]
    gain = gain_ref[...]
    carry = carry_ref[...]
    grad_dec = None
    grad_gain = None
    for b in reversed(range(blocks)):
        lo, hi = b * BLK, (b + 1) * BLK
        state = keep_ref[b]
        term = jnp.sum(carry * (state - update_ref[b]), axis=0, keepdims=True)
        grad_dec = term if grad_dec is None else grad_dec + term
        gup = ((1.0 - dec) * carry).astype(LOW)
        gup_ref[b] = gup
        normed = normed_ref[b]
        grad_normed = gkv_ref[b]
        for m in range(count):
            q = mm(w[m][:span, :], normed, 1, 1).astype(LOW)
            gmix = mm(w[m][span:, :], gup, 1, 1).astype(LOW)
            grad_q = []
            for h in range(heads):
                k = kv[m][lo:hi, h * HS : (h + 1) * HS]
                v = kv[m][lo:hi, (heads + h) * HS : (heads + h + 1) * HS]
                weights = column_softmax(mm(k, q[h * HS : (h + 1) * HS], 1, 0) * SCALE)
                grad_w = mm(v, gmix[h * HS : (h + 1) * HS], 1, 0)
                inner = jnp.sum(grad_w * weights, axis=0, keepdims=True)
                grad_s = (weights * (grad_w - inner)).astype(LOW)
                grad_q.append((mm(k, grad_s, 0, 0) * SCALE).astype(LOW))
            grad_q = grad_q[0] if heads == 1 else jnp.concatenate(grad_q, axis=0)
            grad_normed = grad_normed + mm(grad_q, w[m][:span, :], 0, 0)
        r = rms_scale(state)
        unit = state * r
        scaled = grad_normed * gain
        term = jnp.sum(grad_normed * unit, axis=0, keepdims=True)
        grad_gain = term if grad_gain is None else grad_gain + term
        carry = dec * carry + r * (
            scaled - unit * jnp.mean(scaled * unit, axis=-1, keepdims=True)
        )
    last_ref[...] = carry
    small_ref[0:1, :] = grad_gain
    small_ref[1:2, :] = grad_dec


def chain_backward(carry, gain, dec, keep, normed, update, gkv, kv, weights):
    count = len(kv)
    blocks, rows, width = keep.shape
    heads = kv[0].shape[1] // (2 * HS)
    flops = blocks * (6 * rows * width * count * heads * HS + 6 * rows * BLK * count * heads * HS)
    return pl.pallas_call(
        functools.partial(chain_backward_kernel, count, heads, blocks),
        out_shape=(
            jax.ShapeDtypeStruct((blocks, rows, width), LOW),
            jax.ShapeDtypeStruct((rows, width), F32),
            jax.ShapeDtypeStruct((2, width), F32),
        ),
        in_specs=[whole()] * (7 + 2 * count),
        out_specs=(whole(),) * 3,
        compiler_params=params(),
        cost_estimate=cost(flops, 10 * 1024 * 1024),
        name="chain_backward",
    )(carry, gain, dec, keep, normed, update, gkv, *kv, *weights)


def bucket_tile():
    lane = lax.broadcasted_iota(jnp.int32, (8, DIAG), 1)
    row = lax.broadcasted_iota(jnp.int32, (8, DIAG), 0)
    diff = lane - row
    diff = jnp.where(diff < 0, diff + DIAG, diff)
    offset = jnp.where(diff < BLK, diff, diff - DIAG) + BLK
    distance = jnp.abs(offset)
    far = jnp.full((8, DIAG), 8, jnp.int32)
    for edge in EDGES:
        far = far + (distance >= edge).astype(jnp.int32)
    near = jnp.where(distance < 8, distance, far)
    return jnp.where(offset >= 0, near, near + NBUCKET // 2)


def fill_bias(table_ref, h, bias_ref):
    bucket = bucket_tile()
    base = jnp.zeros((8, DIAG), F32)
    for k in range(NBUCKET):
        base = jnp.where(bucket == k, table_ref[h, k], base)

    def body(g, carry):
        rolled = pltpu.roll(base, 8 * g, 1)
        bias_ref[pl.ds(pl.multiple_of(8 * g, 8), 8), :] = rolled[:, :BLK]
        return carry

    lax.fori_loop(0, 2 * BLK // 8, body, 0, unroll=4)


def collapse_bias(grad_ref, out_ref):
    def body(g, acc):
        tile = grad_ref[pl.ds(pl.multiple_of(8 * g, 8), 8), :]
        wide = jnp.concatenate([tile, jnp.zeros((8, DIAG - BLK), F32)], axis=1)
        return acc + pltpu.roll(wide, lax.rem(DIAG - 8 * g, DIAG), 1)

    acc = lax.fori_loop(0, 2 * BLK // 8, body, jnp.zeros((8, DIAG), F32), unroll=4)
    bucket = bucket_tile()
    lane = lax.broadcasted_iota(jnp.int32, (8, HS), 1)
    out = jnp.zeros((8, HS), F32)
    for k in range(NBUCKET):
        out = jnp.where(lane == k, jnp.sum(jnp.where(bucket == k, acc, 0.0)), out)
    out_ref[...] = out


def current_mask(ids_col_ref, ids_row_ref):
    key = lax.broadcasted_iota(jnp.int32, (BLK, BLK), 0)
    query = lax.broadcasted_iota(jnp.int32, (BLK, BLK), 1)
    ids_row = ids_row_ref[...]
    return (key <= query) | ((ids_col_ref[...] == ids_row) & (ids_row > 0))


def attend_kernel(
    run_ref, table_ref, q_ref, kc_ref, vc_ref, kp_ref, vp_ref, ko_ref, vo_ref, ks_ref, vs_ref,
    row_ref, col_ref, out_ref, lse_ref, bias_ref, score_ref,
):
    h = pl.program_id(0)
    b = pl.program_id(1)

    @pl.when(b == 0)
    def _():
        fill_bias(table_ref, h, bias_ref)

    q = q_ref[...]
    first = b == 0
    keys = (
        ks_ref[...].reshape(BLK, HS),
        jnp.where(first, ko_ref[...], kp_ref[...]),
        kc_ref[...],
    )
    values = (
        vs_ref[...].reshape(BLK, HS),
        jnp.where(first, vo_ref[...], vp_ref[...]),
        vc_ref[...],
    )
    prior_ok = (run_ref[0] > 0) | (b > 0)
    score = mm(keys[0], q, 1, 1) * SCALE
    score_ref[0] = score
    peak = jnp.max(score, axis=0, keepdims=True)
    score = mm(keys[1], q, 1, 1) * SCALE + bias_ref[:BLK]
    score = jnp.where(prior_ok, score, -1e30)
    score_ref[1] = score
    peak = jnp.maximum(peak, jnp.max(score, axis=0, keepdims=True))
    score = mm(keys[2], q, 1, 1) * SCALE + bias_ref[BLK:]
    score = jnp.where(current_mask(col_ref, row_ref), score, -1e30)
    score_ref[2] = score
    peak = jnp.maximum(peak, jnp.max(score, axis=0, keepdims=True))
    total = jnp.zeros((1, BLK), F32)
    for c in range(3):
        exponent = jnp.exp(score_ref[c] - peak)
        score_ref[c] = exponent
        total = total + jnp.sum(exponent, axis=0, keepdims=True)
    inverse = 1.0 / total
    mixed = jnp.zeros((HS, BLK), F32)
    for c in range(3):
        mixed = mixed + mm(values[c], (score_ref[c] * inverse).astype(LOW), 0, 0)
    out_ref[...] = mixed.T.astype(LOW)
    lse_ref[...] = peak + jnp.log(total)


def attend_specs(heads, pieces, part, blocks):
    def at(col):
        return pl.BlockSpec((BLK, HS), lambda h, b: (b, col(h)))

    def before(col):
        return pl.BlockSpec((BLK, HS), lambda h, b: (jnp.maximum(b - 1, 0), col(h)))

    def outer(col):
        return pl.BlockSpec((BLK, HS), lambda h, b: (0, col(h)))

    def state(col):
        return pl.BlockSpec((pieces, None, part, HS), lambda h, b: (0, b, 0, col(h)))

    key, value = (lambda h: h), (lambda h: heads + h)
    return [
        scalars(),
        scalars(),
        at(key),
        at(key),
        at(value),
        before(key),
        before(value),
        outer(key),
        outer(value),
        state(lambda h: 3 * h + 1),
        state(lambda h: 3 * h + 2),
        pl.BlockSpec((None, 1, BLK), lambda h, b: (b, 0, 0)),
        pl.BlockSpec((None, BLK, 1), lambda h, b: (b, 0, 0)),
    ]


def attend(run, table, q, kv, outer, sproj, ids_row, ids_col):
    rows = q.shape[0]
    heads = q.shape[1] // HS
    pieces, blocks, part, _ = sproj.shape
    return pl.pallas_call(
        attend_kernel,
        grid=(heads, blocks),
        out_shape=(
            jax.ShapeDtypeStruct((rows, heads * HS), LOW),
            jax.ShapeDtypeStruct((heads, blocks, 1, BLK), F32),
        ),
        in_specs=attend_specs(heads, pieces, part, blocks),
        out_specs=(
            pl.BlockSpec((BLK, HS), lambda h, b: (b, h)),
            pl.BlockSpec((None, None, 1, BLK), lambda h, b: (h, b, 0, 0)),
        ),
        scratch_shapes=[pltpu.VMEM((2 * BLK, BLK), F32), pltpu.VMEM((3, BLK, BLK), F32)],
        compiler_params=params(2),
        cost_estimate=cost(
            heads * blocks * 12 * BLK * BLK * HS, 6 * 1024 * 1024, heads * blocks * 3 * BLK * BLK
        ),
        name="attend",
    )(run, table, q, kv, kv, kv, kv, outer, outer, sproj, sproj, ids_row, ids_col)


def attend_back_kernel(
    run_ref, table_ref, q_ref, kc_ref, vc_ref, kp_ref, vp_ref, ko_ref, vo_ref, ks_ref, vs_ref,
    row_ref, col_ref, gmix_ref, lse_ref,
    gq_ref, gkc_ref, gvc_ref, gkp_ref, gvp_ref, gs_ref, gtab_ref,
    bias_ref, gbias_ref, prob_ref, gprob_ref,
):
    h = pl.program_id(0)
    b = pl.program_id(1)

    @pl.when(b == 0)
    def _():
        fill_bias(table_ref, h, bias_ref)
        gbias_ref[...] = jnp.zeros_like(gbias_ref)

    q = q_ref[...]
    gmix = gmix_ref[...]
    lse = lse_ref[...]
    first = b == 0
    keys = (
        ks_ref[...].reshape(BLK, HS),
        jnp.where(first, ko_ref[...], kp_ref[...]),
        kc_ref[...],
    )
    values = (
        vs_ref[...].reshape(BLK, HS),
        jnp.where(first, vo_ref[...], vp_ref[...]),
        vc_ref[...],
    )
    prior_ok = (run_ref[0] > 0) | (b > 0)
    inner = jnp.zeros((1, BLK), F32)
    grad_values = []
    for c in range(3):
        score = mm(keys[c], q, 1, 1) * SCALE
        if c == 1:
            score = jnp.where(prior_ok, score + bias_ref[:BLK], -1e30)
        if c == 2:
            score = jnp.where(current_mask(col_ref, row_ref), score + bias_ref[BLK:], -1e30)
        prob = jnp.exp(score - lse)
        prob_ref[c] = prob
        grad_values.append(mm(prob.astype(LOW), gmix, 1, 0))
        grad_prob = mm(values[c], gmix, 1, 1)
        gprob_ref[c] = grad_prob
        inner = inner + jnp.sum(prob * grad_prob, axis=0, keepdims=True)
    grad_q = jnp.zeros((HS, BLK), F32)
    grad_keys = []
    for c in range(3):
        grad_score = (prob_ref[c] * (gprob_ref[c] - inner)).astype(LOW)
        if c > 0:
            gbias_ref[(c - 1) * BLK : c * BLK, :] += grad_score.astype(F32)
        grad_keys.append(mm(grad_score, q, 1, 0) * SCALE)
        grad_q = grad_q + mm(keys[c], grad_score, 0, 0)
    gq_ref[...] = (grad_q * SCALE).T.astype(LOW)
    part = gs_ref.shape[0], gs_ref.shape[1], HS
    gs_ref[:, :, :HS] = grad_keys[0].astype(LOW).reshape(part)
    gs_ref[:, :, HS:] = grad_values[0].astype(LOW).reshape(part)
    gkp_ref[...] = grad_keys[1]
    gvp_ref[...] = grad_values[1]
    gkc_ref[...] = grad_keys[2]
    gvc_ref[...] = grad_values[2]

    @pl.when(b == pl.num_programs(1) - 1)
    def _():
        collapse_bias(gbias_ref, gtab_ref)


def attend_back(run, table, q, kv, outer, sproj, ids_row, ids_col, gmix, lse):
    rows = q.shape[0]
    heads = q.shape[1] // HS
    pieces, blocks, part, _ = sproj.shape

    def at():
        return pl.BlockSpec((BLK, HS), lambda h, b: (b, h))

    side = jax.ShapeDtypeStruct((rows, heads * HS), F32)
    return pl.pallas_call(
        attend_back_kernel,
        grid=(heads, blocks),
        out_shape=(
            jax.ShapeDtypeStruct((rows, heads * HS), LOW),
            side,
            side,
            side,
            side,
            jax.ShapeDtypeStruct((pieces, blocks, part, heads * 2 * HS), LOW),
            jax.ShapeDtypeStruct((heads, 8, HS), F32),
        ),
        in_specs=attend_specs(heads, pieces, part, blocks)
        + [at(), pl.BlockSpec((None, None, 1, BLK), lambda h, b: (h, b, 0, 0))],
        out_specs=(
            at(),
            at(),
            at(),
            at(),
            at(),
            pl.BlockSpec((pieces, None, part, 2 * HS), lambda h, b: (0, b, 0, h)),
            pl.BlockSpec((None, 8, HS), lambda h, b: (h, 0, 0)),
        ),
        scratch_shapes=[
            pltpu.VMEM((2 * BLK, BLK), F32),
            pltpu.VMEM((2 * BLK, BLK), F32),
            pltpu.VMEM((3, BLK, BLK), F32),
            pltpu.VMEM((3, BLK, BLK), F32),
        ],
        compiler_params=params(2),
        cost_estimate=cost(
            heads * blocks * 30 * BLK * BLK * HS, 10 * 1024 * 1024, heads * blocks * 3 * BLK * BLK
        ),
        name="attend_back",
    )(run, table, q, kv, kv, kv, kv, outer, outer, sproj, sproj, ids_row, ids_col, gmix, lse)


def state_back_kernel(
    sq_ref, k_ref, v_ref, gmix_ref, gs_ref, gq_ref, gkc_ref, gvc_ref, gkn_ref, gvn_ref, gko_ref, gvo_ref,
    tok_ref, sproj_ref, smix_ref,
):
    b = pl.program_id(1)
    last = b == pl.num_programs(1) - 1
    pieces, part = gs_ref.shape[0], gs_ref.shape[1]
    sq = sq_ref[...].reshape(BLK, HS)
    gmix = gmix_ref[...].reshape(BLK, HS)
    k, v = k_ref[...], v_ref[...]
    weights = column_softmax(mm(k, sq, 1, 1) * SCALE)
    low = weights.astype(LOW)
    grad_w = mm(v, gmix, 1, 1)
    inner = jnp.sum(grad_w * weights, axis=0, keepdims=True)
    grad_s = (weights * (grad_w - inner)).astype(LOW)
    grad_k = mm(grad_s, sq, 1, 0) * SCALE
    grad_v = mm(low, gmix, 1, 0)
    grad_q = mm(k, grad_s, 0, 0) * SCALE
    smix = mm(v, low, 0, 0)
    later_k = jnp.where(last, gko_ref[...].astype(F32), gkn_ref[...])
    later_v = jnp.where(last, gvo_ref[...].astype(F32), gvn_ref[...])
    tok_ref[:, :HS] = gq_ref[...]
    tok_ref[:, HS : 2 * HS] = (gkc_ref[...] + grad_k + later_k).astype(LOW)
    tok_ref[:, 2 * HS :] = (gvc_ref[...] + grad_v + later_v).astype(LOW)
    sproj_ref[:, :, :HS] = grad_q.T.astype(LOW).reshape(pieces, part, HS)
    sproj_ref[:, :, HS:] = gs_ref[...]
    smix_ref[...] = smix.T.astype(LOW).reshape(pieces, part, HS)


def state_back(sproj, kv, gmix, gs, gq, gkc, gvc, gkp, gvp, outer):
    rows = gq.shape[0]
    heads = gq.shape[1] // HS
    pieces, blocks, part, _ = sproj.shape

    def at(col=lambda h: h):
        return pl.BlockSpec((BLK, HS), lambda h, b: (b, col(h)))

    def after():
        return pl.BlockSpec((BLK, HS), lambda h, b: (jnp.minimum(b + 1, blocks - 1), h))

    def state(width, col):
        return pl.BlockSpec((pieces, None, part, width), lambda h, b: (0, b, 0, col(h)))

    return pl.pallas_call(
        state_back_kernel,
        grid=(heads, blocks),
        out_shape=(
            jax.ShapeDtypeStruct((heads, rows, 384), LOW),
            jax.ShapeDtypeStruct((heads, pieces, blocks, part, 384), LOW),
            jax.ShapeDtypeStruct((pieces, blocks, part, heads * HS), LOW),
        ),
        in_specs=[
            state(HS, lambda h: 3 * h),
            at(),
            at(lambda h: heads + h),
            state(HS, lambda h: h),
            state(2 * HS, lambda h: h),
            at(),
            at(),
            at(),
            after(),
            after(),
            pl.BlockSpec((BLK, HS), lambda h, b: (0, h)),
            pl.BlockSpec((BLK, HS), lambda h, b: (0, heads + h)),
        ],
        out_specs=(
            pl.BlockSpec((None, BLK, 384), lambda h, b: (h, b, 0)),
            pl.BlockSpec((None, pieces, None, part, 384), lambda h, b: (h, 0, b, 0, 0)),
            state(HS, lambda h: h),
        ),
        compiler_params=params(2),
        cost_estimate=cost(heads * blocks * 14 * BLK * BLK * HS, 8 * 1024 * 1024),
        name="state_back",
    )(sproj, kv, kv, gmix, gs, gq, gkc, gvc, gkp, gvp, outer, outer)


def head_back_kernel(g_ref, w_ref, out_ref):
    total = None
    for h in range(w_ref.shape[0]):
        term = mm(g_ref[h], w_ref[h], 1, 1)
        total = term if total is None else total + term
    out_ref[...] = total.astype(LOW)


def head_back(grads, weight):
    heads, width, span = weight.shape
    rows = grads.shape[1]
    tile = 256
    return pl.pallas_call(
        head_back_kernel,
        grid=(rows // tile,),
        out_shape=jax.ShapeDtypeStruct((rows, width), LOW),
        in_specs=[
            pl.BlockSpec((heads, tile, span), lambda i: (0, i, 0)),
            pl.BlockSpec(weight.shape, lambda i: (0, 0, 0)),
        ],
        out_specs=pl.BlockSpec((tile, width), lambda i: (i, 0)),
        compiler_params=params(1),
        cost_estimate=cost(2 * rows * width * heads * span, rows * width * 4),
        name="head_back",
    )(grads, weight)


def passed_along(array, axis, by):
    size = lax.axis_size(axis)
    pairs = [(i, i + by) for i in range(size) if 0 <= i + by < size]
    return lax.ppermute(array, axis, pairs)


def swap(array, axis, bits):
    return lax.ppermute(array, axis, [(i, i ^ bits) for i in range(lax.axis_size(axis))])


def gather_rel(array):
    size = lax.axis_size("tensor")
    pieces = []
    for m in range(0, size, 2):
        piece = array if m == 0 else swap(array, "tensor", m)
        pieces += [piece, swap(piece, "tensor", 1)]
    return pieces


def reduce_rel(array):
    size = lax.axis_size("tensor")
    pairs = array.reshape((size // 2, 2) + array.shape[1:])
    got = swap(pairs[:, 1], "tensor", 1)
    sums = pairs[:, 0].astype(F32) + got.astype(F32)
    total = sums[0]
    for j in range(1, size // 2):
        total = total + swap(sums[j].astype(LOW), "tensor", 2 * j).astype(F32)
    return total


def exchange_rel(parts):
    return [part if m == 0 else swap(part, "tensor", m) for m, part in enumerate(parts)]


def cut(array, me):
    size = lax.axis_size("tensor")
    rows = array.shape[0] // size
    return [lax.dynamic_slice_in_dim(array, (me ^ m) * rows, rows, 0) for m in range(size)]


def place(pieces, me):
    rows = pieces[0].shape[0]
    out = jnp.zeros((rows * len(pieces),) + pieces[0].shape[1:], pieces[0].dtype)
    for m, piece in enumerate(pieces):
        out = lax.dynamic_update_slice_in_dim(out, piece, (me ^ m) * rows, 0)
    return out


def sum_all(array):
    for axis in ("tensor", "context", "shard"):
        bits = 1
        while bits < lax.axis_size(axis):
            array = array + swap(array, axis, bits)
            bits *= 2
    return array


def rms_back(v, gain, grad):
    r = rms_scale(v)
    unit = v * r
    scaled = grad * gain
    grad_v = r * (scaled - unit * jnp.mean(scaled * unit, axis=-1, keepdims=True))
    return grad_v, jnp.sum(grad * unit, axis=0)


def gelu_exact(features):
    return jax.nn.gelu(features, approximate=False)


def dot(a, b, ca, cb):
    return lax.dot_general(a, b, (((ca,), (cb,)), ((), ())), preferred_element_type=F32)


def shards(
    tokens,
    piece_ids,
    tok_qkv,
    state_qkv,
    tok_out,
    state_out,
    mlp_in,
    mlp_out,
    rel_bias,
    init_state,
    norm_gains,
    decay_param,
    cotangent,
):
    size = lax.axis_size("tensor")
    shard_count = lax.axis_size("shard")
    me = lax.axis_index("tensor")
    shard_pos = lax.axis_index("shard")
    run_pos = lax.axis_index("context")
    run_count = lax.axis_size("context")
    me_arr = me.astype(jnp.int32)[None]
    run_arr = run_pos.astype(jnp.int32)[None]
    own = tokens[0]
    own_rows, width = own.shape
    rows = own_rows * size
    blocks = rows // BLK
    heads = tok_qkv.shape[1]
    part = init_state.shape[0]
    span = heads * HS

    cols = norm_gains.shape[1]
    bias_rows = rel_bias.shape[0]
    small = jnp.concatenate(
        [norm_gains.reshape(-1), decay_param.reshape(-1), rel_bias.reshape(-1)]
    )
    small = lax.all_gather(small, ("shard", "tensor"), axis=0, tiled=False).astype(F32)
    vectors = (
        small[:, : 4 * cols].reshape(-1, 4, cols).transpose(1, 0, 2).reshape(4, width)
    )
    gains = vectors[:3]
    decay = jax.nn.sigmoid(vectors[3:4])
    tables = small[:, 4 * cols :].reshape(shard_count, size, bias_rows, heads)
    table = lax.dynamic_index_in_dim(tables, me, 1, keepdims=False).reshape(NBUCKET, heads).T

    w_tok = lax.all_gather(tok_qkv.transpose(1, 0, 2), "shard", axis=1, tiled=True)
    w_state = lax.all_gather(state_qkv.transpose(1, 0, 2), "shard", axis=1, tiled=True)
    outs = jnp.concatenate(
        [tok_out.reshape(span, -1), state_out.reshape(span, -1), init_state], axis=0
    )
    outs = lax.all_gather(outs, "shard", axis=1, tiled=True)
    w_tout, w_sout, start = outs[:span], outs[span : 2 * span], outs[2 * span :].astype(F32)
    w_in = lax.all_gather(mlp_in, "shard", axis=0, tiled=True)
    w_out = lax.all_gather(mlp_out, "shard", axis=1, tiled=True)

    token_pieces = gather_rel(own)
    q, kv, normed_a = token_proj(me_arr, gains[0:1], w_tok, token_pieces)
    chain_q = w_state[:, :, :HS].transpose(0, 2, 1).reshape(span, width)
    chain_w = gather_rel(jnp.concatenate([chain_q, w_sout], axis=0))
    kv_pieces = gather_rel(kv)
    outer = passed_along(kv[rows - BLK :], "context", 1)
    full_tout = jnp.concatenate(gather_rel(w_tout), axis=0)

    incoming = start
    for round_index in range(run_count):
        current = jnp.where(run_pos == 0, start, incoming)
        keep, normed_s, update, last = chain_forward(
            current, gains[2:3], decay, kv_pieces, chain_w, blocks
        )
        if round_index + 1 < run_count:
            incoming = passed_along(last.astype(LOW), "context", 1).astype(F32)
    state_pieces = gather_rel(normed_s.reshape(blocks * part, width))
    sproj = state_proj(w_state, state_pieces).reshape(size, blocks, part, heads * 384)

    ids_row = piece_ids.reshape(blocks, 1, BLK)
    ids_col = piece_ids.reshape(blocks, BLK, 1)
    mixed, lse = attend(run_arr, table, q, kv, outer, sproj, ids_row, ids_col)
    mixed_parts = cut(mixed, me)
    mixed_rel = jnp.concatenate(mixed_parts, axis=0)
    mixed_rows = jnp.concatenate(exchange_rel(mixed_parts), axis=1)
    branch_a = dot(mixed_rows, full_tout, 1, 0)
    inputs = own.astype(F32)
    residual = inputs + branch_a
    normed_m = (residual * rms_scale(residual) * gains[1]).astype(LOW)

    mlp_rows = jnp.concatenate(gather_rel(normed_m), axis=0)
    grad_rows = jnp.concatenate(gather_rel(cotangent[0]), axis=0)
    pre = dot(mlp_rows, w_in, 1, 0)
    hidden = gelu_exact(pre).astype(LOW)
    branch_m = reduce_rel(dot(hidden, w_out, 1, 0).astype(LOW).reshape(size, own_rows, width))
    output = residual + branch_m
    grad_hidden = dot(grad_rows, w_out, 1, 1)
    grad_pre = jax.vjp(gelu_exact, pre)[1](grad_hidden)[0].astype(LOW)
    grad_normed_m = reduce_rel(dot(grad_pre, w_in, 1, 1).astype(LOW).reshape(size, own_rows, width))
    grad_w_out = dot(hidden, grad_rows, 0, 0)
    grad_w_in = dot(mlp_rows, grad_pre, 0, 0)
    grad_res_n, grad_gain_m = rms_back(residual, gains[1], grad_normed_m)
    grad_res = cotangent[0].astype(F32) + grad_res_n

    grad_branch = grad_res.astype(LOW)
    grad_branch_rel = jnp.concatenate(gather_rel(grad_branch), axis=0)
    grad_w_tout = dot(mixed_rel, grad_branch_rel, 0, 0)
    gmix_rows = dot(grad_branch, full_tout, 1, 1).astype(LOW)
    gmix = place(
        exchange_rel([gmix_rows[:, m * span : (m + 1) * span] for m in range(size)]), me
    )
    gq, gkc, gvc, gkp, gvp, gs, gtab = attend_back(
        run_arr, table, q, kv, outer, sproj, ids_row, ids_col, gmix, lse
    )
    outer_back = passed_along(
        jnp.concatenate([gkp[:BLK], gvp[:BLK]], axis=1).astype(LOW), "context", -1
    )

    grad_state_kv = reduce_rel(
        proj_back(gs.reshape(-1, heads * 2 * HS), w_state, HS).reshape(
            size, blocks * part, width
        )
    ).reshape(blocks, part, width)
    incoming = jnp.zeros_like(start)
    for round_index in range(run_count):
        carry = jnp.where(run_pos == run_count - 1, 0.0, incoming)
        gup, first_grad, chain_small = chain_backward(
            carry, gains[2:3], decay, keep, normed_s, update, grad_state_kv, kv_pieces, chain_w
        )
        if round_index + 1 < run_count:
            incoming = passed_along(first_grad.astype(LOW), "context", -1).astype(F32)
    grad_start = jnp.where(run_pos == 0, first_grad, 0.0).astype(LOW)
    gup_rel = jnp.concatenate(gather_rel(gup.reshape(blocks * part, width)), axis=0)
    gsmix = dot(gup_rel, w_sout, 1, 1).astype(LOW).reshape(size, blocks, part, span)
    gtproj, gsproj, smix = state_back(sproj, kv, gsmix, gs, gq, gkc, gvc, gkp, gvp, outer_back)
    normed_s_rel = jnp.concatenate(state_pieces, axis=0)
    grad_w_state = jnp.einsum(
        "rd,hre->hde", normed_s_rel, gsproj.reshape(heads, -1, 384), preferred_element_type=F32
    )
    grad_w_sout = dot(smix.reshape(-1, span), gup_rel, 0, 0)

    grad_w_tok = jnp.einsum("rd,hre->hde", normed_a, gtproj, preferred_element_type=F32)
    partial = head_back(gtproj, w_tok)
    grad_normed_a = reduce_rel(jnp.stack(cut(partial, me)))
    grad_in_n, grad_gain_a = rms_back(inputs, gains[0], grad_normed_a)
    grad_tokens = (grad_res + grad_in_n).astype(LOW)

    def scatter(array, dim):
        return lax.psum_scatter(array.astype(LOW), "shard", scatter_dimension=dim, tiled=True)

    def both_runs(array):
        return array.astype(F32) + swap(array, "context", 1).astype(F32)

    g_in = both_runs(scatter(grad_w_in, 0))
    g_out = both_runs(scatter(grad_w_out, 1))
    g_state = both_runs(scatter(grad_w_state, 1)).transpose(1, 0, 2)
    g_outs = both_runs(
        scatter(jnp.concatenate([grad_w_tout.astype(LOW), grad_w_sout.astype(LOW), grad_start], 0), 1)
    )
    g_tok = both_runs(scatter(grad_w_tok, 1)).transpose(1, 0, 2)

    squares = jnp.stack(
        [jnp.sum(inputs * inputs), jnp.sum(branch_a * branch_a), jnp.sum(branch_m * branch_m)]
    )
    slot = gtab[:, 0, :NBUCKET].reshape(-1)
    slots = lax.dynamic_update_slice_in_dim(
        jnp.zeros((size * slot.size,), F32), slot, me * slot.size, 0
    )
    tail = jnp.concatenate([slots, squares])
    tail = jnp.pad(tail, (0, width - tail.size))
    grad_decay = chain_small[1] * (decay * (1.0 - decay))[0]
    sums = sum_all(
        jnp.stack([grad_gain_a, grad_gain_m, chain_small[0], grad_decay, tail])
    )
    place_at = (shard_pos * size + me) * cols
    mine = lax.dynamic_slice_in_dim(sums[:4], place_at, cols, 1)
    table_sum = lax.dynamic_slice_in_dim(sums[4], me * slot.size, slot.size, 0)
    table_sum = table_sum.reshape(heads, NBUCKET).T
    g_table = lax.dynamic_slice_in_dim(table_sum, shard_pos * bias_rows, bias_rows, 0)
    entries = inputs.size * shard_count * run_count * size
    first = size * slot.size
    rms_out = jnp.sqrt(sums[4, first : first + 3] / entries)

    return (
        output.astype(LOW)[None],
        grad_tokens[None],
        g_tok,
        g_state,
        g_outs[:span].reshape(heads, HS, -1),
        g_outs[span : 2 * span].reshape(heads, HS, -1),
        g_in,
        g_out,
        g_table,
        g_outs[2 * span :],
        mine[:3],
        mine[3],
        rms_out,
    )


def solution(mesh):
    return jax.shard_map(
        shards,
        mesh=mesh,
        in_specs=(
            P("shard", ("context", "tensor"), None),
            P("shard", "context"),
            P("shard", "tensor", None),
            P("shard", "tensor", None),
            P("tensor", None, "shard"),
            P("tensor", None, "shard"),
            P("shard", "tensor"),
            P("tensor", "shard"),
            P("shard", "tensor"),
            P("tensor", "shard"),
            P(None, ("shard", "tensor")),
            P(("shard", "tensor")),
            P("shard", ("context", "tensor"), None),
        ),
        out_specs=(
            P("shard", ("context", "tensor"), None),
            P("shard", ("context", "tensor"), None),
            P("shard", "tensor", None),
            P("shard", "tensor", None),
            P("tensor", None, "shard"),
            P("tensor", None, "shard"),
            P("shard", "tensor"),
            P("tensor", "shard"),
            P("shard", "tensor"),
            P("tensor", "shard"),
            P(None, ("shard", "tensor")),
            P(("shard", "tensor")),
            P(),
        ),
        check_vma=False,
    )
```

time: 1380 us -> 667 us (0.48)
  waiting for transfers between devices: 700 us -> 248 us
  Pallas kernels: 0 us -> 147 us
  matrix products: 199 us -> 61.6 us
  blocking collectives: 193 us -> 63.6 us
  local copies, waits for them, and re-layouts: 164 us -> 38.7 us
  other arithmetic: 69.7 us -> 37.7 us
  starting transfers between devices: 17.9 us -> 44.6 us
    reduce_scatter x19 -> x5, waiting for transfers between devices: 393 us -> 25.2 us  [scatter(): lax.psum_scatter(array.astype(LOW), 'shard', scatter_dimension=dim, tiled...]
    all_gather x16 -> x5, waiting for transfers between devices: 290 us -> 36.4 us  [the longest x1 19.9 us: shards(): w_out = lax.all_gather(mlp_out, 'shard', axis=1, tiled=True)]
    ppermute x0 -> x51, waiting for transfers between devices: none -> 164 us  [swap(): lax.ppermute(array, axis, [(i, i ^ bits) for i in range(lax.axis_size(axi...]
    pallas_call x0 -> x11, Pallas kernels: none -> 147 us  [the longest x2 35.5 us: chain_backward(): pl.pallas_call(functools.partial(chain_backward_kernel, count, heads, blo...]
    dot_general x58 -> x13, matrix products: 186 us -> 61.6 us  [the longest x11 51.9 us: dot(): lax.dot_general(a, b, (((ca,), (cb,)), ((), ())), preferred_element_type=...]
    all_gather x5 -> x0, blocking collectives: 78.6 us -> none  [the longest x1 23.5 us: shards(): lax.all_gather(norm_gains, ('shard', 'tensor'), axis=1, tiled=True)]
    rev x2 -> x0, local copies, waits for them, and re-layouts: 68.8 us -> none  [the longest x1 34.4 us: collapse_bias(): grad_window[:, :, ::-1]]
    psum x2 -> x0, blocking collectives: 42.2 us -> none  [the longest x1 37.1 us: shards(): totals = lax.psum(squares, ('shard', 'context', 'tensor'))]
  transfers between devices with their start and end apart: 43 -> 65, of which waited for: 30 -> 27; matrix products, arithmetic and copies ran while one was open for 23% -> 17% of each run, Pallas kernels for 0% -> 18%
where the time goes in v1:
time: 667 us; the launch traced here: 657 us
  waiting for transfers between devices  248 us (37%)
  Pallas kernels  147 us (22%)
  blocking collectives  63.6 us (10%)
  matrix products  61.6 us (9%)
  starting transfers between devices  44.6 us (7%)
  local copies, waits for them, and re-layouts  38.7 us (6%)
  other arithmetic  37.7 us (6%)
  between operations  16.3 us (2%)
    ppermute x51, waiting for transfers between devices, swap(): lax.ppermute(array, axis, [(i, i ^ bits) for i in range(lax.axis_size(axi...  164 us
    unnamed x1, blocking collectives  63.6 us
    dot_general x11, matrix products, dot(): lax.dot_general(a, b, (((ca,), (cb,)), ((), ())), preferred_element_type=...  51.9 us
    pallas_call x2, Pallas kernels, chain_backward(): pl.pallas_call(functools.partial(chain_backward_kernel, count, heads, blo...  35.5 us
    ppermute x51, starting transfers between devices, swap(): lax.ppermute(array, axis, [(i, i ^ bits) for i in range(lax.axis_size(axi...  32 us
    pallas_call x1, Pallas kernels, attend_back(): pl.pallas_call(attend_back_kernel, grid=(heads, blocks), out_shape=(jax.S...  31.4 us
    pallas_call x2, Pallas kernels, chain_forward(): pl.pallas_call(functools.partial(chain_forward_kernel, count, heads, bloc...  30.5 us
    reduce_scatter x5, waiting for transfers between devices, scatter(): lax.psum_scatter(array.astype(LOW), 'shard', scatter_dimension=dim, tiled...  25.2 us
  transfers between devices with their start and end apart: 65, of which 27 were waited for; matrix products, arithmetic and copies ran while one was open for 17% of the time, Pallas kernels for 18%

profile of v1, /device:TPU:0, one launch (start us, length us, event | category | flops | bytes accessed | tf_op | source)
XLA Modules:
  0.0 656.9 jit_solution(8357934063068917082)
XLA Ops:
  17.4 10.5 %collective-permute-done.1.refs_2_ = bf16[256,1024]{1,0:T(8,128)(2,1)S(1)} collective-permute-done((bf16[256,1024]{1,0:T(8,128)(2,1)}, bf16[256,1024]{1,0:T(8,128)(2,1)S(1)}, u32[]{:S(2)}, u32[]{:S(2)}) %collective-permute-start.1) | collective-permute-done | bytes 524320 | tf_op jit(solution)/shard_map/ppermute | solution.py:637
  30.9 63.6 %all-reduce.1 = bf16[4352]{0:T(1024)(128)(2,1)S(1)} all-reduce(bf16[4352]{0:T(1024)(128)(2,1)S(1)} %dynamic-update-slice), channel_id=2, replica_groups=mesh['shard'=4,'context'=2,'tensor'=4] {'shard','tensor'}, use_global_device_ids=true, to_apply=%add.1 | all-reduce | flops 4352 | bytes 17408
  99.2 6.5 token_proj.1
  105.6 16.5 %all-gather.9.cloned.1.call-done.w_ref = bf16[2,1024,384]{2,1,0:T(8,128)(2,1)} async-done(((bf16[2,256,384]{2,1,0:T(8,128)(2,1)}), bf16[2,1024,384]{2,1,0:T(8,128)(2,1)}) %all-gather.9.cloned.1.call-update) | async-done | bytes 1572880 | tf_op jit(solution)/shard_map/all_gather | solution.py:749
  127.6 22.8 %collective-permute-done.8.refs_6_ = bf16[512,1024]{1,0:T(8,128)(2,1)} collective-permute-done((bf16[512,1024]{1,0:T(8,128)(2,1)S(1)}, bf16[512,1024]{1,0:T(8,128)(2,1)}, u32[]{:S(2)}, u32[]{:S(2)}) %collective-permute-start.8) | collective-permute-done | bytes 1048608 | tf_op jit(solution)/shard_map/ppermute | solution.py:637
  153.6 15.2 %chain_forward.2 = (f32[2,128,1024]{2,1,0:T(8,128)}, bf16[2,128,1024]{2,1,0:T(8,128)(2,1)}, f32[2,128,1024]{2,1,0:T(8,128)}, f32[128,1024]{1,0:T(8,128)}) custom-call(f32[128,1024]{1,0:T(8,128)} %slice_convert_fusion.6.start_ref, f32[1,1024]{1,0:T(1,128)} %slice.163.gain_ref, f32[1,1024]{1,0:T(1,128)} %div.22.dec_ref, ...), custom_call_target="tpu_custom_call" | custom-call | flops 1610612736 | bytes 8388608 | tf_op jit(solution)/shard_map/chain_forward/pallas_call | solution.py:178
  173.7 5.7 collective-permute-done.10
  181.3 15.3 %chain_forward.3 = (f32[2,128,1024]{2,1,0:T(8,128)}, bf16[2,128,1024]{2,1,0:T(8,128)(2,1)}, f32[2,128,1024]{2,1,0:T(8,128)}, f32[128,1024]{1,0:T(8,128)}) custom-call(f32[128,1024]{1,0:T(8,128)} %convert_select_fusion.1.start_ref, f32[1,1024]{1,0:T(1,128)} %slice.163.gain_ref, f32[1,1024]{1,0:T(1,128)} %div.22.dec_ref, ...), custom_call_target="tpu_custom_call" | custom-call | flops 1610612736 | bytes 8388608 | tf_op jit(solution)/shard_map/chain_forward/pallas_call | solution.py:178
  198.8 12.9 %collective-permute-done.12.refs_2_ = bf16[256,1024]{1,0:T(8,128)(2,1)S(1)} collective-permute-done((bf16[256,1024]{1,0:T(8,128)(2,1)}, bf16[256,1024]{1,0:T(8,128)(2,1)S(1)}, u32[]{:S(2)}, u32[]{:S(2)}) %collective-permute-start.12) | collective-permute-done | bytes 524320 | tf_op jit(solution)/shard_map/ppermute | solution.py:637
  228.8 17.7 %attend.1 = (bf16[1024,256]{1,0:T(8,128)(2,1)}, f32[2,2,1,512]{3,2,1,0:T(1,128)}) custom-call(s32[1]{0:T(128)} %bitcast.1.run_ref, f32[2,32]{1,0:T(2,128)} %bitcast.235, bf16[1024,256]{1,0:T(8,128)(2,1)} %get-tuple-element.36.q_ref, bf16[1024,512]{1,0:T(8,128)(2,1)} %get-tuple-element.37.refs_0_.kc_ref.vc_ref.kp_ref.vp_ref.k_ref.v_ref, ...), custom_call_target="tpu_custom_call" | custom-call | flops 1610612736 | bytes 6291456 | tf_op jit(solution)/shard_map/attend/pallas_call | solution.py:395
  261.2 12.7 %collective-permute-done.21 = bf16[256,1024]{1,0:T(8,128)(2,1)} collective-permute-done((bf16[256,1024]{1,0:T(8,128)(2,1)S(1)}, bf16[256,1024]{1,0:T(8,128)(2,1)}, u32[]{:S(2)}, u32[]{:S(2)}) %collective-permute-start.21) | collective-permute-done | bytes 524320 | tf_op jit(solution)/shard_map/ppermute | solution.py:637
  274.5 10.2 %collective-permute-done.26 = bf16[256,1024]{1,0:T(8,128)(2,1)S(1)} collective-permute-done((bf16[256,1024]{1,0:T(8,128)(2,1)S(1)}, bf16[256,1024]{1,0:T(8,128)(2,1)S(1)}, u32[]{:S(2)}, u32[]{:S(2)}) %collective-permute-start.26) | collective-permute-done | bytes 524320 | tf_op jit(solution)/shard_map/ppermute | solution.py:637
  284.8 15.9 %multiply_convert_fusion = (bf16[1024,1024]{1,0:T(8,128)(2,1)}, f32[1024,1024]{1,0:T(8,128)}, f32[1024,1024]{1,0:T(8,128)}) fusion(bf16[1024,1024]{1,0:T(8,128)(2,1)} %all-gather.13.cloned.1.call-done, bf16[256,1024]{1,0:T(8,128)(2,1)} %collective-permute-done.22, bf16[256,1024]{1,0:T(8,128)(2,1)} %collective-permute-done.21, ...), kind=kOutput, calls=%fused_computation.3 | convolution fusion | flops 2224029696 | bytes 14680064 | tf_op jit(solution)/shard_map/dot_general | solution.py:700
  300.7 19.9 %all-gather.15.cloned.1.call-done = bf16[1024,1024]{1,0:T(8,128)(2,1)} async-done(((bf16[1024,256]{1,0:T(8,128)(2,1)}), bf16[1024,1024]{1,0:T(8,128)(2,1)}) %all-gather.15.cloned.1.call-update) | async-done | bytes 2097168 | tf_op jit(solution)/shard_map/all_gather | solution.py:756
  320.6 7.9 %add_convert_fusion = bf16[1024,1024]{1,0:T(8,128)(2,1)S(1)} fusion(f32[1024,1024]{1,0:T(8,128)} %get-tuple-element.107, f32[1024,1024]{1,0:T(8,128)} %get-tuple-element.139, bf16[1024,1024]{1,0:T(8,128)(2,1)} %all-gather.15.cloned.1.call-done, bf16[256,1024]{1,0:T(8,128)(2,1)} %collective-permute-done.27, ...), kind=kOutput, calls=%fused_computation.2 | convolution fusion | flops 2170552320 | bytes 14680064 | tf_op jit(solution)/shard_map/dot_general | solution.py:700
  347.3 10.6 %collective-permute-done.29 = bf16[256,1024]{1,0:T(8,128)(2,1)S(1)} collective-permute-done((bf16[256,1024]{1,0:T(8,128)(2,1)S(1)}, bf16[256,1024]{1,0:T(8,128)(2,1)S(1)}, u32[]{:S(2)}, u32[]{:S(2)}) %collective-permute-start.29) | collective-permute-done | bytes 524320 | tf_op jit(solution)/shard_map/ppermute | solution.py:637
  358.4 9.9 %collective-permute-done.24 = bf16[256,1024]{1,0:T(8,128)(2,1)S(1)} collective-permute-done((bf16[256,1024]{1,0:T(8,128)(2,1)S(1)}, bf16[256,1024]{1,0:T(8,128)(2,1)S(1)}, u32[]{:S(2)}, u32[]{:S(2)}) %collective-permute-start.24) | collective-permute-done | bytes 524320 | tf_op jit(solution)/shard_map/ppermute | solution.py:637
  381.9 31.4 %attend_back.1 = (bf16[1024,256]{1,0:T(8,128)(2,1)}, f32[1024,256]{1,0:T(8,128)}, f32[1024,256]{1,0:T(8,128)}, f32[1024,256]{1,0:T(8,128)}, f32[1024,256]{1,0:T(...) custom-call(s32[1]{0:T(128)} %bitcast.1.run_ref, f32[2,32]{1,0:T(2,128)} %bitcast.236, ...), custom_call_target="tpu_custom_call" | custom-call | flops 4026531840 | bytes 10485760 | tf_op jit(solution)/shard_map/attend_back/pallas_call | solution.py:490
  421.3 5.7 convolution_convert_fusion
  430.6 12.4 %collective-permute-done.34 = bf16[256,1024]{1,0:T(8,128)(2,1)S(1)} collective-permute-done((bf16[256,1024]{1,0:T(8,128)(2,1)S(1)}, bf16[256,1024]{1,0:T(8,128)(2,1)S(1)}, u32[]{:S(2)}, u32[]{:S(2)}) %collective-permute-start.34) | collective-permute-done | bytes 524320 | tf_op jit(solution)/shard_map/ppermute | solution.py:637
  445.0 17.8 %chain_backward.2 = (bf16[2,128,1024]{2,1,0:T(8,128)(2,1)}, f32[128,1024]{1,0:T(8,128)}, f32[2,1024]{1,0:T(2,128)}) custom-call(f32[128,1024]{1,0:T(8,128)} %broadcast_in_dim.34.carry_ref, f32[1,1024]{1,0:T(1,128)} %slice.163.gain_ref, f32[1,1024]{1,0:T(1,128)} %div.22.dec_ref, f32[2,128,1024]{2,1,0:T(8,128)} %get-tuple-element.41.keep_ref, ...), custom_call_target="tpu_custom_call" | custom-call | flops 2415919104 | bytes 10485760 | tf_op jit(solution)/shard_map/chain_backward/pallas_call | solution.py:247
  467.0 6.4 collective-permute-done.35
  474.3 17.7 %chain_backward.3 = (bf16[2,128,1024]{2,1,0:T(8,128)(2,1)}, f32[128,1024]{1,0:T(8,128)}, f32[2,1024]{1,0:T(2,128)}) custom-call(f32[128,1024]{1,0:T(8,128)} %convert_select_fusion.carry_ref, f32[1,1024]{1,0:T(1,128)} %slice.163.gain_ref, f32[1,1024]{1,0:T(1,128)} %div.22.dec_ref, f32[2,128,1024]{2,1,0:T(8,128)} %get-tuple-element.41.keep_ref, ...), custom_call_target="tpu_custom_call" | custom-call | flops 2415919104 | bytes 10485760 | tf_op jit(solution)/shard_map/chain_backward/pallas_call | solution.py:247
  496.2 8.4 %collective-permute-done.37 = bf16[256,1024]{1,0:T(8,128)(2,1)S(1)} collective-permute-done((bf16[256,1024]{1,0:T(8,128)(2,1)}, bf16[256,1024]{1,0:T(8,128)(2,1)S(1)}, u32[]{:S(2)}, u32[]{:S(2)}) %collective-permute-start.37) | collective-permute-done | bytes 524320 | tf_op jit(solution)/shard_map/ppermute | solution.py:637
  511.2 9.8 %collective-permute-done.39.gko_ref.gvo_ref = bf16[512,512]{1,0:T(8,128)(2,1)S(1)} collective-permute-done((bf16[512,512]{1,0:T(8,128)(2,1)S(1)}, bf16[512,512]{1,0:T(8,128)(2,1)S(1)}, u32[]{:S(2)}, u32[]{:S(2)}) %collective-permute-start.39) | collective-permute-done | bytes 524320 | tf_op jit(solution)/shard_map/ppermute | solution.py:633
  521.8 8.9 %state_back.1 = (bf16[2,1024,384]{2,1,0:T(8,128)(2,1)}, bf16[2,4,2,128,384]{4,3,2,1,0:T(8,128)(2,1)}, bf16[4,2,128,256]{3,2,1,0:T(8,128)(2,1)}) custom-call(bf16[4,2,128,768]{3,2,1,0:T(8,128)(2,1)} %bitcast.198, bf16[1024,512]{1,0:T(8,128)(2,1)} %get-tuple-element.37.refs_0_.kc_ref.vc_ref.kp_ref.vp_ref.k_ref.v_ref, ...), custom_call_target="tpu_custom_call" | custom-call | flops 1879048192 | bytes 8388608 | tf_op jit(solution)/shard_map/state_back/pallas_call | solution.py:570
  539.2 5.8 head_back.1
  563.1 7.9 %collective-permute-done.41 = bf16[256,1024]{1,0:T(8,128)(2,1)} collective-permute-done((bf16[256,1024]{1,0:T(8,128)(2,1)}, bf16[256,1024]{1,0:T(8,128)(2,1)}, u32[]{:S(2)}, u32[]{:S(2)}) %collective-permute-start.41) | collective-permute-done | bytes 524320 | tf_op jit(solution)/shard_map/ppermute | solution.py:637
  578.0 6.9 %collective-permute-done.49 = bf16[1024,256]{1,0:T(8,128)(2,1)} collective-permute-done((bf16[1024,256]{1,0:T(8,128)(2,1)}, bf16[1024,256]{1,0:T(8,128)(2,1)}, u32[]{:S(2)}, u32[]{:S(2)}) %collective-permute-start.49) | collective-permute-done | bytes 524320 | tf_op jit(solution)/shard_map/ppermute | solution.py:637
  602.9 7.7 %collective-permute-done.47 = bf16[640,256]{1,0:T(8,128)(2,1)S(1)} collective-permute-done((bf16[640,256]{1,0:T(8,128)(2,1)}, bf16[640,256]{1,0:T(8,128)(2,1)S(1)}, u32[]{:S(2)}, u32[]{:S(2)}) %collective-permute-start.47) | collective-permute-done | bytes 327712 | tf_op jit(solution)/shard_map/ppermute | solution.py:637
  612.3 25.1 %reduce-scatter.6.cloned.1.call-done = bf16[2,256,384]{1,2,0:T(8,128)(2,1)} async-done(((bf16[2,1024,384]{1,2,0:T(8,128)(2,1)}), bf16[2,256,384]{1,2,0:T(8,128)(2,1)}) %reduce-scatter.6.cloned.1.call-update) | async-done | bytes 393232 | tf_op jit(solution)/shard_map/reduce_scatter | solution.py:846
  642.0 6.4 collective-permute-done.42
  (335 shorter events, 188.3 us)
Async XLA Ops:
  7.2 88.8 %all-gather.11.cloned.1.call-start = ((), (), s32[]{:S(2)}) async-start(), calls=%async_computation.7 | async-start | bytes 1638400 | tf_op jit(solution)/shard_map/all_gather | solution.py:753
  9.0 89.3 %all-gather.7.cloned.1.call-start = ((), (), s32[]{:S(2)}) async-start(), calls=%async_computation.5 | async-start | bytes 1966080 | tf_op jit(solution)/shard_map/all_gather | solution.py:748
  10.9 111.3 %all-gather.9.cloned.1.call-start = ((), (), s32[]{:S(2)}) async-start(), calls=%async_computation.6 | async-start | bytes 1966080 | tf_op jit(solution)/shard_map/all_gather | solution.py:749
  12.7 272.0 %all-gather.13.cloned.1.call-start = ((), (), s32[]{:S(2)}) async-start(), calls=%async_computation.8 | async-start | bytes 2621440 | tf_op jit(solution)/shard_map/all_gather | solution.py:755
  15.8 82.4 %collective-permute-start = (bf16[256,1024]{1,0:T(8,128)(2,1)}, bf16[256,1024]{1,0:T(8,128)(2,1)S(1)}, u32[]{:S(2)}, u32[]{:S(2)}) collective-permute-start(bf16[256,1024]{1,0:T(8,128)(2,1)} %bitcast.207), channel_id=1, source_target_pairs={{0,1},{1,0},{2,3},{3,2},{4,5},{5,4},{6,7},{7,6},{8,9},{9,8},{10,11... | collective-permute-start | bytes 1572872 | tf_op jit(solution)/shard_map/ppermute | solution.py:637
  27.9 70.3 %collective-permute-start.2 = (bf16[256,1024]{1,0:T(8,128)(2,1)S(1)}, bf16[256,1024]{1,0:T(8,128)(2,1)S(1)}, u32[]{:S(2)}, u32[]{:S(2)}) collective-permute-start(bf16[256,1024]{1,0:T(8,128)(2,1)S(1)} %collective-permute-done.1.refs_2_), channel_id=1, source_target_pairs={{0,1},{1,0},{2,3},{3,2},{4,5},{5,4},{6,7},{7,6},{8,9},{9,8},{10,11... | collective-permute-start | bytes 1572872 | tf_op jit(solution)/shard_map/ppermute | solution.py:637
  105.6 21.9 %collective-permute-start.5 = (bf16[1024,512]{1,0:T(8,128)(2,1)}, bf16[1024,512]{1,0:T(8,128)(2,1)S(1)}, u32[]{:S(2)}, u32[]{:S(2)}) collective-permute-start(bf16[1024,512]{1,0:T(8,128)(2,1)} %get-tuple-element.37.refs_0_.kc_ref.vc_ref.kp_ref.vp_ref.k_ref.v_ref), channel_id=1, source_target_pairs={{0,2},{1,3},{2,0},{3,1},{4,6},{5,7},{6,4},{7,5},{8,10},{9,11},{10,... | collective-permute-start | bytes 3145736 | tf_op jit(solution)/shard_map/ppermute | solution.py:637
  125.5 24.9 %collective-permute-start.8 = (bf16[512,1024]{1,0:T(8,128)(2,1)S(1)}, bf16[512,1024]{1,0:T(8,128)(2,1)}, u32[]{:S(2)}, u32[]{:S(2)}) collective-permute-start(bf16[512,1024]{1,0:T(8,128)(2,1)S(1)} %pad_maximum_fusion.6.refs_4_), channel_id=1, source_target_pairs={{0,2},{1,3},{2,0},{3,1},{4,6},{5,7},{6,4},{7,5},{8,10},{9,11},{10,... | collective-permute-start | bytes 3145736 | tf_op jit(solution)/shard_map/ppermute | solution.py:637
  127.1 26.5 %collective-permute-start.4 = (bf16[1024,512]{1,0:T(8,128)(2,1)S(1)}, bf16[1024,512]{1,0:T(8,128)(2,1)}, u32[]{:S(2)}, u32[]{:S(2)}) collective-permute-start(bf16[1024,512]{1,0:T(8,128)(2,1)S(1)} %copy-done), channel_id=1, source_target_pairs={{0,1},{1,0},{2,3},{3,2},{4,5},{5,4},{6,7},{7,6},{8,9},{9,8},{10,11... | collective-permute-start | bytes 3145736 | tf_op jit(solution)/shard_map/ppermute | solution.py:637
  127.1 26.5 %collective-permute-start.7 = (bf16[512,1024]{1,0:T(8,128)(2,1)S(1)}, bf16[512,1024]{1,0:T(8,128)(2,1)}, u32[]{:S(2)}, u32[]{:S(2)}) collective-permute-start(bf16[512,1024]{1,0:T(8,128)(2,1)S(1)} %pad_maximum_fusion.6.refs_4_), channel_id=1, source_target_pairs={{0,1},{1,0},{2,3},{3,2},{4,5},{5,4},{6,7},{7,6},{8,9},{9,8},{10,11... | collective-permute-start | bytes 3145736 | tf_op jit(solution)/shard_map/ppermute | solution.py:637
  127.6 26.0 %collective-permute-start.6 = (bf16[1024,512]{1,0:T(8,128)(2,1)S(1)}, bf16[1024,512]{1,0:T(8,128)(2,1)}, u32[]{:S(2)}, u32[]{:S(2)}) collective-permute-start(bf16[1024,512]{1,0:T(8,128)(2,1)S(1)} %collective-permute-done.5.refs_2_), channel_id=1, source_target_pairs={{0,1},{1,0},{2,3},{3,2},{4,5},{5,4},{6,7},{7,6},{8,9},{9,8},{10,11... | collective-permute-start | bytes 3145736 | tf_op jit(solution)/shard_map/ppermute | solution.py:637
  198.1 122.5 %all-gather.15.cloned.1.call-start = ((), (), s32[]{:S(2)}) async-start(), calls=%async_computation.9 | async-start | bytes 2621440 | tf_op jit(solution)/shard_map/all_gather | solution.py:756
  198.2 23.6 %collective-permute-start.18 = (bf16[256,1024]{1,0:T(8,128)(2,1)S(1)}, bf16[256,1024]{1,0:T(8,128)(2,1)}, u32[]{:S(2)}, u32[]{:S(2)}) collective-permute-start(bf16[256,1024]{1,0:T(8,128)(2,1)S(1)} %copy-done.19), channel_id=1, source_target_pairs={{0,2},{1,3},{2,0},{3,1},{4,6},{5,7},{6,4},{7,5},{8,10},{9,11},{10,... | collective-permute-start | bytes 1572872 | tf_op jit(solution)/shard_map/ppermute | solution.py:637
  198.8 22.9 %collective-permute-start.11 = (bf16[256,1024]{1,0:T(8,128)(2,1)}, bf16[256,1024]{1,0:T(8,128)(2,1)S(1)}, u32[]{:S(2)}, u32[]{:S(2)}) collective-permute-start(bf16[256,1024]{1,0:T(8,128)(2,1)} %bitcast.215), channel_id=1, source_target_pairs={{0,1},{1,0},{2,3},{3,2},{4,5},{5,4},{6,7},{7,6},{8,9},{9,8},{10,11... | collective-permute-start | bytes 1572872 | tf_op jit(solution)/shard_map/ppermute | solution.py:637
  211.7 16.3 %collective-permute-start.3 = (bf16[512,512]{1,0:T(8,128)(2,1)S(1)}, bf16[512,512]{1,0:T(8,128)(2,1)S(1)}, u32[]{:S(2)}, u32[]{:S(2)}) collective-permute-start(bf16[512,512]{1,0:T(8,128)(2,1)S(1)} %slice.160), channel_id=1, source_target_pairs={{0,4},{1,5},{2,6},{3,7},{8,12},{9,13},{10,14},{11,15},{16,20},{17,... | collective-permute-start | bytes 1572872 | tf_op jit(solution)/shard_map/ppermute | solution.py:633
  219.7 30.2 %collective-permute-start.17 = (bf16[256,1024]{1,0:T(8,128)(2,1)S(1)}, bf16[256,1024]{1,0:T(8,128)(2,1)}, u32[]{:S(2)}, u32[]{:S(2)}) collective-permute-start(bf16[256,1024]{1,0:T(8,128)(2,1)S(1)} %copy-done.19), channel_id=1, source_target_pairs={{0,1},{1,0},{2,3},{3,2},{4,5},{5,4},{6,7},{7,6},{8,9},{9,8},{10,11... | collective-permute-start | bytes 1572872 | tf_op jit(solution)/shard_map/ppermute | solution.py:637
  221.7 28.2 %collective-permute-start.19 = (bf16[256,1024]{1,0:T(8,128)(2,1)}, bf16[256,1024]{1,0:T(8,128)(2,1)}, u32[]{:S(2)}, u32[]{:S(2)}) collective-permute-start(bf16[256,1024]{1,0:T(8,128)(2,1)} %collective-permute-done.18), channel_id=1, source_target_pairs={{0,1},{1,0},{2,3},{3,2},{4,5},{5,4},{6,7},{7,6},{8,9},{9,8},{10,11... | collective-permute-start | bytes 1572872 | tf_op jit(solution)/shard_map/ppermute | solution.py:637
  260.4 24.3 %collective-permute-start.26 = (bf16[256,1024]{1,0:T(8,128)(2,1)S(1)}, bf16[256,1024]{1,0:T(8,128)(2,1)S(1)}, u32[]{:S(2)}, u32[]{:S(2)}) collective-permute-start(bf16[256,1024]{1,0:T(8,128)(2,1)S(1)} %bitcast.220), channel_id=1, source_target_pairs={{0,2},{1,3},{2,0},{3,1},{4,6},{5,7},{6,4},{7,5},{8,10},{9,11},{10,... | collective-permute-start | bytes 1572872 | tf_op jit(solution)/shard_map/ppermute | solution.py:637
  261.0 23.7 %collective-permute-start.20 = (bf16[256,1024]{1,0:T(8,128)(2,1)S(1)}, bf16[256,1024]{1,0:T(8,128)(2,1)}, u32[]{:S(2)}, u32[]{:S(2)}) collective-permute-start(bf16[256,1024]{1,0:T(8,128)(2,1)S(1)} %multiply_convert_fusion.1), channel_id=1, source_target_pairs={{0,1},{1,0},{2,3},{3,2},{4,5},{5,4},{6,7},{7,6},{8,9},{9,8},{10,11... | collective-permute-start | bytes 1572872 | tf_op jit(solution)/shard_map/ppermute | solution.py:637
  273.9 285.1 %reduce-scatter.12.cloned.1.call-start = ((), (), s32[]{:S(2)}) async-start(), calls=%async_computation.13 | async-start | bytes 2621440 | tf_op jit(solution)/shard_map/reduce_scatter | solution.py:846
  274.0 26.8 %collective-permute-start.25 = (bf16[256,1024]{1,0:T(8,128)(2,1)S(1)}, bf16[256,1024]{1,0:T(8,128)(2,1)}, u32[]{:S(2)}, u32[]{:S(2)}) collective-permute-start(bf16[256,1024]{1,0:T(8,128)(2,1)S(1)} %bitcast.221), channel_id=1, source_target_pairs={{0,1},{1,0},{2,3},{3,2},{4,5},{5,4},{6,7},{7,6},{8,9},{9,8},{10,11... | collective-permute-start | bytes 1572872 | tf_op jit(solution)/shard_map/ppermute | solution.py:637
  284.7 16.0 %collective-permute-start.27 = (bf16[256,1024]{1,0:T(8,128)(2,1)S(1)}, bf16[256,1024]{1,0:T(8,128)(2,1)}, u32[]{:S(2)}, u32[]{:S(2)}) collective-permute-start(bf16[256,1024]{1,0:T(8,128)(2,1)S(1)} %collective-permute-done.26), channel_id=1, source_target_pairs={{0,1},{1,0},{2,3},{3,2},{4,5},{5,4},{6,7},{7,6},{8,9},{9,8},{10,11... | collective-permute-start | bytes 1572872 | tf_op jit(solution)/shard_map/ppermute | solution.py:637
  340.6 220.4 %reduce-scatter.14.cloned.1.call-start = ((), (), s32[]{:S(2)}) async-start(), calls=%async_computation.14 | async-start | bytes 2621440 | tf_op jit(solution)/shard_map/reduce_scatter | solution.py:846
  346.8 21.5 %collective-permute-start.24 = (bf16[256,1024]{1,0:T(8,128)(2,1)S(1)}, bf16[256,1024]{1,0:T(8,128)(2,1)S(1)}, u32[]{:S(2)}, u32[]{:S(2)}) collective-permute-start(bf16[256,1024]{1,0:T(8,128)(2,1)S(1)} %fusion.50), channel_id=1, source_target_pairs={{0,2},{1,3},{2,0},{3,1},{4,6},{5,7},{6,4},{7,5},{8,10},{9,11},{10,... | collective-permute-start | bytes 1572872 | tf_op jit(solution)/shard_map/ppermute | solution.py:637
  427.0 172.6 %reduce-scatter.10.cloned.1.call-start = ((), (), s32[]{:S(2)}) async-start(), calls=%async_computation.12 | async-start | bytes 1638400 | tf_op jit(solution)/shard_map/reduce_scatter | solution.py:846
  465.4 28.1 %collective-permute-start.45 = (bf16[256,1024]{1,0:T(8,128)(2,1)S(1)}, bf16[256,1024]{1,0:T(8,128)(2,1)}, u32[]{:S(2)}, u32[]{:S(2)}) collective-permute-start(bf16[256,1024]{1,0:T(8,128)(2,1)S(1)} %copy-done.16), channel_id=1, source_target_pairs={{0,2},{1,3},{2,0},{3,1},{4,6},{5,7},{6,4},{7,5},{8,10},{9,11},{10,... | collective-permute-start | bytes 1572872 | tf_op jit(solution)/shard_map/ppermute | solution.py:637
  504.7 16.4 %collective-permute-start.39 = (bf16[512,512]{1,0:T(8,128)(2,1)S(1)}, bf16[512,512]{1,0:T(8,128)(2,1)S(1)}, u32[]{:S(2)}, u32[]{:S(2)}) collective-permute-start(bf16[512,512]{1,0:T(8,128)(2,1)S(1)} %pad_maximum_fusion.7), channel_id=1, source_target_pairs={{4,0},{5,1},{6,2},{7,3},{12,8},{13,9},{14,10},{15,11},{20,16},{21,... | collective-permute-start | bytes 1572872 | tf_op jit(solution)/shard_map/ppermute | solution.py:633
  534.4 67.2 %reduce-scatter.8.cloned.1.call-start = ((), (), s32[]{:S(2)}) async-start(), calls=%async_computation.11 | async-start | bytes 1966080 | tf_op jit(solution)/shard_map/reduce_scatter | solution.py:846
  539.1 98.3 %reduce-scatter.6.cloned.1.call-start = ((), (), s32[]{:S(2)}) async-start(), calls=%async_computation.10 | async-start | bytes 1966080 | tf_op jit(solution)/shard_map/reduce_scatter | solution.py:846
  559.0 16.6 %collective-permute-start.48 = (bf16[256,1024]{1,0:T(8,128)(2,1)}, bf16[256,1024]{1,0:T(8,128)(2,1)}, u32[]{:S(2)}, u32[]{:S(2)}) collective-permute-start(bf16[256,1024]{1,0:T(8,128)(2,1)} %reduce-scatter.12.cloned.1.call-done), channel_id=1, source_target_pairs={{0,4},{4,0},{1,5},{5,1},{2,6},{6,2},{3,7},{7,3},{8,12},{12,8},{9,1... | collective-permute-start | bytes 1572872 | tf_op jit(solution)/shard_map/ppermute | solution.py:637
  561.0 23.9 %collective-permute-start.49 = (bf16[1024,256]{1,0:T(8,128)(2,1)}, bf16[1024,256]{1,0:T(8,128)(2,1)}, u32[]{:S(2)}, u32[]{:S(2)}) collective-permute-start(bf16[1024,256]{1,0:T(8,128)(2,1)} %reduce-scatter.14.cloned.1.call-done), channel_id=1, source_target_pairs={{0,4},{4,0},{1,5},{5,1},{2,6},{6,2},{3,7},{7,3},{8,12},{12,8},{9,1... | collective-permute-start | bytes 1572872 | tf_op jit(solution)/shard_map/ppermute | solution.py:637
  601.6 38.1 %collective-permute-start.43 = (bf16[2,256,384]{1,2,0:T(8,128)(2,1)}, bf16[2,256,384]{1,2,0:T(8,128)(2,1)S(1)}, u32[]{:S(2)}, u32[]{:S(2)}) collective-permute-start(bf16[2,256,384]{1,2,0:T(8,128)(2,1)} %reduce-scatter.8.cloned.1.call-done), channel_id=1, source_target_pairs={{0,4},{4,0},{1,5},{5,1},{2,6},{6,2},{3,7},{7,3},{8,12},{12,8},{9,1... | collective-permute-start | bytes 1179656 | tf_op jit(solution)/shard_map/ppermute | solution.py:637
  (82 other events, 996.4 us)
Sparse Core Ops, SparseCore 0:
  10.1 36.2 all-gather.10
  48.6 35.9 all-gather.6
  86.1 35.9 all-gather.8
  198.2 45.1 all-gather.12
  274.0 46.5 all-gather.14
  340.7 42.0 reduce-scatter.11
  427.2 42.0 reduce-scatter.13
  534.5 28.5 reduce-scatter.9
  565.4 35.4 reduce-scatter.7
  603.1 34.2 reduce-scatter.5

commit v2 on v1

v2 whole, which is shorter than its diff:
```python
import functools

import jax
import jax.numpy as jnp
from jax import lax
from jax.experimental import pallas as pl
from jax.experimental.pallas import tpu as pltpu
from jax.sharding import PartitionSpec as P

HS = 128
BLK = 512
NBUCKET = 32
EDGES = (12, 16, 23, 32, 46, 64, 91)
LOW = jnp.bfloat16
F32 = jnp.float32
SCALE = HS ** (-0.5)
EPS = 1e-06
DIAG = 3 * BLK
SMALL = 16
PACE = 0.5


def mm(a, b, ca, cb):
    return lax.dot_general(a, b, (((ca,), (cb,)), ((), ())), preferred_element_type=F32)


def whole():
    return pl.BlockSpec(memory_space=pltpu.VMEM)


def scalars():
    return pl.BlockSpec(memory_space=pltpu.SMEM)


def params(grid_rank=0, mib=40):
    limit = mib * 1024 * 1024
    if grid_rank:
        return pltpu.CompilerParams(
            dimension_semantics=("arbitrary",) * grid_rank, vmem_limit_bytes=limit
        )
    return pltpu.CompilerParams(vmem_limit_bytes=limit)


def lasts(microseconds):
    return pl.CostEstimate(
        flops=int(microseconds * PACE * 1.1e9), bytes_accessed=int(microseconds * PACE * 3e6), transcendentals=0
    )


def rms_scale(v):
    return lax.rsqrt(jnp.mean(v * v, axis=-1, keepdims=True) + EPS)


def assemble_kernel(count, pos_ref, *refs):
    pieces, other_ref, outs = refs[:count], refs[count], refs[count + 1 :]
    part = pieces[0].shape[0]
    for s in range(count):
        base = (pos_ref[0] ^ s) * (2 * part)
        mine = pl.multiple_of(base + pos_ref[1] * part, part)
        theirs = pl.multiple_of(base + (1 - pos_ref[1]) * part, part)
        first = 0
        for out_ref in outs:
            last = first + out_ref.shape[1]
            out_ref[pl.ds(mine, part), :] = pieces[s][:, first:last]
            out_ref[pl.ds(theirs, part), :] = other_ref[s, :, first:last]
            first = last


def assemble(pos, pieces, other, widths):
    part, cols = pieces[0].shape
    rows = 2 * part * len(pieces)
    return pl.pallas_call(
        functools.partial(assemble_kernel, len(pieces)),
        out_shape=tuple(jax.ShapeDtypeStruct((rows, w), LOW) for w in widths),
        in_specs=[scalars()] + [whole()] * (len(pieces) + 1),
        out_specs=(whole(),) * len(widths),
        compiler_params=params(mib=16),
        cost_estimate=lasts(1.5),
        name="assemble",
    )(pos, *pieces, other)


def weight_grad_kernel(counts, *refs):
    out_ref = refs[-1]
    at = 0
    first = 0
    for count in counts:
        right = refs[at + count]
        total = None
        row = 0
        for left in refs[at : at + count]:
            term = mm(left[...], right[row : row + left.shape[0], :], 0, 0)
            row += left.shape[0]
            total = term if total is None else total + term
        out_ref[:, first : first + right.shape[1]] = total.astype(LOW)
        first += right.shape[1]
        at += count + 1


def weight_grad(pairs):
    width = pairs[0][0][0].shape[1]
    tile = 256
    specs, args, flops = [], [], 0
    for lefts, right in pairs:
        specs += [pl.BlockSpec((left.shape[0], tile), lambda i: (0, i)) for left in lefts]
        specs.append(pl.BlockSpec(right.shape, lambda i: (0, 0)))
        args += list(lefts) + [right]
        flops += 2 * right.size * width
    cols = sum(right.shape[1] for _, right in pairs)
    return pl.pallas_call(
        functools.partial(weight_grad_kernel, [len(lefts) for lefts, _ in pairs]),
        grid=(width // tile,),
        out_shape=jax.ShapeDtypeStruct((width, cols), LOW),
        in_specs=specs,
        out_specs=pl.BlockSpec((tile, cols), lambda i: (i, 0)),
        compiler_params=params(1, 32),
        cost_estimate=lasts(6),
        name="weight_grad",
    )(*args)


def token_proj_kernel(count, shards, blocks, me_ref, pos_ref, *refs):
    pieces, parts = refs[:count], refs[count : count + shards]
    q_ref, normed_ref, vec_ref, wq_ref, wkv_ref, scratch, *kv_refs, w_ref = refs[count + shards :]
    heads = w_ref.shape[1] // 384
    span = heads * HS
    rows = pieces[0].shape[0] - SMALL
    for s in range(shards):
        part = parts[s].shape[0]
        at = pl.ds(pl.multiple_of((pos_ref[0] ^ s) * part, part), part)
        w_ref[at, :] = parts[s][...]
    vectors = pieces[0][rows:, :].astype(F32)
    for m in range(1, count):
        vectors = vectors + pieces[m][rows:, :].astype(F32)
    vec_ref[...] = vectors
    gain = vectors[0:1]
    for m in range(count):
        start = pl.multiple_of((me_ref[0] ^ m) * rows, rows)
        v = pieces[m][:rows, :].astype(F32)
        normed = (v * rms_scale(v) * gain).astype(LOW)
        normed_ref[pl.ds(start, rows), :] = normed
        for h in range(heads):
            out = mm(normed, w_ref[:, h * 384 : (h + 1) * 384], 1, 0).astype(LOW)
            q_ref[pl.ds(start, rows), h * HS : (h + 1) * HS] = out[:, :HS]
            scratch[pl.ds(start, rows), h * HS : (h + 1) * HS] = out[:, HS : 2 * HS]
            scratch[pl.ds(start, rows), span + h * HS : span + (h + 1) * HS] = out[:, 2 * HS :]
    for b in range(blocks):
        kv_refs[b][...] = scratch[b * BLK : (b + 1) * BLK, :]
    for h in range(heads):
        wq_ref[:, h * HS : (h + 1) * HS] = w_ref[:, h * 384 : h * 384 + HS]
        wkv_ref[:, 2 * h * HS : 2 * (h + 1) * HS] = w_ref[:, h * 384 + HS : (h + 1) * 384]


def token_proj(me, pos, pieces, parts, blocks):
    width = pieces[0].shape[1]
    cols = parts[0].shape[1]
    span = cols // 3
    rows = (pieces[0].shape[0] - SMALL) * len(pieces)
    return pl.pallas_call(
        functools.partial(token_proj_kernel, len(pieces), len(parts), blocks),
        out_shape=(
            jax.ShapeDtypeStruct((rows, span), LOW),
            jax.ShapeDtypeStruct((rows, width), LOW),
            jax.ShapeDtypeStruct((SMALL, width), F32),
            jax.ShapeDtypeStruct((width, span), LOW),
            jax.ShapeDtypeStruct((width, 2 * span), LOW),
            jax.ShapeDtypeStruct((rows, 2 * span), LOW),
        )
        + (jax.ShapeDtypeStruct((BLK, 2 * span), LOW),) * blocks,
        in_specs=[scalars(), scalars()] + [whole()] * (len(pieces) + len(parts)),
        out_specs=(whole(),) * (6 + blocks),
        scratch_shapes=[pltpu.VMEM((width, cols), LOW)],
        compiler_params=params(mib=24),
        cost_estimate=lasts(5),
        name="token_proj",
    )(me, pos, *pieces, *parts)


def proj_kernel(count, weights, *refs):
    pieces, ws, outs = refs[:count], refs[count : count + weights], refs[count + weights :]
    rows = pieces[0].shape[0]
    for m in range(count):
        for w, out in zip(ws, outs, strict=True):
            out[m * rows : (m + 1) * rows, :] = mm(pieces[m][...], w[...], 1, 0).astype(LOW)


def proj(pieces, weights):
    rows, width = pieces[0].shape[0] * len(pieces), pieces[0].shape[1]
    cols = sum(w.shape[1] for w in weights)
    return pl.pallas_call(
        functools.partial(proj_kernel, len(pieces), len(weights)),
        out_shape=tuple(jax.ShapeDtypeStruct((rows, w.shape[1]), LOW) for w in weights),
        in_specs=[whole()] * (len(pieces) + len(weights)),
        out_specs=(whole(),) * len(weights),
        compiler_params=params(mib=24),
        cost_estimate=lasts(3),
        name="proj",
    )(*pieces, *weights)


def back_kernel(count, gained, me_ref, *refs):
    even_ref, odd_ref = refs[2 * count + gained : 2 * count + gained + 2]
    total = None
    for i in range(count):
        term = mm(refs[i][...], refs[count + i][...], 1, 1)
        total = term if total is None else total + term
    if gained:
        sums = jnp.sum(total * refs[2 * count][...].astype(F32), axis=0, keepdims=True)
        first = pl.program_id(0) == 0
        refs[-1][...] = sums + jnp.where(first, 0.0, refs[-1][...])
    total = total.astype(LOW)
    even = lax.rem(pl.program_id(0), 2) == 0

    @pl.when(even)
    def _():
        even_ref[...] = total

    @pl.when(jnp.logical_not(even))
    def _():
        odd_ref[...] = total


def back(me, grads, weights, normed=None):
    rows, width = grads[0].shape[0], weights[0].shape[0]
    size = lax.axis_size("tensor")
    tile = rows // size
    inner = sum(w.shape[1] for w in weights)
    half = jax.ShapeDtypeStruct((size // 2, tile, width), LOW)
    extra = [] if normed is None else [normed]
    grid_spec = pltpu.PrefetchScalarGridSpec(
        num_scalar_prefetch=1,
        grid=(size,),
        in_specs=[pl.BlockSpec((tile, g.shape[1]), lambda i, me_ref: (i ^ me_ref[0], 0)) for g in grads]
        + [pl.BlockSpec(w.shape, lambda i, me_ref: (0, 0)) for w in weights]
        + [pl.BlockSpec((tile, width), lambda i, me_ref: (i ^ me_ref[0], 0)) for _ in extra],
        out_specs=(
            pl.BlockSpec((None, tile, width), lambda i, me_ref: (i // 2, 0, 0)),
            pl.BlockSpec((None, tile, width), lambda i, me_ref: (i // 2, 0, 0)),
        )
        + (pl.BlockSpec((1, width), lambda i, me_ref: (0, 0)),) * len(extra),
    )
    return pl.pallas_call(
        functools.partial(back_kernel, len(grads), len(extra)),
        grid_spec=grid_spec,
        out_shape=(half, half) + (jax.ShapeDtypeStruct((1, width), F32),) * len(extra),
        compiler_params=params(1, 24),
        cost_estimate=lasts(3),
        name="back",
    )(me, *grads, *weights, *extra)


def branch_kernel(count, own_ref, gain_ref, *refs):
    parts, weights = refs[:count], refs[count : 2 * count]
    residual_ref, normed_ref, sums_ref = refs[2 * count :]
    branch = None
    for part, weight in zip(parts, weights, strict=True):
        term = mm(part[...], weight[...], 1, 1)
        branch = term if branch is None else branch + term
    own = own_ref[...].astype(F32)
    residual = own + branch
    residual_ref[...] = residual
    normed_ref[...] = (residual * rms_scale(residual) * gain_ref[...]).astype(LOW)
    sums_ref[0:1, :] = jnp.sum(own * own, axis=0, keepdims=True)
    sums_ref[1:2, :] = jnp.sum(branch * branch, axis=0, keepdims=True)


def branch_out(own, gain, parts, weights):
    rows, width = own.shape
    return pl.pallas_call(
        functools.partial(branch_kernel, len(parts)),
        out_shape=(
            jax.ShapeDtypeStruct((rows, width), F32),
            jax.ShapeDtypeStruct((rows, width), LOW),
            jax.ShapeDtypeStruct((2, width), F32),
        ),
        in_specs=[whole()] * (2 + 2 * len(parts)),
        out_specs=(whole(),) * 3,
        compiler_params=params(mib=12),
        cost_estimate=lasts(3),
        name="branch_out",
    )(own, gain, *parts, *weights)


def branch_back_kernel(count, sums, cot_ref, residual_ref, gain_ref, *refs):
    terms, weights, outs = refs[:sums], refs[sums : sums + count], refs[sums + count :]
    grad_ref, low_ref, gain_sum_ref, parts = outs[0], outs[1], outs[2], outs[3:]
    grad = terms[0][...].astype(F32)
    for term in terms[1:]:
        grad = grad + term[...].astype(F32)
    residual = residual_ref[...]
    r = rms_scale(residual)
    unit = residual * r
    gain_sum_ref[...] = jnp.sum(grad * unit, axis=0, keepdims=True)
    scaled = grad * gain_ref[...]
    grad = cot_ref[...].astype(F32) + r * (
        scaled - unit * jnp.mean(scaled * unit, axis=-1, keepdims=True)
    )
    grad_ref[...] = grad
    low = grad.astype(LOW)
    low_ref[...] = low
    for part, weight in zip(parts, weights, strict=True):
        part[...] = mm(low, weight[...], 1, 0).astype(LOW)


def branch_back(cot, residual, gain, terms, weights):
    rows, width = cot.shape
    span = weights[0].shape[1]
    return pl.pallas_call(
        functools.partial(branch_back_kernel, len(weights), len(terms)),
        out_shape=(
            jax.ShapeDtypeStruct((rows, width), F32),
            jax.ShapeDtypeStruct((rows, width), LOW),
            jax.ShapeDtypeStruct((1, width), F32),
        )
        + (jax.ShapeDtypeStruct((rows, span), LOW),) * len(weights),
        in_specs=[whole()] * (3 + len(terms) + len(weights)),
        out_specs=(whole(),) * (3 + len(weights)),
        compiler_params=params(mib=56),
        cost_estimate=lasts(2.5),
        name="branch_back",
    )(cot, residual, gain, *terms, *weights)


def gelu_parts(pre):
    half = 0.5 * (1.0 + lax.erf(pre * 0.7071067811865476))
    density = jnp.exp(pre * pre * -0.5) * 0.3989422804014327
    return half, density


def feed_kernel(count, w_ref, ghid_ref, *refs):
    pieces = refs[:count]
    hidden_ref, gpre_ref, even_ref, odd_ref = refs[count:]
    rows = pieces[0].shape[0]
    for m in range(count):
        at = slice(m * rows, (m + 1) * rows)
        pre = mm(pieces[m][...], w_ref[...], 1, 0)
        half, density = gelu_parts(pre)
        hidden_ref[at, :] = (pre * half).astype(LOW)
        gpre = ((half + pre * density) * ghid_ref[at, :].astype(F32)).astype(LOW)
        gpre_ref[at, :] = gpre
        (even_ref, odd_ref)[m % 2][m // 2] = mm(gpre, w_ref[...], 1, 1).astype(LOW)


def feed(w_in, ghid, pieces):
    width, units = w_in.shape
    own = pieces[0].shape[0]
    rows = own * len(pieces)
    half = jax.ShapeDtypeStruct((len(pieces) // 2, own, width), LOW)
    return pl.pallas_call(
        functools.partial(feed_kernel, len(pieces)),
        out_shape=(
            jax.ShapeDtypeStruct((rows, units), LOW),
            jax.ShapeDtypeStruct((rows, units), LOW),
            half,
            half,
        ),
        in_specs=[whole()] * (2 + len(pieces)),
        out_specs=(whole(),) * 4,
        compiler_params=params(mib=32),
        cost_estimate=lasts(7),
        name="feed",
    )(w_in, ghid, *pieces)


def column_softmax(scores):
    peak = jnp.max(scores, axis=0, keepdims=True)
    exponent = jnp.exp(scores - peak)
    return exponent * (1.0 / jnp.sum(exponent, axis=0, keepdims=True))


def chain_forward_kernel(count, heads, state_ref, gain_ref, dec_ref, *refs):
    kv = refs[:count]
    w = refs[count : 2 * count]
    normed_ref, update_ref, next_ref = refs[2 * count :]
    span = heads * HS
    dec = dec_ref[...]
    state = state_ref[...]
    normed = (state * rms_scale(state) * gain_ref[...]).astype(LOW)
    normed_ref[...] = normed
    update = None
    for m in range(count):
        q = mm(normed, w[m][:, :span], 1, 0).astype(LOW)
        mixed = []
        for h in range(heads):
            k = kv[m][:, h * HS : (h + 1) * HS]
            v = kv[m][:, (heads + h) * HS : (heads + h + 1) * HS]
            weights = column_softmax(mm(k, q[:, h * HS : (h + 1) * HS], 1, 1) * SCALE)
            mixed.append(mm(v, weights.astype(LOW), 0, 0))
        mixed = mixed[0] if heads == 1 else jnp.concatenate(mixed, axis=0)
        term = mm(mixed.T.astype(LOW), w[m][:, span:], 1, 1)
        update = term if update is None else update + term
    update_ref[...] = update
    next_ref[...] = dec * state + (1.0 - dec) * update


def chain_forward(state, gain, dec, kv, weights):
    count = len(kv)
    rows, width = state.shape
    heads = kv[0].shape[1] // (2 * HS)
    flops = 4 * rows * width * count * heads * HS + 4 * rows * BLK * count * heads * HS
    return pl.pallas_call(
        functools.partial(chain_forward_kernel, count, heads),
        out_shape=(
            jax.ShapeDtypeStruct((rows, width), LOW),
            jax.ShapeDtypeStruct((rows, width), F32),
            jax.ShapeDtypeStruct((rows, width), F32),
        ),
        in_specs=[whole()] * (3 + 2 * count),
        out_specs=(whole(),) * 3,
        compiler_params=params(mib=56),
        cost_estimate=lasts(6.5),
        name="chain_forward",
    )(state, gain, dec, *kv, *weights)


def chain_backward_kernel(
    count, heads, carry_ref, gain_ref, dec_ref, state_ref, normed_ref, update_ref, gkv_ref, *refs
):
    kv = refs[:count]
    w = refs[count : 2 * count]
    next_ref, gup_next_ref, small_ref = refs[2 * count :]
    span = heads * HS
    dec = dec_ref[...]
    gain = gain_ref[...]
    carry = carry_ref[...]
    state = state_ref[...]
    small_ref[1:2, :] = jnp.sum(carry * (state - update_ref[...]), axis=0, keepdims=True)
    gup = ((1.0 - dec) * carry).astype(LOW)
    normed = normed_ref[...]
    grad_normed = gkv_ref[...]
    for m in range(count):
        q = mm(normed, w[m][:, :span], 1, 0).astype(LOW)
        gmix = mm(gup, w[m][:, span:], 1, 0).astype(LOW)
        grad_q = []
        for h in range(heads):
            at = slice(h * HS, (h + 1) * HS)
            k = kv[m][:, at]
            v = kv[m][:, (heads + h) * HS : (heads + h + 1) * HS]
            weights = column_softmax(mm(k, q[:, at], 1, 1) * SCALE)
            grad_w = mm(v, gmix[:, at], 1, 1)
            inner = jnp.sum(grad_w * weights, axis=0, keepdims=True)
            grad_s = (weights * (grad_w - inner)).astype(LOW)
            grad_q.append(mm(k, grad_s, 0, 0) * SCALE)
        grad_q = grad_q[0] if heads == 1 else jnp.concatenate(grad_q, axis=0)
        grad_normed = grad_normed + mm(grad_q.T.astype(LOW), w[m][:, :span], 1, 1)
    r = rms_scale(state)
    unit = state * r
    scaled = grad_normed * gain
    small_ref[0:1, :] = jnp.sum(grad_normed * unit, axis=0, keepdims=True)
    carry = dec * carry + r * (scaled - unit * jnp.mean(scaled * unit, axis=-1, keepdims=True))
    next_ref[...] = carry
    gup_next_ref[...] = ((1.0 - dec) * carry).astype(LOW)


def chain_backward(carry, gain, dec, state, normed, update, gkv, kv, weights):
    count = len(kv)
    rows, width = state.shape
    heads = kv[0].shape[1] // (2 * HS)
    flops = 6 * rows * width * count * heads * HS + 6 * rows * BLK * count * heads * HS
    return pl.pallas_call(
        functools.partial(chain_backward_kernel, count, heads),
        out_shape=(
            jax.ShapeDtypeStruct((rows, width), F32),
            jax.ShapeDtypeStruct((rows, width), LOW),
            jax.ShapeDtypeStruct((2, width), F32),
        ),
        in_specs=[whole()] * (7 + 2 * count),
        out_specs=(whole(),) * 3,
        compiler_params=params(mib=56),
        cost_estimate=lasts(8.3),
        name="chain_backward",
    )(carry, gain, dec, state, normed, update, gkv, *kv, *weights)


def bucket_tile():
    lane = lax.broadcasted_iota(jnp.int32, (8, DIAG), 1)
    row = lax.broadcasted_iota(jnp.int32, (8, DIAG), 0)
    diff = lane - row
    diff = jnp.where(diff < 0, diff + DIAG, diff)
    offset = jnp.where(diff < BLK, diff, diff - DIAG) + BLK
    distance = jnp.abs(offset)
    far = jnp.full((8, DIAG), 8, jnp.int32)
    for edge in EDGES:
        far = far + (distance >= edge).astype(jnp.int32)
    near = jnp.where(distance < 8, distance, far)
    return jnp.where(offset >= 0, near, near + NBUCKET // 2)


def fill_bias(table_ref, h, bias_ref):
    bucket = bucket_tile()
    base = jnp.zeros((8, DIAG), F32)
    for k in range(NBUCKET):
        base = jnp.where(bucket == k, table_ref[h, k], base)
    for r in range(16):
        rolled = pltpu.roll(base, 8 * r, 1) if r else base
        wide = jnp.concatenate([rolled, rolled[:, :BLK]], axis=1)
        for k in range(2 * BLK // 128):
            start = (DIAG - 128 * k) % DIAG
            row = 8 * (16 * k + r)
            bias_ref[row : row + 8, :] = wide[:, start : start + BLK]


def collapse_bias(grad_ref, out_ref):
    total = jnp.zeros((8, DIAG), F32)
    for r in range(16):
        acc = [jnp.zeros((8, 128), F32)] * (DIAG // 128)
        for k in range(2 * BLK // 128):
            row = 8 * (16 * k + r)
            for c in range(BLK // 128):
                at = (c - k) % (DIAG // 128)
                acc[at] = acc[at] + grad_ref[row : row + 8, c * 128 : (c + 1) * 128]
        acc = jnp.concatenate(acc, axis=1)
        total = total + (pltpu.roll(acc, DIAG - 8 * r, 1) if r else acc)
    bucket = bucket_tile()
    lane = lax.broadcasted_iota(jnp.int32, (8, HS), 1)
    out = jnp.zeros((8, HS), F32)
    for k in range(NBUCKET):
        out = jnp.where(lane == k, jnp.sum(jnp.where(bucket == k, total, 0.0)), out)
    out_ref[...] = out


def current_mask(ids_col_ref, ids_row_ref):
    key = lax.broadcasted_iota(jnp.int32, (BLK, BLK), 0)
    query = lax.broadcasted_iota(jnp.int32, (BLK, BLK), 1)
    ids_row = ids_row_ref[...]
    return (key <= query) | ((ids_col_ref[...] == ids_row) & (ids_row > 0))


def attend_kernel(
    run_ref, table_ref, q_ref, kc_ref, vc_ref, kp_ref, vp_ref, ko_ref, vo_ref, ks_ref, vs_ref,
    row_ref, col_ref, out_ref, lse_ref, bias_ref, score_ref,
):
    h = pl.program_id(0)
    b = pl.program_id(1)

    @pl.when(b == 0)
    def _():
        fill_bias(table_ref, h, bias_ref)

    q = q_ref[...]
    first = b == 0
    keys = (
        ks_ref[...].reshape(BLK, HS),
        jnp.where(first, ko_ref[...], kp_ref[...]),
        kc_ref[...],
    )
    values = (
        vs_ref[...].reshape(BLK, HS),
        jnp.where(first, vo_ref[...], vp_ref[...]),
        vc_ref[...],
    )
    prior_ok = (run_ref[0] > 0) | (b > 0)
    score = mm(keys[0], q, 1, 1) * SCALE
    score_ref[0] = score
    peak = jnp.max(score, axis=0, keepdims=True)
    score = mm(keys[1], q, 1, 1) * SCALE + bias_ref[:BLK]
    score = jnp.where(prior_ok, score, -1e30)
    score_ref[1] = score
    peak = jnp.maximum(peak, jnp.max(score, axis=0, keepdims=True))
    score = mm(keys[2], q, 1, 1) * SCALE + bias_ref[BLK:]
    score = jnp.where(current_mask(col_ref, row_ref), score, -1e30)
    score_ref[2] = score
    peak = jnp.maximum(peak, jnp.max(score, axis=0, keepdims=True))
    total = jnp.zeros((1, BLK), F32)
    for c in range(3):
        exponent = jnp.exp(score_ref[c] - peak)
        score_ref[c] = exponent
        total = total + jnp.sum(exponent, axis=0, keepdims=True)
    inverse = 1.0 / total
    mixed = jnp.zeros((HS, BLK), F32)
    for c in range(3):
        mixed = mixed + mm(values[c], (score_ref[c] * inverse).astype(LOW), 0, 0)
    out_ref[...] = mixed.T.astype(LOW)
    lse_ref[...] = peak + jnp.log(total)


def attend_specs(heads, pieces, part, blocks):
    def at(col):
        return pl.BlockSpec((BLK, HS), lambda h, b: (b, col(h)))

    def before(col):
        return pl.BlockSpec((BLK, HS), lambda h, b: (jnp.maximum(b - 1, 0), col(h)))

    def outer(col):
        return pl.BlockSpec((BLK, HS), lambda h, b: (0, col(h)))

    def state(col):
        return pl.BlockSpec((pieces, None, part, HS), lambda h, b: (0, b, 0, col(h)))

    key, value = (lambda h: h), (lambda h: heads + h)
    return [
        scalars(),
        scalars(),
        at(key),
        at(key),
        at(value),
        before(key),
        before(value),
        outer(key),
        outer(value),
        state(lambda h: 2 * h),
        state(lambda h: 2 * h + 1),
        pl.BlockSpec((None, 1, BLK), lambda h, b: (b, 0, 0)),
        pl.BlockSpec((None, BLK, 1), lambda h, b: (b, 0, 0)),
    ]


def attend(run, table, q, kv, outer, sproj, ids_row, ids_col):
    rows = q.shape[0]
    heads = q.shape[1] // HS
    pieces, blocks, part, _ = sproj.shape
    return pl.pallas_call(
        attend_kernel,
        grid=(heads, blocks),
        out_shape=(
            jax.ShapeDtypeStruct((rows, heads * HS), LOW),
            jax.ShapeDtypeStruct((heads, blocks, 1, BLK), F32),
        ),
        in_specs=attend_specs(heads, pieces, part, blocks),
        out_specs=(
            pl.BlockSpec((BLK, HS), lambda h, b: (b, h)),
            pl.BlockSpec((None, None, 1, BLK), lambda h, b: (h, b, 0, 0)),
        ),
        scratch_shapes=[pltpu.VMEM((2 * BLK, BLK), F32), pltpu.VMEM((3, BLK, BLK), F32)],
        compiler_params=params(2, 20),
        cost_estimate=lasts(9.7),
        name="attend",
    )(run, table, q, kv, kv, kv, kv, outer, outer, sproj, sproj, ids_row, ids_col)


def attend_back_kernel(
    run_ref, table_ref, q_ref, kc_ref, vc_ref, kp_ref, vp_ref, ko_ref, vo_ref, ks_ref, vs_ref,
    row_ref, col_ref, gmix_ref, lse_ref,
    gq_ref, gcur_ref, gprev_ref, gs_ref, gtab_ref,
    bias_ref, gbias_ref, prob_ref, gprob_ref,
):
    h = pl.program_id(0)
    b = pl.program_id(1)

    @pl.when(b == 0)
    def _():
        fill_bias(table_ref, h, bias_ref)
        gbias_ref[...] = jnp.zeros_like(gbias_ref)

    q = q_ref[...]
    gmix = gmix_ref[...]
    lse = lse_ref[...]
    first = b == 0
    keys = (
        ks_ref[...].reshape(BLK, HS),
        jnp.where(first, ko_ref[...], kp_ref[...]),
        kc_ref[...],
    )
    values = (
        vs_ref[...].reshape(BLK, HS),
        jnp.where(first, vo_ref[...], vp_ref[...]),
        vc_ref[...],
    )
    prior_ok = (run_ref[0] > 0) | (b > 0)
    inner = jnp.zeros((1, BLK), F32)
    grad_values = []
    for c in range(3):
        score = mm(keys[c], q, 1, 1) * SCALE
        if c == 1:
            score = jnp.where(prior_ok, score + bias_ref[:BLK], -1e30)
        if c == 2:
            score = jnp.where(current_mask(col_ref, row_ref), score + bias_ref[BLK:], -1e30)
        prob = jnp.exp(score - lse)
        prob_ref[c] = prob
        grad_values.append(mm(prob.astype(LOW), gmix, 1, 0))
        grad_prob = mm(values[c], gmix, 1, 1)
        gprob_ref[c] = grad_prob
        inner = inner + jnp.sum(prob * grad_prob, axis=0, keepdims=True)
    grad_q = jnp.zeros((HS, BLK), F32)
    grad_keys = []
    for c in range(3):
        grad_score = (prob_ref[c] * (gprob_ref[c] - inner)).astype(LOW)
        if c > 0:
            gbias_ref[(c - 1) * BLK : c * BLK, :] += grad_score.astype(F32)
        grad_keys.append(mm(grad_score, q, 1, 0) * SCALE)
        grad_q = grad_q + mm(keys[c], grad_score, 0, 0)
    gq_ref[...] = (grad_q * SCALE).T.astype(LOW)
    part = gs_ref.shape[0], gs_ref.shape[1], HS
    gs_ref[:, :, :HS] = grad_keys[0].astype(LOW).reshape(part)
    gs_ref[:, :, HS:] = grad_values[0].astype(LOW).reshape(part)
    gprev_ref[:, :HS] = grad_keys[1].astype(LOW)
    gprev_ref[:, HS:] = grad_values[1].astype(LOW)
    gcur_ref[:, :HS] = grad_keys[2].astype(LOW)
    gcur_ref[:, HS:] = grad_values[2].astype(LOW)

    @pl.when(b == pl.num_programs(1) - 1)
    def _():
        collapse_bias(gbias_ref, gtab_ref)


def attend_back(run, table, q, kv, outer, sproj, ids_row, ids_col, gmix, lse):
    rows = q.shape[0]
    heads = q.shape[1] // HS
    pieces, blocks, part, _ = sproj.shape

    def at():
        return pl.BlockSpec((BLK, HS), lambda h, b: (b, h))

    side = jax.ShapeDtypeStruct((rows, heads * 2 * HS), LOW)
    pair = pl.BlockSpec((BLK, 2 * HS), lambda h, b: (b, h))
    return pl.pallas_call(
        attend_back_kernel,
        grid=(heads, blocks),
        out_shape=(
            jax.ShapeDtypeStruct((rows, heads * HS), LOW),
            side,
            side,
            jax.ShapeDtypeStruct((pieces, blocks, part, heads * 2 * HS), LOW),
            jax.ShapeDtypeStruct((heads, 8, HS), F32),
        ),
        in_specs=attend_specs(heads, pieces, part, blocks)
        + [at(), pl.BlockSpec((None, None, 1, BLK), lambda h, b: (h, b, 0, 0))],
        out_specs=(
            at(),
            pair,
            pair,
            pl.BlockSpec((pieces, None, part, 2 * HS), lambda h, b: (0, b, 0, h)),
            pl.BlockSpec((None, 8, HS), lambda h, b: (h, 0, 0)),
        ),
        scratch_shapes=[
            pltpu.VMEM((2 * BLK, BLK), F32),
            pltpu.VMEM((2 * BLK, BLK), F32),
            pltpu.VMEM((3, BLK, BLK), F32),
            pltpu.VMEM((3, BLK, BLK), F32),
        ],
        compiler_params=params(2, 28),
        cost_estimate=lasts(16),
        name="attend_back",
    )(run, table, q, kv, kv, kv, kv, outer, outer, sproj, sproj, ids_row, ids_col, gmix, lse)


def state_back_kernel(
    sq_ref, k_ref, v_ref, gmix_ref, gcur_ref, gnext_ref, gouter_ref,
    gkv_ref, gsq_ref, smix_ref,
):
    b = pl.program_id(1)
    last = b == pl.num_programs(1) - 1
    pieces, part = sq_ref.shape[0], sq_ref.shape[1]
    sq = sq_ref[...].reshape(BLK, HS)
    gmix = gmix_ref[...].reshape(BLK, HS)
    k, v = k_ref[...], v_ref[...]
    weights = column_softmax(mm(k, sq, 1, 1) * SCALE)
    low = weights.astype(LOW)
    grad_w = mm(v, gmix, 1, 1)
    inner = jnp.sum(grad_w * weights, axis=0, keepdims=True)
    grad_s = (weights * (grad_w - inner)).astype(LOW)
    grad_k = mm(grad_s, sq, 1, 0) * SCALE
    grad_v = mm(low, gmix, 1, 0)
    grad_q = mm(k, grad_s, 0, 0) * SCALE
    smix = mm(v, low, 0, 0)
    rest = gcur_ref[...].astype(F32) + jnp.where(last, gouter_ref[...], gnext_ref[...]).astype(F32)
    gkv_ref[:, :HS] = (rest[:, :HS] + grad_k).astype(LOW)
    gkv_ref[:, HS:] = (rest[:, HS:] + grad_v).astype(LOW)
    gsq_ref[...] = grad_q.T.astype(LOW).reshape(pieces, part, HS)
    smix_ref[...] = smix.T.astype(LOW).reshape(pieces, part, HS)


def state_back(sq, kv, gmix, gcur, gprev, outer):
    rows = gcur.shape[0]
    heads = gcur.shape[1] // (2 * HS)
    pieces, blocks, part, _ = sq.shape

    def at(col=lambda h: h):
        return pl.BlockSpec((BLK, HS), lambda h, b: (b, col(h)))

    def state():
        return pl.BlockSpec((pieces, None, part, HS), lambda h, b: (0, b, 0, h))

    side = jax.ShapeDtypeStruct((pieces, blocks, part, heads * HS), LOW)
    return pl.pallas_call(
        state_back_kernel,
        grid=(heads, blocks),
        out_shape=(jax.ShapeDtypeStruct((rows, heads * 2 * HS), LOW), side, side),
        in_specs=[
            state(),
            at(),
            at(lambda h: heads + h),
            state(),
            pl.BlockSpec((BLK, 2 * HS), lambda h, b: (b, h)),
            pl.BlockSpec((BLK, 2 * HS), lambda h, b: (jnp.minimum(b + 1, blocks - 1), h)),
            pl.BlockSpec((BLK, 2 * HS), lambda h, b: (0, h)),
        ],
        out_specs=(
            pl.BlockSpec((BLK, 2 * HS), lambda h, b: (b, h)),
            state(),
            state(),
        ),
        compiler_params=params(2, 16),
        cost_estimate=lasts(6.5),
        name="state_back",
    )(sq, kv, kv, gmix, gcur, gprev, outer)


def passed_along(array, axis, by):
    size = lax.axis_size(axis)
    pairs = [(i, i + by) for i in range(size) if 0 <= i + by < size]
    return lax.ppermute(array, axis, pairs)


def swap(array, axis, bits):
    return lax.ppermute(array, axis, [(i, i ^ bits) for i in range(lax.axis_size(axis))])


def gather_rel(array, filler=None):
    size = lax.axis_size("tensor")
    pieces = []
    for m in range(0, size, 2):
        piece = array if m == 0 else swap(array, "tensor", m)
        if m and filler is not None:
            piece = after(piece, filler)
        pieces += [piece, swap(piece, "tensor", 1)]
    return pieces


def reduce_first(even, odd):
    got = swap(odd, "tensor", 1)
    return [even[j].astype(F32) + got[j].astype(F32) for j in range(even.shape[0])]


def reduce_last(sums, filler=None):
    terms = [sums[0]]
    for j, send in enumerate(sums[1:], 1):
        term = swap(send, "tensor", 2 * j)
        terms.append(term if filler is None else after(term, filler))
    return terms


def lower(sums):
    return [sums[0]] + [term.astype(LOW) for term in sums[1:]]


def exchange_rel(parts):
    return [part if m == 0 else swap(part, "tensor", m) for m, part in enumerate(parts)]


def cut(array, me):
    size = lax.axis_size("tensor")
    rows = array.shape[0] // size
    return [lax.dynamic_slice_in_dim(array, (me ^ m) * rows, rows, 0) for m in range(size)]


def place(pieces, me):
    rows = pieces[0].shape[0]
    out = jnp.zeros((rows * len(pieces),) + pieces[0].shape[1:], pieces[0].dtype)
    for m, piece in enumerate(pieces):
        out = lax.dynamic_update_slice_in_dim(out, piece, (me ^ m) * rows, 0)
    return out


def sum_all(array):
    for axis in ("tensor", "context", "shard"):
        bits = 1
        while bits < lax.axis_size(axis):
            array = array + swap(array, axis, bits)
            bits *= 2
    return array


def rms_back(v, gain, grad):
    r = rms_scale(v)
    unit = v * r
    scaled = grad * gain
    return r * (scaled - unit * jnp.mean(scaled * unit, axis=-1, keepdims=True))


def dot(a, b, ca, cb):
    return lax.dot_general(a, b, (((ca,), (cb,)), ((), ())), preferred_element_type=F32)


def after(array, *others):
    return lax.optimization_barrier((array,) + others)[0]


def half_rows(local, run):
    part = local.shape[0] // 2
    return lax.dynamic_slice_in_dim(local, run * part, part, 0)


def shard_pieces(array):
    return [array if s == 0 else swap(array, "shard", s) for s in range(lax.axis_size("shard"))]


def scatter_rows(grad):
    return lax.psum_scatter(grad, "shard", scatter_dimension=0, tiled=True)


def shards(
    tokens,
    piece_ids,
    tok_qkv,
    state_qkv,
    tok_out,
    state_out,
    mlp_in,
    mlp_out,
    rel_bias,
    init_state,
    norm_gains,
    decay_param,
    cotangent,
):
    size = lax.axis_size("tensor")
    shard_count = lax.axis_size("shard")
    me = lax.axis_index("tensor")
    shard_pos = lax.axis_index("shard")
    run_pos = lax.axis_index("context")
    run_count = lax.axis_size("context")
    me_arr = me.astype(jnp.int32)[None]
    run_arr = run_pos.astype(jnp.int32)[None]
    pos = jnp.stack([shard_pos, run_pos]).astype(jnp.int32)
    own = tokens[0]
    own_rows, width = own.shape
    rows = own_rows * size
    blocks = rows // BLK
    heads = tok_qkv.shape[1]
    part = init_state.shape[0]
    span = heads * HS

    cols = norm_gains.shape[1]
    bias_rows = rel_bias.shape[0]
    slot_size = NBUCKET * heads
    small = jnp.zeros((SMALL, width), LOW)
    small = lax.dynamic_update_slice(
        small, jnp.concatenate([norm_gains, decay_param[None]], 0), (0, (shard_pos * size + me) * cols)
    )
    small = lax.dynamic_update_slice(
        small, rel_bias.reshape(1, -1), (4, me * slot_size + shard_pos * bias_rows * heads)
    )
    small = sum(piece.astype(F32) for piece in shard_pieces(small)).astype(LOW)
    token_pieces = gather_rel(jnp.concatenate([own, small], axis=0))

    local_chain = jnp.concatenate(
        [state_qkv[:, :, :HS].reshape(-1, span), state_out.reshape(span, -1).T, init_state.T], axis=1
    )
    chain_pieces = shard_pieces(half_rows(local_chain, run_pos))
    chain_other = swap(jnp.stack(chain_pieces), "context", 1)
    tok_parts = shard_pieces(after(tok_qkv.reshape(-1, heads * 384), small, *chain_pieces))
    chain_other = after(chain_other, *token_pieces)
    chain_own, start = assemble(pos, chain_pieces, chain_other, (2 * span, part))
    start = start.astype(F32).T
    chain_w = gather_rel(chain_own)
    w_sq, w_sout = chain_own[:, :span], chain_own[:, span:]

    local_side = jnp.concatenate(
        [state_qkv[:, :, HS:].reshape(-1, 2 * span), tok_out.reshape(span, -1).T], axis=1
    )
    local_mlp = jnp.concatenate([mlp_in, mlp_out.T], axis=1)

    q, normed_a, vectors, wq_tok, wkv_tok, kv, *kv_blocks = token_proj(
        me_arr, pos, token_pieces, [after(piece, chain_own) for piece in tok_parts], blocks
    )
    w_side = lax.all_gather(after(local_side, q), "shard", axis=0, tiled=True)
    w_skv, w_tout = w_side[:, : 2 * span], w_side[:, 2 * span :]
    gains = vectors[:3]
    decay = jax.nn.sigmoid(vectors[3:4])
    table = lax.dynamic_slice_in_dim(vectors[4], me * slot_size, slot_size, 0)
    table = table.reshape(NBUCKET, heads).T
    kv_pieces = [gather_rel(after(kv_blocks[0], *chain_w))]
    outer = passed_along(kv_blocks[-1], "context", 1)

    gain_s = gains[2:3]
    incoming = start = after(start, outer)
    for round_index in range(run_count):
        state = jnp.where(run_pos == 0, start, incoming)
        states, normeds, updates = [], [], []
        for b in range(blocks):
            states.append(state)
            if b == len(kv_pieces):
                kv_pieces.append(gather_rel(after(kv_blocks[b], *kv_pieces[-1]), state))
            normed, update, state = chain_forward(state, gain_s, decay, kv_pieces[b], chain_w)
            if round_index + b == 0:
                w_mlp = lax.all_gather(after(local_mlp, state), "shard", axis=0, tiled=True)
            normeds.append(normed)
            updates.append(update)
        if round_index + 1 < run_count:
            incoming = passed_along(state.astype(LOW), "context", 1)
            if round_index == 0:
                grad_pieces = gather_rel(after(cotangent[0], *kv_pieces[-1]))
                tout_pieces = gather_rel(after(w_tout, *grad_pieces))
            incoming = incoming.astype(F32)
    units = mlp_in.shape[1]
    w_in, w_out = w_mlp[:, :units], w_mlp[:, units:]
    normeds[-1] = (states[-1] * rms_scale(states[-1]) * gain_s).astype(LOW)
    state_pieces = gather_rel(jnp.concatenate(normeds, axis=0), updates[-1])
    sq, skv = proj(state_pieces, [w_sq, w_skv])
    sq = sq.reshape(size, blocks, part, span)
    skv = skv.reshape(size, blocks, part, 2 * span)

    ids_row = piece_ids.reshape(blocks, 1, BLK)
    ids_col = piece_ids.reshape(blocks, BLK, 1)
    mixed, lse = attend(run_arr, table, q, kv, outer, skv, ids_row, ids_col)
    mixed_parts = cut(mixed, me)
    residual, normed_m, squares = branch_out(own, gains[1:2], exchange_rel(mixed_parts), tout_pieces)

    (grad_hidden,) = proj([after(piece, normed_m) for piece in grad_pieces], [w_out])
    mlp_pieces = gather_rel(normed_m, grad_hidden)
    hidden, grad_pre, even, odd = feed(w_in, grad_hidden, mlp_pieces)
    sums = lower(reduce_first(even, odd))
    grad_w_mlp = weight_grad([(mlp_pieces, after(grad_pre, *sums)), (grad_pieces, hidden)])
    terms = reduce_last(sums, grad_w_mlp)
    mlp_mine = scatter_rows(grad_w_mlp)

    grad_res, grad_branch, grad_gain_m, *gmix_parts = branch_back(
        cotangent[0], residual, gains[1:2], terms, tout_pieces
    )
    gmix = place(exchange_rel(gmix_parts), me)
    gq, gcur, gprev, gs, gtab = attend_back(
        run_arr, table, q, kv, outer, skv, ids_row, ids_col, gmix, lse
    )
    branch_pieces = gather_rel(after(grad_branch, gmix), gq)
    gs = after(gs, branch_pieces[-2])
    outer_back = passed_along(gprev[:BLK], "context", -1)

    gs = gs.reshape(-1, 2 * span)
    zero_arr = jnp.zeros((1,), jnp.int32)
    even, odd = back(zero_arr, [gs], [w_skv])
    sums = lower(reduce_first(even, odd))
    even, odd = back(zero_arr, [after(hidden, *sums)], [w_out])
    grad_state_kv = sum(term.astype(F32) for term in reduce_last(sums, even))
    grad_state_kv = after(grad_state_kv, outer_back).reshape(blocks, part, width)
    sums = lower(reduce_first(even, odd))
    branch_m = reduce_last([after(term, grad_state_kv) for term in sums])

    incoming = jnp.zeros_like(start)
    for round_index in range(run_count):
        carry = jnp.where(run_pos == run_count - 1, 0.0, incoming)
        gups = [None] * blocks
        gup = ((1.0 - decay) * carry).astype(LOW)
        chain_small = jnp.zeros((2, width), F32)
        for b in reversed(range(blocks)):
            gups[b] = gup
            carry, gup, row_sums = chain_backward(
                carry, gain_s, decay, states[b], normeds[b], updates[b], grad_state_kv[b],
                kv_pieces[b], chain_w,
            )
            chain_small = chain_small + row_sums
        if round_index + 1 < run_count:
            incoming = passed_along(carry.astype(LOW), "context", -1)
            if round_index == 0:
                grad_w_early = weight_grad(
                    [
                        ([normed_a], after(gq, carry)),
                        (state_pieces, gs),
                        (branch_pieces, jnp.concatenate(mixed_parts, axis=0)),
                    ]
                )
                incoming = after(incoming, grad_w_early, mlp_mine, *branch_m)
            incoming = incoming.astype(F32)
    grad_start = jnp.where(run_pos == 0, carry, 0.0).astype(LOW)
    branch_m = sum(term.astype(F32) for term in branch_m)
    output = (residual + branch_m).astype(LOW)
    gup_pieces = gather_rel(jnp.concatenate(gups, axis=0), carry)
    mlp_got = swap(after(mlp_mine, incoming), "context", 1)
    early_mine = scatter_rows(after(grad_w_early, mlp_mine))
    (gsmix,) = proj(gup_pieces, [w_sout])
    gsmix = gsmix.reshape(size, blocks, part, span)
    gkv, gsq, smix = state_back(sq, kv, gsmix, gcur, gprev, outer_back)
    grad_w_late = weight_grad(
        [([normed_a], gkv), (state_pieces, gsq.reshape(-1, span)), (gup_pieces, smix.reshape(-1, span))]
    )
    late_mine = scatter_rows(jnp.concatenate([after(grad_w_late, early_mine), grad_start.T], axis=1))
    early_got = swap(after(early_mine, mlp_got), "context", 1)
    g_mlp = mlp_mine.astype(F32) + mlp_got.astype(F32)
    g_early = early_mine.astype(F32) + early_got.astype(F32)
    g_late = late_mine.astype(F32) + swap(late_mine, "context", 1).astype(F32)

    even, odd, gain_sums = back(me_arr, [gq, after(gkv, grad_w_late)], [wq_tok, wkv_tok], normed_a)
    grad_gain_a = (gain_sums / gains[0:1])[0]
    inputs = own.astype(F32)
    grad_normed_a = sum(
        term.astype(F32) for term in reduce_last(lower(reduce_first(even, odd)))
    )
    grad_tokens = (grad_res + rms_back(inputs, gains[0], grad_normed_a)).astype(LOW)

    def by_head(array):
        return array.reshape(array.shape[0], heads, -1)

    g_tok = jnp.concatenate([by_head(g_early[:, :span]), by_head(g_late[:, : 2 * span])], axis=2)
    g_state = jnp.concatenate(
        [by_head(g_late[:, 2 * span : 3 * span]), by_head(g_early[:, span : 3 * span])], axis=2
    )
    g_tout = g_early[:, 3 * span :].T.reshape(heads, HS, -1)
    g_sout = g_late[:, 3 * span : 4 * span].T.reshape(heads, HS, -1)

    squares = jnp.concatenate([jnp.sum(squares, axis=1), jnp.sum(branch_m * branch_m)[None]])
    slot = gtab[:, 0, :NBUCKET].reshape(-1)
    slots = lax.dynamic_update_slice_in_dim(
        jnp.zeros((size * slot.size,), F32), slot, me * slot.size, 0
    )
    tail = jnp.concatenate([slots, squares])
    tail = jnp.pad(tail, (0, width - tail.size))
    grad_decay = chain_small[1] * (decay * (1.0 - decay))[0]
    sums = sum_all(
        jnp.stack([grad_gain_a, grad_gain_m[0], chain_small[0], grad_decay, tail])
    )
    place_at = (shard_pos * size + me) * cols
    mine = lax.dynamic_slice_in_dim(sums[:4], place_at, cols, 1)
    table_sum = lax.dynamic_slice_in_dim(sums[4], me * slot.size, slot.size, 0)
    table_sum = table_sum.reshape(heads, NBUCKET).T
    g_table = lax.dynamic_slice_in_dim(table_sum, shard_pos * bias_rows, bias_rows, 0)
    entries = own.size * shard_count * run_count * size
    first = size * slot.size
    rms_out = jnp.sqrt(sums[4, first : first + 3] / entries)

    return (
        output[None],
        grad_tokens[None],
        g_tok,
        g_state,
        g_tout,
        g_sout,
        g_mlp[:, :units],
        g_mlp[:, units:].T,
        g_table,
        g_late[:, 4 * span :].T,
        mine[:3],
        mine[3],
        rms_out,
    )


def solution(mesh):
    return jax.shard_map(
        shards,
        mesh=mesh,
        in_specs=(
            P("shard", ("context", "tensor"), None),
            P("shard", "context"),
            P("shard", "tensor", None),
            P("shard", "tensor", None),
            P("tensor", None, "shard"),
            P("tensor", None, "shard"),
            P("shard", "tensor"),
            P("tensor", "shard"),
            P("shard", "tensor"),
            P("tensor", "shard"),
            P(None, ("shard", "tensor")),
            P(("shard", "tensor")),
            P("shard", ("context", "tensor"), None),
        ),
        out_specs=(
            P("shard", ("context", "tensor"), None),
            P("shard", ("context", "tensor"), None),
            P("shard", "tensor", None),
            P("shard", "tensor", None),
            P("tensor", None, "shard"),
            P("tensor", None, "shard"),
            P("shard", "tensor"),
            P("tensor", "shard"),
            P("shard", "tensor"),
            P("tensor", "shard"),
            P(None, ("shard", "tensor")),
            P(("shard", "tensor")),
            P(),
        ),
        check_vma=False,
    )
```

time: 667 us -> 536 us (0.80)
  blocking collectives: 63.6 us -> 0 us
  matrix products: 61.6 us -> 0 us
  waiting for transfers between devices: 248 us -> 194 us
  local copies, waits for them, and re-layouts: 38.7 us -> 61.1 us
  Pallas kernels: 147 us -> 160 us
  starting transfers between devices: 44.6 us -> 56.9 us
    unnamed x1 -> x0, blocking collectives: 63.6 us -> none
    dot_general x13 -> x0, matrix products: 61.6 us -> none  [the longest x11 51.9 us: dot(): lax.dot_general(a, b, (((ca,), (cb,)), ((), ())), preferred_element_type=...]
    pallas_call x8 -> x22, Pallas kernels: 88.8 us -> 128 us  [the longest x4 42.2 us: chain_backward(): pl.pallas_call(functools.partial(chain_backward_kernel, count, heads), ou...]
    all_gather x5 -> x2, waiting for transfers between devices: 36.4 us -> 0.01 us  [the longest x1 0.01 us: shards(): w_side = lax.all_gather(after(local_side, q), 'shard', axis=0, tiled=True)]
    unnamed x107 -> x233, local copies, waits for them, and re-layouts: 15.5 us -> 40.7 us
    reduce_scatter x5 -> x3, waiting for transfers between devices: 25.2 us -> 0.01 us  [scatter_rows(): return lax.psum_scatter(grad, 'shard', scatter_dimension=0, tiled=True)]
    pallas_call x1, Pallas kernels: 31.4 us -> 15.6 us  [attend_back(): pl.pallas_call(attend_back_kernel, grid=(heads, blocks), out_shape=(jax.S...]
    ppermute x51 -> x62, waiting for transfers between devices: 164 us -> 179 us  [swap(): lax.ppermute(array, axis, [(i, i ^ bits) for i in range(lax.axis_size(axi...]
  transfers between devices with their start and end apart: 65 -> 71, of which waited for: 27 -> 36; matrix products, arithmetic and copies ran while one was open for 17% -> 11% of each run, Pallas kernels for 18% -> 28%
where the time goes in v2:
time: 536 us; the launch traced here: 528 us
  waiting for transfers between devices  194 us (36%)
  Pallas kernels  160 us (30%)
  local copies, waits for them, and re-layouts  61.1 us (11%)
  starting transfers between devices  56.9 us (11%)
  other arithmetic  40.2 us (8%)
  between operations  15.7 us (3%)
    ppermute x62, waiting for transfers between devices, swap(): lax.ppermute(array, axis, [(i, i ^ bits) for i in range(lax.axis_size(axi...  179 us
    ppermute x62, starting transfers between devices, swap(): lax.ppermute(array, axis, [(i, i ^ bits) for i in range(lax.axis_size(axi...  46.9 us
    pallas_call x4, Pallas kernels, chain_backward(): pl.pallas_call(functools.partial(chain_backward_kernel, count, heads), ou...  42.2 us
    unnamed x233, local copies, waits for them, and re-layouts  40.7 us
    pallas_call x4, Pallas kernels, chain_forward(): pl.pallas_call(functools.partial(chain_forward_kernel, count, heads), out...  33.9 us
    pallas_call x3, Pallas kernels, weight_grad(): pl.pallas_call(functools.partial(weight_grad_kernel, [len(lefts) for left...  17.3 us
    pallas_call x1, Pallas kernels, attend_back(): pl.pallas_call(attend_back_kernel, grid=(heads, blocks), out_shape=(jax.S...  15.6 us
    ppermute x4, waiting for transfers between devices, passed_along(): return lax.ppermute(array, axis, pairs)  14.7 us
  transfers between devices with their start and end apart: 71, of which 36 were waited for; matrix products, arithmetic and copies ran while one was open for 11% of the time, Pallas kernels for 28%

profile of v2, /device:TPU:0, one launch (start us, length us, event | category | flops | bytes accessed | tf_op | source)
XLA Modules:
  0.0 527.6 jit_solution(4955161661243742096)
XLA Ops:
  29.3 7.9 %collective-permute-done.7.refs_2_ = bf16[128,640]{1,0:T(8,128)(2,1)S(1)} collective-permute-done((bf16[128,640]{1,0:T(8,128)(2,1)S(1)}, bf16[128,640]{1,0:T(8,128)(2,1)S(1)}, u32[]{:S(2)}, u32[]{:S(2)}) %collective-permute-start.7) | collective-permute-done | bytes 163872 | tf_op jit(solution)/shard_map/ppermute | solution.py:806
  41.7 11.3 %collective-permute-done.9.refs_4_ = bf16[4,128,640]{2,1,0:T(8,128)(2,1)S(1)} collective-permute-done((bf16[4,128,640]{2,1,0:T(8,128)(2,1)S(1)}, bf16[4,128,640]{2,1,0:T(8,128)(2,1)S(1)}, u32[]{:S(2)}, u32[]{:S(2)}) %collective-permute-start.9) | collective-permute-done | bytes 655392 | tf_op jit(solution)/shard_map/ppermute | solution.py:806
  62.2 14.8 %collective-permute-done.15.refs_6_ = bf16[1024,512]{1,0:T(8,128)(2,1)} collective-permute-done((bf16[1024,512]{1,0:T(8,128)(2,1)S(1)}, bf16[1024,512]{1,0:T(8,128)(2,1)}, u32[]{:S(2)}, u32[]{:S(2)}) %collective-permute-start.15) | collective-permute-done | bytes 1048608 | tf_op jit(solution)/shard_map/ppermute | solution.py:806
  79.5 11.1 %collective-permute-done.11.refs_6_ = bf16[256,768]{1,0:T(8,128)(2,1)} collective-permute-done((bf16[256,768]{1,0:T(8,128)(2,1)S(1)}, bf16[256,768]{1,0:T(8,128)(2,1)}, u32[]{:S(2)}, u32[]{:S(2)}) %collective-permute-start.11) | collective-permute-done | bytes 393248 | tf_op jit(solution)/shard_map/ppermute | solution.py:806
  110.4 8.0 %collective-permute-done.18.refs_2_ = bf16[512,512]{1,0:T(8,128)(2,1)S(1)} collective-permute-done((bf16[512,512]{1,0:T(8,128)(2,1)}, bf16[512,512]{1,0:T(8,128)(2,1)S(1)}, u32[]{:S(2)}, u32[]{:S(2)}) %collective-permute-start.18) | collective-permute-done | bytes 524320 | tf_op jit(solution)/shard_map/ppermute | solution.py:806
  123.4 8.4 %chain_forward.4 = (bf16[128,1024]{1,0:T(8,128)(2,1)}, f32[128,1024]{1,0:T(8,128)}, f32[128,1024]{1,0:T(8,128)}) custom-call(f32[128,1024]{1,0:T(8,128)} %convert_bitcast_fusion.state_ref, f32[1,1024]{1,0:T(1,128)} %get-tuple-element.255.gain_ref, f32[1,1024]{1,0:T(1,128)} %get-tuple-element.228.dec_ref, bf16[512,512]{1,0:T(8,128)(2,1)} %copy-done.40, ...), custom_call_target="tpu_custom_call" | custom-call | flops 3575000064 | bytes 9750000 | tf_op jit(solution)/shard_map/chain_forward/pallas_call | solution.py:401
  133.4 12.8 %collective-permute-done.21.refs_2_ = bf16[512,512]{1,0:T(8,128)(2,1)S(1)} collective-permute-done((bf16[512,512]{1,0:T(8,128)(2,1)S(1)}, bf16[512,512]{1,0:T(8,128)(2,1)S(1)}, u32[]{:S(2)}, u32[]{:S(2)}) %collective-permute-start.21) | collective-permute-done | bytes 524320 | tf_op jit(solution)/shard_map/ppermute | solution.py:806
  149.0 8.8 %chain_forward.5 = (bf16[128,1024]{1,0:T(8,128)(2,1)}, f32[128,1024]{1,0:T(8,128)}, f32[128,1024]{1,0:T(8,128)}) custom-call(f32[128,1024]{1,0:T(8,128)} %get-tuple-element.122.state_ref, f32[1,1024]{1,0:T(1,128)} %get-tuple-element.255.gain_ref, f32[1,1024]{1,0:T(1,128)} %get-tuple-element.228.dec_ref, bf16[512,512]{1,0:T(8,128)(2,1)} %copy-done.41, ...), custom_call_target="tpu_custom_call" | custom-call | flops 3575000064 | bytes 9750000 | tf_op jit(solution)/shard_map/chain_forward/pallas_call | solution.py:401
  163.7 4.5 collective-permute-done.23
  169.0 8.3 %chain_forward.6 = (bf16[128,1024]{1,0:T(8,128)(2,1)}, f32[128,1024]{1,0:T(8,128)}, f32[128,1024]{1,0:T(8,128)}) custom-call(f32[128,1024]{1,0:T(8,128)} %convert_select_fusion.state_ref, f32[1,1024]{1,0:T(1,128)} %get-tuple-element.255.gain_ref, f32[1,1024]{1,0:T(1,128)} %get-tuple-element.228.dec_ref, bf16[512,512]{1,0:T(8,128)(2,1)} %copy-done.40, ...), custom_call_target="tpu_custom_call" | custom-call | flops 3575000064 | bytes 9750000 | tf_op jit(solution)/shard_map/chain_forward/pallas_call | solution.py:401
  182.7 8.3 %chain_forward.7 = (bf16[128,1024]{1,0:T(8,128)(2,1)}, f32[128,1024]{1,0:T(8,128)}, f32[128,1024]{1,0:T(8,128)}) custom-call(f32[128,1024]{1,0:T(8,128)} %get-tuple-element.127.state_ref, f32[1,1024]{1,0:T(1,128)} %get-tuple-element.255.gain_ref, f32[1,1024]{1,0:T(1,128)} %get-tuple-element.228.dec_ref, bf16[512,512]{1,0:T(8,128)(2,1)} %copy-done.41, ...), custom_call_target="tpu_custom_call" | custom-call | flops 3575000064 | bytes 9750000 | tf_op jit(solution)/shard_map/chain_forward/pallas_call | solution.py:401
  209.7 9.5 %attend.1 = (bf16[1024,256]{1,0:T(8,128)(2,1)S(1)}, f32[2,2,1,512]{3,2,1,0:T(1,128)S(1)}) custom-call(s32[1]{0:T(128)} %bitcast.3.run_ref, f32[2,32]{1,0:T(2,128)S(1)} %bitcast.109, bf16[1024,256]{1,0:T(8,128)(2,1)S(1)} %copy-done.80, bf16[1024,512]{1,0:T(8,128)(2,1)S(1)} %copy-done.74, bf16[1024,512]{1,0:T(8,128)(2,1)S(1)} %copy-done.74, ...), custom_call_target="tpu_custom_call" | custom-call | flops 5335000064 | bytes 14549999 | tf_op jit(solution)/shard_map/attend/pallas_call | solution.py:612
  221.3 4.9 collective-permute-done.28.refs_2_
  239.9 5.0 collective-permute-done.37.refs_2_
  247.0 6.8 %feed.1 = (bf16[1024,1024]{1,0:T(8,128)(2,1)S(1)}, bf16[1024,1024]{1,0:T(8,128)(2,1)S(1)}, bf16[2,256,1024]{2,1,0:T(8,128)(2,1)S(1)}, bf16[2,256,1024]{2,1,0:T(8,128)(2,1)S(1)}) custom-call(bf16[1024,1024]{1,0:T(8,128)(2,1)S(1)} %get-tuple-element.230.w_ref, bf16[1024,1024]{1,0:T(8,128)(2,1)S(1)} %proj.4.ghid_ref, ...), custom_call_target="tpu_custom_call" | custom-call | flops 3849999872 | bytes 10500000 | tf_op jit(solution)/shard_map/feed/pallas_call | solution.py:349
  258.2 6.8 %weight_grad.3 = bf16[1024,2048]{1,0:T(8,128)(2,1)S(1)} custom-call(bf16[256,1024]{1,0:T(8,128)(2,1)} %get-tuple-element.137.refs_0_, bf16[256,1024]{1,0:T(8,128)(2,1)} %collective-permute-done.36.refs_1_, bf16[256,1024]{1,0:T(8,128)(2,1)} %collective-permute-done.37.refs_2_, bf16[256,1024]{1,0:T(8,128)(2,1)S(1)} %collective-permute-done.38.refs_3_, ...), custom_call_target="tpu_custom_call" | custom-call | flops 3300000000 | bytes 9000000 | tf_op jit(solution)/shard_map/weight_grad/pallas_call | solution.py:110
  269.3 12.7 %collective-permute-done.40.refs_1_ = bf16[256,1024]{1,0:T(8,128)(2,1)S(1)} collective-permute-done((bf16[256,1024]{1,0:T(8,128)(2,1)S(1)}, bf16[256,1024]{1,0:T(8,128)(2,1)S(1)}, u32[]{:S(2)}, u32[]{:S(2)}) %collective-permute-start.40) | collective-permute-done | bytes 524320 | tf_op jit(solution)/shard_map/ppermute | solution.py:806
  282.8 4.6 branch_back.1
  298.5 15.6 %attend_back.1 = (bf16[1024,256]{1,0:T(8,128)(2,1)S(1)}, bf16[1024,512]{1,0:T(8,128)(2,1)S(1)}, bf16[1024,512]{1,0:T(8,128)(2,1)S(1)}, bf16[4,2,128,512]{3,2,1,0:T(8,128)(2,1)S(1)}, f32[2,8,128]{2,1,0:T(8,128)S(1)}) custom-call(s32[1]{0:T(128)} %bitcast.3.run_ref, f32[2,32]{1,0:T(2,128)S(1)} %bitcast.110, bf16[1024,256]{1,0:T(8,128)(2,1)S(1)} %copy-done.81, ...), custom_call_target="tpu_custom_call" | custom-call | flops 8800000000 | bytes 24000000 | tf_op jit(solution)/shard_map/attend_back/pallas_call | solution.py:706
  326.4 7.2 %collective-permute-done.47 = bf16[256,1024]{1,0:T(8,128)(2,1)S(1)} collective-permute-done((bf16[256,1024]{1,0:T(8,128)(2,1)S(1)}, bf16[256,1024]{1,0:T(8,128)(2,1)S(1)}, u32[]{:S(2)}, u32[]{:S(2)}) %collective-permute-start.47) | collective-permute-done | bytes 524320 | tf_op jit(solution)/shard_map/ppermute | solution.py:806
  338.2 10.5 %chain_backward.4 = (f32[128,1024]{1,0:T(8,128)}, bf16[128,1024]{1,0:T(8,128)(2,1)}, f32[2,1024]{1,0:T(2,128)}) custom-call(f32[128,1024]{1,0:T(8,128)} %broadcast_in_dim.41.carry_ref, f32[1,1024]{1,0:T(1,128)} %get-tuple-element.255.gain_ref, f32[1,1024]{1,0:T(1,128)} %get-tuple-element.228.dec_ref, f32[128,1024]{1,0:T(8,128)} %get-tuple-element.127.state_ref, ...), custom_call_target="tpu_custom_call" | custom-call | flops 4565000192 | bytes 12450000 | tf_op jit(solution)/shard_map/chain_backward/pallas_call | solution.py:460
  348.7 10.6 %chain_backward.5 = (f32[128,1024]{1,0:T(8,128)}, bf16[128,1024]{1,0:T(8,128)(2,1)}, f32[2,1024]{1,0:T(2,128)}) custom-call(f32[128,1024]{1,0:T(8,128)} %get-tuple-element.172.carry_ref, f32[1,1024]{1,0:T(1,128)} %get-tuple-element.255.gain_ref, f32[1,1024]{1,0:T(1,128)} %get-tuple-element.228.dec_ref, f32[128,1024]{1,0:T(8,128)} %convert_select_fusion.state_ref, ...), custom_call_target="tpu_custom_call" | custom-call | flops 4565000192 | bytes 12450000 | tf_op jit(solution)/shard_map/chain_backward/pallas_call | solution.py:460
  359.4 5.7 %weight_grad.4 = bf16[1024,1024]{1,0:T(8,128)(2,1)} custom-call(bf16[1024,1024]{1,0:T(8,128)(2,1)S(1)} %copy-done.62, bf16[1024,256]{1,0:T(8,128)(2,1)S(1)} %get-tuple-element.176.refs_1_.refs_0_, bf16[256,1024]{1,0:T(8,128)(2,1)S(1)} %copy-done.26, bf16[256,1024]{1,0:T(8,128)(2,1)} %collective-permute-done.24.refs_1_.refs_3_, ...), custom_call_target="tpu_custom_call" | custom-call | flops 3300000000 | bytes 9000000 | tf_op jit(solution)/shard_map/weight_grad/pallas_call | solution.py:110
  371.6 7.9 %collective-permute-done.50 = bf16[128,1024]{1,0:T(8,128)(2,1)S(1)} collective-permute-done((bf16[128,1024]{1,0:T(8,128)(2,1)S(1)}, bf16[128,1024]{1,0:T(8,128)(2,1)S(1)}, u32[]{:S(2)}, u32[]{:S(2)}) %collective-permute-start.50) | collective-permute-done | bytes 262176 | tf_op jit(solution)/shard_map/ppermute | solution.py:802
  383.2 10.6 %chain_backward.6 = (f32[128,1024]{1,0:T(8,128)}, bf16[128,1024]{1,0:T(8,128)(2,1)}, f32[2,1024]{1,0:T(2,128)}) custom-call(f32[128,1024]{1,0:T(8,128)} %get-tuple-element.251.carry_ref, f32[1,1024]{1,0:T(1,128)} %get-tuple-element.255.gain_ref, f32[1,1024]{1,0:T(1,128)} %get-tuple-element.228.dec_ref, f32[128,1024]{1,0:T(8,128)} %get-tuple-element.127.state_ref, ...), custom_call_target="tpu_custom_call" | custom-call | flops 4565000192 | bytes 12450000 | tf_op jit(solution)/shard_map/chain_backward/pallas_call | solution.py:460
  396.1 10.5 %chain_backward.7 = (f32[128,1024]{1,0:T(8,128)}, bf16[128,1024]{1,0:T(8,128)(2,1)}, f32[2,1024]{1,0:T(2,128)}) custom-call(f32[128,1024]{1,0:T(8,128)} %get-tuple-element.179.carry_ref, f32[1,1024]{1,0:T(1,128)} %get-tuple-element.255.gain_ref, f32[1,1024]{1,0:T(1,128)} %get-tuple-element.228.dec_ref, f32[128,1024]{1,0:T(8,128)} %convert_select_fusion.state_ref, ...), custom_call_target="tpu_custom_call" | custom-call | flops 4565000192 | bytes 12450000 | tf_op jit(solution)/shard_map/chain_backward/pallas_call | solution.py:460
  416.5 6.8 %state_back.1 = (bf16[1024,512]{1,0:T(8,128)(2,1)S(1)}, bf16[4,2,128,256]{3,2,1,0:T(8,128)(2,1)S(1)}, bf16[4,2,128,256]{3,2,1,0:T(8,128)(2,1)S(1)}) custom-call(bf16[4,2,128,256]{3,2,1,0:T(8,128)(2,1)S(1)} %bitcast.117, bf16[1024,512]{1,0:T(8,128)(2,1)S(1)} %copy-done.76, bf16[1024,512]{1,0:T(8,128)(2,1)S(1)} %copy-done.76, ...), custom_call_target="tpu_custom_call" | custom-call | flops 3575000064 | bytes 9750000 | tf_op jit(solution)/shard_map/state_back/pallas_call | solution.py:775
  423.3 4.8 weight_grad.5
  450.3 12.0 %collective-permute-done.63 = f32[5,1024]{1,0:T(8,128)S(1)} collective-permute-done((f32[5,1024]{1,0:T(8,128)S(1)}, f32[5,1024]{1,0:T(8,128)S(1)}, u32[]{:S(2)}, u32[]{:S(2)}) %collective-permute-start.63) | collective-permute-done | bytes 20512 | tf_op jit(solution)/shard_map/ppermute | solution.py:806
  480.5 7.5 %collective-permute-done.57 = bf16[256,1024]{1,0:T(8,128)(2,1)S(1)} collective-permute-done((bf16[256,1024]{1,0:T(8,128)(2,1)S(1)}, bf16[256,1024]{1,0:T(8,128)(2,1)S(1)}, u32[]{:S(2)}, u32[]{:S(2)}) %collective-permute-start.57) | collective-permute-done | bytes 524320 | tf_op jit(solution)/shard_map/ppermute | solution.py:806
  493.8 10.9 %collective-permute-done.59 = bf16[256,1024]{1,0:T(8,128)(2,1)} collective-permute-done((bf16[256,1024]{1,0:T(8,128)(2,1)}, bf16[256,1024]{1,0:T(8,128)(2,1)}, u32[]{:S(2)}, u32[]{:S(2)}) %collective-permute-start.59) | collective-permute-done | bytes 524320 | tf_op jit(solution)/shard_map/ppermute | solution.py:806
  507.3 8.0 %collective-permute-done.60 = bf16[256,1152]{1,0:T(8,128)(2,1)} collective-permute-done((bf16[256,1152]{1,0:T(8,128)(2,1)}, bf16[256,1152]{1,0:T(8,128)(2,1)}, u32[]{:S(2)}, u32[]{:S(2)}) %collective-permute-start.60) | collective-permute-done | bytes 589856 | tf_op jit(solution)/shard_map/ppermute | solution.py:806
  (472 shorter events, 228.7 us)
Async XLA Ops:
  7.2 186.9 %all-gather.3.cloned.1.call-start = ((), (), s32[]{:S(2)}) async-start(), calls=%async_computation.3 | async-start | bytes 1966080 | tf_op jit(solution)/shard_map/all_gather | solution.py:957
  21.9 17.8 %collective-permute-start.4 = (bf16[272,1024]{1,0:T(8,128)(2,1)S(1)}, bf16[272,1024]{1,0:T(8,128)(2,1)S(1)}, u32[]{:S(2)}, u32[]{:S(2)}) collective-permute-start(bf16[272,1024]{1,0:T(8,128)(2,1)S(1)} %pad_maximum_fusion.5.refs_0_), channel_id=1, source_target_pairs={{0,2},{1,3},{2,0},{3,1},{4,6},{5,7},{6,4},{7,5},{8,10},{9,11},{10,... | collective-permute-start | bytes 1671176 | tf_op jit(solution)/shard_map/ppermute | solution.py:806
  38.2 14.9 %collective-permute-start.9 = (bf16[4,128,640]{2,1,0:T(8,128)(2,1)S(1)}, bf16[4,128,640]{2,1,0:T(8,128)(2,1)S(1)}, u32[]{:S(2)}, u32[]{:S(2)}) collective-permute-start(bf16[4,128,640]{2,1,0:T(8,128)(2,1)S(1)} %pad_maximum_fusion.4), channel_id=1, source_target_pairs={{0,4},{4,0},{1,5},{5,1},{2,6},{6,2},{3,7},{7,3},{8,12},{12,8},{9,1... | collective-permute-start | bytes 1966088 | tf_op jit(solution)/shard_map/ppermute | solution.py:806
  54.5 22.5 %collective-permute-start.15 = (bf16[1024,512]{1,0:T(8,128)(2,1)S(1)}, bf16[1024,512]{1,0:T(8,128)(2,1)}, u32[]{:S(2)}, u32[]{:S(2)}) collective-permute-start(bf16[1024,512]{1,0:T(8,128)(2,1)S(1)} %get-tuple-element.109.refs_4_), channel_id=1, source_target_pairs={{0,2},{1,3},{2,0},{3,1},{4,6},{5,7},{6,4},{7,5},{8,10},{9,11},{10,... | collective-permute-start | bytes 3145736 | tf_op jit(solution)/shard_map/ppermute | solution.py:806
  55.3 23.5 %collective-permute-start.12 = (bf16[256,768]{1,0:T(8,128)(2,1)S(1)}, bf16[256,768]{1,0:T(8,128)(2,1)S(1)}, u32[]{:S(2)}, u32[]{:S(2)}) collective-permute-start(bf16[256,768]{1,0:T(8,128)(2,1)S(1)} %bitcast.100), channel_id=1, source_target_pairs={{0,24},{8,16},{16,8},{24,0},{1,25},{9,17},{17,9},{25,1},{2,26},{10... | collective-permute-start | bytes 1179656 | tf_op jit(solution)/shard_map/ppermute | solution.py:806
  57.0 33.6 %collective-permute-start.11 = (bf16[256,768]{1,0:T(8,128)(2,1)S(1)}, bf16[256,768]{1,0:T(8,128)(2,1)}, u32[]{:S(2)}, u32[]{:S(2)}) collective-permute-start(bf16[256,768]{1,0:T(8,128)(2,1)S(1)} %bitcast.101), channel_id=1, source_target_pairs={{0,16},{8,24},{16,0},{24,8},{1,17},{9,25},{17,1},{25,9},{2,18},{10... | collective-permute-start | bytes 1179656 | tf_op jit(solution)/shard_map/ppermute | solution.py:806
  60.3 30.2 %collective-permute-start.10 = (bf16[256,768]{1,0:T(8,128)(2,1)S(1)}, bf16[256,768]{1,0:T(8,128)(2,1)}, u32[]{:S(2)}, u32[]{:S(2)}) collective-permute-start(bf16[256,768]{1,0:T(8,128)(2,1)S(1)} %bitcast.102), channel_id=1, source_target_pairs={{0,8},{8,0},{16,24},{24,16},{1,9},{9,1},{17,25},{25,17},{2,10},{10... | collective-permute-start | bytes 1179656 | tf_op jit(solution)/shard_map/ppermute | solution.py:806
  62.1 42.2 %collective-permute-start.14 = (bf16[1024,512]{1,0:T(8,128)(2,1)S(1)}, bf16[1024,512]{1,0:T(8,128)(2,1)}, u32[]{:S(2)}, u32[]{:S(2)}) collective-permute-start(bf16[1024,512]{1,0:T(8,128)(2,1)S(1)} %get-tuple-element.109.refs_4_), channel_id=1, source_target_pairs={{0,1},{1,0},{2,3},{3,2},{4,5},{5,4},{6,7},{7,6},{8,9},{9,8},{10,11... | collective-permute-start | bytes 3145736 | tf_op jit(solution)/shard_map/ppermute | solution.py:806
  77.0 27.3 %collective-permute-start.16 = (bf16[1024,512]{1,0:T(8,128)(2,1)}, bf16[1024,512]{1,0:T(8,128)(2,1)}, u32[]{:S(2)}, u32[]{:S(2)}) collective-permute-start(bf16[1024,512]{1,0:T(8,128)(2,1)} %collective-permute-done.15.refs_6_), channel_id=1, source_target_pairs={{0,1},{1,0},{2,3},{3,2},{4,5},{5,4},{6,7},{7,6},{8,9},{9,8},{10,11... | collective-permute-start | bytes 3145736 | tf_op jit(solution)/shard_map/ppermute | solution.py:806
  104.2 127.6 %all-gather.5.cloned.1.call-start = ((), (), s32[]{:S(2)}) async-start(), calls=%async_computation.4 | async-start | bytes 5242880 | tf_op jit(solution)/shard_map/all_gather | solution.py:977
  106.9 15.4 %collective-permute-start.13 = (bf16[512,512]{1,0:T(8,128)(2,1)}, bf16[512,512]{1,0:T(8,128)(2,1)S(1)}, u32[]{:S(2)}, u32[]{:S(2)}) collective-permute-start(bf16[512,512]{1,0:T(8,128)(2,1)} %copy-done.41), channel_id=1, source_target_pairs={{0,4},{1,5},{2,6},{3,7},{8,12},{9,13},{10,14},{11,15},{16,20},{17,... | collective-permute-start | bytes 1572872 | tf_op jit(solution)/shard_map/ppermute | solution.py:802
  131.8 233.2 %reduce-scatter.4.cloned.1.call-start = ((), (), s32[]{:S(2)}) async-start(), calls=%async_computation.5 | async-start | bytes 5242880 | tf_op jit(solution)/shard_map/reduce_scatter | solution.py:889
  132.0 14.2 %collective-permute-start.21 = (bf16[512,512]{1,0:T(8,128)(2,1)S(1)}, bf16[512,512]{1,0:T(8,128)(2,1)S(1)}, u32[]{:S(2)}, u32[]{:S(2)}) collective-permute-start(bf16[512,512]{1,0:T(8,128)(2,1)S(1)} %copy-done.42), channel_id=1, source_target_pairs={{0,2},{1,3},{2,0},{3,1},{4,6},{5,7},{6,4},{7,5},{8,10},{9,11},{10,... | collective-permute-start | bytes 1572872 | tf_op jit(solution)/shard_map/ppermute | solution.py:806
  162.3 19.8 %collective-permute-start.31 = (bf16[256,1024]{1,0:T(8,128)(2,1)S(1)}, bf16[256,1024]{1,0:T(8,128)(2,1)S(1)}, u32[]{:S(2)}, u32[]{:S(2)}) collective-permute-start(bf16[256,1024]{1,0:T(8,128)(2,1)S(1)} %bitcast.95), channel_id=1, source_target_pairs={{0,2},{1,3},{2,0},{3,1},{4,6},{5,7},{6,4},{7,5},{8,10},{9,11},{10,... | collective-permute-start | bytes 1572872 | tf_op jit(solution)/shard_map/ppermute | solution.py:806
  182.7 19.2 %collective-permute-start.24 = (bf16[256,1024]{1,0:T(8,128)(2,1)S(1)}, bf16[256,1024]{1,0:T(8,128)(2,1)}, u32[]{:S(2)}, u32[]{:S(2)}) collective-permute-start(bf16[256,1024]{1,0:T(8,128)(2,1)S(1)} %pad_maximum_fusion.6.refs_0_.refs_2_), channel_id=1, source_target_pairs={{0,1},{1,0},{2,3},{3,2},{4,5},{5,4},{6,7},{7,6},{8,9},{9,8},{10,11... | collective-permute-start | bytes 1572872 | tf_op jit(solution)/shard_map/ppermute | solution.py:806
  195.2 14.4 %collective-permute-start.34 = (bf16[1024,256]{1,0:T(8,128)(2,1)S(1)}, bf16[1024,256]{1,0:T(8,128)(2,1)S(1)}, u32[]{:S(2)}, u32[]{:S(2)}) collective-permute-start(bf16[1024,256]{1,0:T(8,128)(2,1)S(1)} %slice.207.refs_4_.refs_2_), channel_id=1, source_target_pairs={{0,2},{1,3},{2,0},{3,1},{4,6},{5,7},{6,4},{7,5},{8,10},{9,11},{10,... | collective-permute-start | bytes 1572872 | tf_op jit(solution)/shard_map/ppermute | solution.py:806
  201.6 25.7 %collective-permute-start.33 = (bf16[1024,256]{1,0:T(8,128)(2,1)S(1)}, bf16[1024,256]{1,0:T(8,128)(2,1)S(1)}, u32[]{:S(2)}, u32[]{:S(2)}) collective-permute-start(bf16[1024,256]{1,0:T(8,128)(2,1)S(1)} %slice.207.refs_4_.refs_2_), channel_id=1, source_target_pairs={{0,1},{1,0},{2,3},{3,2},{4,5},{5,4},{6,7},{7,6},{8,9},{9,8},{10,11... | collective-permute-start | bytes 1572872 | tf_op jit(solution)/shard_map/ppermute | solution.py:806
  209.7 17.6 %collective-permute-start.35 = (bf16[1024,256]{1,0:T(8,128)(2,1)S(1)}, bf16[1024,256]{1,0:T(8,128)(2,1)S(1)}, u32[]{:S(2)}, u32[]{:S(2)}) collective-permute-start(bf16[1024,256]{1,0:T(8,128)(2,1)S(1)} %collective-permute-done.34.refs_6_.refs_4_), channel_id=1, source_target_pairs={{0,1},{1,0},{2,3},{3,2},{4,5},{5,4},{6,7},{7,6},{8,9},{9,8},{10,11... | collective-permute-start | bytes 1572872 | tf_op jit(solution)/shard_map/ppermute | solution.py:806
  230.1 14.8 %collective-permute-start.37 = (bf16[256,1024]{1,0:T(8,128)(2,1)}, bf16[256,1024]{1,0:T(8,128)(2,1)}, u32[]{:S(2)}, u32[]{:S(2)}) collective-permute-start(bf16[256,1024]{1,0:T(8,128)(2,1)} %get-tuple-element.137.refs_0_), channel_id=1, source_target_pairs={{0,2},{1,3},{2,0},{3,1},{4,6},{5,7},{6,4},{7,5},{8,10},{9,11},{10,... | collective-permute-start | bytes 1572872 | tf_op jit(solution)/shard_map/ppermute | solution.py:806
  267.0 162.1 %reduce-scatter.6.cloned.1.call-start = ((), (), s32[]{:S(2)}) async-start(), calls=%async_computation.6 | async-start | bytes 2621440 | tf_op jit(solution)/shard_map/reduce_scatter | solution.py:889
  295.9 18.3 %collective-permute-start.44 = (bf16[256,1024]{1,0:T(8,128)(2,1)}, bf16[256,1024]{1,0:T(8,128)(2,1)S(1)}, u32[]{:S(2)}, u32[]{:S(2)}) collective-permute-start(bf16[256,1024]{1,0:T(8,128)(2,1)} %get-tuple-element.156.refs_7_), channel_id=1, source_target_pairs={{0,2},{1,3},{2,0},{3,1},{4,6},{5,7},{6,4},{7,5},{8,10},{9,11},{10,... | collective-permute-start | bytes 1572872 | tf_op jit(solution)/shard_map/ppermute | solution.py:806
  319.3 14.3 %collective-permute-start.47 = (bf16[256,1024]{1,0:T(8,128)(2,1)S(1)}, bf16[256,1024]{1,0:T(8,128)(2,1)S(1)}, u32[]{:S(2)}, u32[]{:S(2)}) collective-permute-start(bf16[256,1024]{1,0:T(8,128)(2,1)S(1)} %fusion.10), channel_id=1, source_target_pairs={{0,2},{1,3},{2,0},{3,1},{4,6},{5,7},{6,4},{7,5},{8,10},{9,11},{10,... | collective-permute-start | bytes 1572872 | tf_op jit(solution)/shard_map/ppermute | solution.py:806
  320.2 16.0 %collective-permute-start.48 = (bf16[512,512]{1,0:T(8,128)(2,1)S(1)}, bf16[512,512]{1,0:T(8,128)(2,1)S(1)}, u32[]{:S(2)}, u32[]{:S(2)}) collective-permute-start(bf16[512,512]{1,0:T(8,128)(2,1)S(1)} %slice.178), channel_id=1, source_target_pairs={{4,0},{5,1},{6,2},{7,3},{12,8},{13,9},{14,10},{15,11},{20,16},{21,... | collective-permute-start | bytes 1572872 | tf_op jit(solution)/shard_map/ppermute | solution.py:802
  321.6 37.8 %collective-permute-start.51 = (bf16[256,1024]{1,0:T(8,128)(2,1)S(1)}, bf16[256,1024]{1,0:T(8,128)(2,1)S(1)}, u32[]{:S(2)}, u32[]{:S(2)}) collective-permute-start(bf16[256,1024]{1,0:T(8,128)(2,1)S(1)} %copy-done.48), channel_id=1, source_target_pairs={{0,1},{1,0},{2,3},{3,2},{4,5},{5,4},{6,7},{7,6},{8,9},{9,8},{10,11... | collective-permute-start | bytes 1572872 | tf_op jit(solution)/shard_map/ppermute | solution.py:806
  321.7 37.6 %collective-permute-start.52 = (bf16[256,1024]{1,0:T(8,128)(2,1)S(1)}, bf16[256,1024]{1,0:T(8,128)(2,1)S(1)}, u32[]{:S(2)}, u32[]{:S(2)}) collective-permute-start(bf16[256,1024]{1,0:T(8,128)(2,1)S(1)} %collective-permute-done.44.refs_9_), channel_id=1, source_target_pairs={{0,1},{1,0},{2,3},{3,2},{4,5},{5,4},{6,7},{7,6},{8,9},{9,8},{10,11... | collective-permute-start | bytes 1572872 | tf_op jit(solution)/shard_map/ppermute | solution.py:806
  326.3 38.8 %collective-permute-start.46 = (bf16[2,256,1024]{2,1,0:T(8,128)(2,1)}, bf16[2,256,1024]{2,1,0:T(8,128)(2,1)}, u32[]{:S(2)}, u32[]{:S(2)}) collective-permute-start(bf16[2,256,1024]{2,1,0:T(8,128)(2,1)} %get-tuple-element.164), channel_id=1, source_target_pairs={{0,1},{1,0},{2,3},{3,2},{4,5},{5,4},{6,7},{7,6},{8,9},{9,8},{10,11... | collective-permute-start | bytes 3145736 | tf_op jit(solution)/shard_map/ppermute | solution.py:806
  365.1 126.2 %reduce-scatter.8.cloned.1.call-start = ((), (), s32[]{:S(2)}) async-start(), calls=%async_computation.7 | async-start | bytes 2949120 | tf_op jit(solution)/shard_map/reduce_scatter | solution.py:889
  396.1 15.1 %collective-permute-start.53 = (bf16[256,1024]{1,0:T(8,128)(2,1)S(1)}, bf16[256,1024]{1,0:T(8,128)(2,1)S(1)}, u32[]{:S(2)}, u32[]{:S(2)}) collective-permute-start(bf16[256,1024]{1,0:T(8,128)(2,1)S(1)} %pad_maximum_fusion.8.refs_0_.refs_7_), channel_id=1, source_target_pairs={{0,1},{1,0},{2,3},{3,2},{4,5},{5,4},{6,7},{7,6},{8,9},{9,8},{10,11... | collective-permute-start | bytes 1572872 | tf_op jit(solution)/shard_map/ppermute | solution.py:806
  436.1 26.3 %collective-permute-start.58 = (bf16[256,2048]{1,0:T(8,128)(2,1)}, bf16[256,2048]{1,0:T(8,128)(2,1)}, u32[]{:S(2)}, u32[]{:S(2)}) collective-permute-start(bf16[256,2048]{1,0:T(8,128)(2,1)} %reduce-scatter.4.cloned.1.call-done), channel_id=1, source_target_pairs={{0,4},{4,0},{1,5},{5,1},{2,6},{6,2},{3,7},{7,3},{8,12},{12,8},{9,1... | collective-permute-start | bytes 3145736 | tf_op jit(solution)/shard_map/ppermute | solution.py:806
  445.9 30.2 %collective-permute-start.56 = (bf16[2,256,1024]{2,1,0:T(8,128)(2,1)S(1)}, bf16[2,256,1024]{2,1,0:T(8,128)(2,1)}, u32[]{:S(2)}, u32[]{:S(2)}) collective-permute-start(bf16[2,256,1024]{2,1,0:T(8,128)(2,1)S(1)} %get-tuple-element.190), channel_id=1, source_target_pairs={{0,1},{1,0},{2,3},{3,2},{4,5},{5,4},{6,7},{7,6},{8,9},{9,8},{10,11... | collective-permute-start | bytes 3145736 | tf_op jit(solution)/shard_map/ppermute | solution.py:806
  489.4 15.2 %collective-permute-start.59 = (bf16[256,1024]{1,0:T(8,128)(2,1)}, bf16[256,1024]{1,0:T(8,128)(2,1)}, u32[]{:S(2)}, u32[]{:S(2)}) collective-permute-start(bf16[256,1024]{1,0:T(8,128)(2,1)} %reduce-scatter.6.cloned.1.call-done), channel_id=1, source_target_pairs={{0,4},{4,0},{1,5},{5,1},{2,6},{6,2},{3,7},{7,3},{8,12},{12,8},{9,1... | collective-permute-start | bytes 1572872 | tf_op jit(solution)/shard_map/ppermute | solution.py:806
  491.2 24.1 %collective-permute-start.60 = (bf16[256,1152]{1,0:T(8,128)(2,1)}, bf16[256,1152]{1,0:T(8,128)(2,1)}, u32[]{:S(2)}, u32[]{:S(2)}) collective-permute-start(bf16[256,1152]{1,0:T(8,128)(2,1)} %reduce-scatter.8.cloned.1.call-done), channel_id=1, source_target_pairs={{0,4},{4,0},{1,5},{5,1},{2,6},{6,2},{3,7},{7,3},{8,12},{12,8},{9,1... | collective-permute-start | bytes 1769480 | tf_op jit(solution)/shard_map/ppermute | solution.py:806
  (151 other events, 1292.7 us)
Sparse Core Ops, SparseCore 0:
  104.3 36.1 all-gather.2
  142.7 79.6 all-gather.4
  267.2 76.9 reduce-scatter.3
  365.2 42.0 reduce-scatter.5
  431.8 47.2 reduce-scatter.7
